TPU v7x, 32 devices: a whole 2x2x4 slice. The times are simulated.
32 devices in a mesh: lamella: 2 (over x), lat: 16 (over z, y, core).
Axes of the slice: x: 2, y: 2, z: 4, core: 2. Of those that a mesh axis runs over, the one named last changes fastest.
Arguments:
- potential: bfloat16 [6, 2048, 4096], P(None, ('lamella', 'lat')), parts along dimension 1, may hold values from -6 to 6
- tilt_index: int32 [4], P('lamella'), parts along dimension 0, may hold values from 0 to 40
- slice_order: int32 [6], P('lamella'), parts along dimension 0, may hold values from 0 to 5
- tilt_table: float32 [41, 2], replicated, may hold values from -8 to 8
- fresnel_taps: float32 [2, 63], replicated, may hold values from -0.5 to 0.5
- ctf_taps: float32 [2, 127], replicated, may hold values from -0.375 to 0.375
- mtf_taps: float32 [15], replicated, may hold values from 0.02 to 0.12
- owner: int32 [32], P('lamella'), parts along dimension 0, may hold values from 0 to 15, each once
Outputs:
- exit_wave: float32 [2, 2, 2048, 4096], P(None, None, ('lamella', 'lat')), parts along dimension 2
- detector: float32 [32, 256, 1024], P(('lamella', 'lat')), parts along dimension 0
There are 2 independent parts, one for each index of `lamella`. A program takes and returns all parts, laid end to end along the dimension named above; an argument that names none is the same for every part. Nothing has to cross between parts.
Inputs may be any that keep to these rules, and one draw needn't show every extreme that they name: owner names every tile position once.
All inputs are finite; a program needn't handle non-finite values.
Results may differ from a plain program's by a relative error of at most 0.012.
Values may be sent and summed in bfloat16 or wider, within the bound.
No kernel may reach another device: no remote copies, remote signals or barrier semaphores. Data moves between devices by JAX's collectives and lax.ppermute only.
A program may use at most 64 MiB of HBM per device.

v0:
```python
import functools
import math

import jax
import jax.numpy as jnp
from jax import lax
from jax.experimental import pallas as pl
from jax.experimental.pallas import tpu as pltpu
from jax.sharding import PartitionSpec as P

highest = lax.Precision.HIGHEST
SIN_TURN = (
    6.2831854820251465,
    -41.34170150756836,
    81.60513305664062,
    -76.70301818847656,
    42.02592849731445,
    -14.899847030639648,
    3.2381374835968018,
)
COS_TURN = (
    1.0,
    -19.73920440673828,
    64.93911743164062,
    -85.45014190673828,
    60.16762924194336,
    -25.967599868774414,
    6.528658390045166,
)
HALO = 32
STEP = 256


def spread_taps(tap_list, tap_index):
    count = tap_list.shape[-1]
    which = jnp.arange(count, dtype=jnp.int32)
    onehot = (tap_index[..., None] == which).astype(jnp.float32)
    return jnp.einsum("...k,iok->...io", tap_list, onehot, precision=highest)


def short(tap_pair):
    return tap_pair.astype(jnp.bfloat16).astype(jnp.float32)


def column_band(tap_pair):
    reach = (tap_pair.shape[1] - 1) // 2
    inputs = jnp.arange(256, dtype=jnp.int32)[:, None]
    outputs = jnp.arange(128, dtype=jnp.int32)[None, :]
    real, imag = spread_taps(short(tap_pair), inputs - outputs - 64 + reach)
    joined = jnp.stack(
        [jnp.stack([real, imag], axis=1), jnp.stack([-imag, real], axis=1)], axis=0
    )
    joined = joined.reshape(2, 2, 128, 2, 128).transpose(1, 0, 2, 3, 4)
    return joined.reshape(512, 256).astype(jnp.bfloat16)


def row_band(tap_pair, rows_out, rows_in, offset):
    outputs = jnp.arange(rows_out, dtype=jnp.int32)[:, None]
    inputs = jnp.arange(rows_in, dtype=jnp.int32)[None, :]
    return spread_taps(short(tap_pair), inputs - outputs - offset)


def horner(coefs, z):
    total = coefs[-1] * z + coefs[-2]
    for coef in coefs[-3::-1]:
        total = total * z + coef
    return total


def cos_sin(phase):
    turns = phase * (1.0 / (2.0 * math.pi))
    rest = turns - jnp.round(turns)
    z = rest * rest
    return horner(COS_TURN, z), horner(SIN_TURN, z) * rest


def dot(a, b):
    return jnp.dot(a, b, preferred_element_type=jnp.float32)


def split_parts(product, rows):
    out = []
    for k in range(product.shape[1] // 256):
        top = product[:rows, 256 * k : 256 * (k + 1)]
        low = product[rows:, 256 * k : 256 * (k + 1)]
        out.append((top[:, :128] - low[:, 128:], top[:, 128:] + low[:, :128]))
    return out


def lanes_inside(block, shift, col_count):
    cols = block * 128 - shift + lax.broadcasted_iota(jnp.int32, (1, 128), 1)
    return ((cols >= 0) & (cols < col_count)).astype(jnp.float32)


def first_kernel(waves, order, *refs):
    pieces, (ex, ey, band, out, ring) = refs[:5], refs[5:]

    @pl.when(pl.program_id(0) == 0)
    def _():
        ring[:, :, :256] = jnp.zeros((waves, ring.shape[1], 256), jnp.bfloat16)

    for blk in range(2):
        lanes = pl.ds(128 * blk, 128)
        row = 0
        for piece in pieces:
            rows = piece.shape[-2]
            for start in range(0, rows, 32):
                if len(piece.shape) == 3:
                    phase = piece[0, pl.ds(start, 32), lanes]
                else:
                    phase = piece[pl.ds(start, 32), lanes]
                cosine, sine = cos_sin(phase.astype(jnp.float32))
                for w in range(waves):
                    yr, yi = ey[2 * w : 2 * w + 1, lanes], ey[2 * w + 1 : 2 * w + 2, lanes]
                    ur, ui = cosine * yr - sine * yi, cosine * yi + sine * yr
                    xr = ex[pl.ds(row, 32), 2 * w : 2 * w + 1]
                    xi = ex[pl.ds(row, 32), 2 * w + 1 : 2 * w + 2]
                    to = 256 * (blk + 1)
                    ring[w, pl.ds(row, 32), to : to + 128] = (ur * xr - ui * xi).astype(jnp.bfloat16)
                    ring[w, pl.ds(row, 32), to + 128 : to + 256] = (ur * xi + ui * xr).astype(
                        jnp.bfloat16
                    )
                row += 32
    for w in range(waves):
        for blk in range(2):
            lanes = pl.ds(256 * blk, 256)
            out[w, :, lanes] = dot(ring[w, :, 256 * blk : 256 * blk + 512], band[...]).astype(
                jnp.bfloat16
            )
        ring[w, :, :256] = ring[w, :, 512:768]


def gather_rows(pieces, lanes):
    found = []
    for piece in pieces:
        if len(piece.shape) == 3:
            found.append(piece[0, :, lanes])
        else:
            found.append(piece[:, lanes])
    return jnp.concatenate(found, axis=0).astype(jnp.float32)


def transmit(ring, product, phases, masks, waves, rows):
    factors = []
    for phase, mask in zip(phases, masks):
        cosine, sine = cos_sin(phase)
        factors.append((cosine * mask, sine * mask))
    for w in range(waves):
        for blk, (real, imag) in enumerate(split_parts(product[w], rows)):
            cosine, sine = factors[blk]
            to = 256 * (blk + 1)
            ring[w, :, to : to + 128] = (real * cosine - imag * sine).astype(jnp.bfloat16)
            ring[w, :, to + 128 : to + 256] = (real * sine + imag * cosine).astype(jnp.bfloat16)


def second_kernel(waves, col_count, order, *refs):
    pieces, (spread, rows_band, band, out, ring, last) = refs[:3], refs[3:]
    g = pl.program_id(0)

    @pl.when(g == 0)
    def _():
        ring[:, :, :256] = jnp.zeros((waves, ring.shape[1], 256), jnp.bfloat16)
        last[...] = jnp.zeros_like(last)

    rows = ring.shape[1]
    low = lax.broadcasted_iota(jnp.int32, (rows, 128), 1) < 64
    turned = [last[...]]
    for blk in range(2):
        turned.append(pltpu.roll(gather_rows(pieces, pl.ds(128 * blk, 128)), 64, 1))
    last[...] = turned[2]
    phases = [jnp.where(low, turned[0], turned[1]), jnp.where(low, turned[1], turned[2])]
    masks = [lanes_inside(2 * g, 64, col_count), lanes_inside(2 * g + 1, 64, col_count)]
    product = [dot(rows_band[...], spread[w]) for w in range(waves)]
    transmit(ring, product, phases, masks, waves, rows)
    for w in range(waves):
        for blk in range(2):
            out[w, :, 256 * blk : 256 * (blk + 1)] = dot(
                ring[w, :, 256 * blk : 256 * blk + 512], band[...]
            ).astype(jnp.bfloat16)
        ring[w, :, :256] = ring[w, :, 512:768]


def third_kernel(waves, col_count, order, owner, *refs):
    pieces = refs[:3]
    spread, rows_band, band, last_band, wide_band, exit_wave, focused, ring, last, waved, turned = refs[3:]
    g = pl.program_id(0)

    @pl.when(g == 0)
    def _():
        ring[:, :, :256] = jnp.zeros((waves, ring.shape[1], 256), jnp.bfloat16)
        waved[:, :, :256] = jnp.zeros((waves, waved.shape[1], 256), jnp.bfloat16)
        turned[...] = jnp.zeros_like(turned)
        last[...] = jnp.zeros_like(last)

    rows, kept = ring.shape[1], waved.shape[1]
    phases = [last[...], gather_rows(pieces, pl.ds(0, 128))]
    last[...] = gather_rows(pieces, pl.ds(128, 128))
    masks = [lanes_inside(2 * g - 1, 0, col_count), lanes_inside(2 * g, 0, col_count)]
    product = [dot(rows_band[...], spread[w]) for w in range(waves)]
    transmit(ring, product, phases, masks, waves, rows)
    low = lax.broadcasted_iota(jnp.int32, (kept, 128), 1) < 64
    masks = [lanes_inside(2 * g - 1, 64, col_count), lanes_inside(2 * g, 64, col_count)]
    for w in range(waves):
        for blk in range(2):
            made = dot(ring[w, :, 256 * blk : 256 * blk + 512], band[...]).astype(jnp.bfloat16)
            ((real, imag),) = split_parts(dot(last_band[...], made), kept)
            to = 256 * (blk + 1)
            for part, value in enumerate((real, imag)):
                waved[w, :, to + 128 * part : to + 128 * part + 128] = (value * masks[blk]).astype(
                    jnp.bfloat16
                )
                rolled = pltpu.roll(value, 64, 1)
                exit_wave[w, part, :, 128 * blk : 128 * blk + 128] = jnp.where(
                    low, turned[w, part], rolled
                )
                turned[w, part] = rolled
            made = dot(waved[w, :, 256 * blk : 256 * blk + 512], wide_band[...]).astype(jnp.bfloat16)
            for part in range(2):
                block = made[:, 128 * part : 128 * part + 128]
                if len(focused.shape) == 5:
                    focused[0, w, part, :, 128 * blk : 128 * blk + 128] = block
                else:
                    focused[w, part, :, 128 * blk : 128 * blk + 128] = block
        ring[w, :, :256] = ring[w, :, 512:768]
        waved[w, :, :256] = waved[w, :, 512:768]


def detector_kernel(waves, tile_wave, taps_band, row_taps, col_taps, out, padded):
    sources, rows, width = tile_wave.shape[0], tile_wave.shape[3], tile_wave.shape[4]
    total = sources * rows
    edge = jnp.zeros((64, width), jnp.float32)
    padded[:64] = edge
    padded[64 + total :] = edge
    for b in range(total // 128):
        image = None
        for w in range(waves):
            parts = []
            for part in range(2):
                window = []
                for k in range(2 * b - 1, 2 * b + 3):
                    if 0 <= k < total // 64:
                        window.append(tile_wave[k, w, part])
                    else:
                        window.append(jnp.zeros((64, width), jnp.bfloat16))
                parts.append(jnp.concatenate(window, axis=0))
            real, imag = dot(taps_band[...], parts[0]), dot(taps_band[...], parts[1])
            re = real[:128] - imag[128:]
            im = imag[:128] + real[128:]
            term = re * re + im * im
            image = term if image is None else image + term
        padded[64 + 128 * b : 192 + 128 * b] = image / waves
    for b in range(total // 128):
        rows_done = jnp.dot(
            row_taps[...],
            padded[128 * b : 128 * b + 256],
            precision=highest,
            preferred_element_type=jnp.float32,
        )
        out[:, 128 * b : 128 * b + 128] = lax.dot_general(
            col_taps[...],
            rows_done,
            (((1,), (1,)), ((), ())),
            precision=highest,
            preferred_element_type=jnp.float32,
        )


def block_windows(values):
    length = values.shape[-1]
    padded = jnp.pad(values, [(0, 0)] * (values.ndim - 1) + [(64, 64)])
    blocks = padded.reshape(values.shape[:-1] + (length // 128 + 1, 128))
    return jnp.concatenate([blocks[..., :-1, :], blocks[..., 1:, :]], axis=-1)


def narrow_tiles(focused, owner, wide_rows, row_taps, col_taps, lane_count):
    waves, _, rows, col_count = focused.shape
    width = col_count // lane_count
    slots = jnp.arange(lane_count, dtype=jnp.int32)
    placing = (owner[None, :] == slots[:, None]).astype(jnp.bfloat16)
    focused = focused.reshape(waves, 2, rows, lane_count, width)
    focused = jnp.einsum("jl,acrlk->jackr", placing, focused, preferred_element_type=jnp.float32)
    sent = focused.astype(jnp.bfloat16)
    tile_wave = lax.all_to_all(sent, "lat", split_axis=0, concat_axis=4, tiled=True)[0]
    windows = block_windows(tile_wave)
    taps_band = wide_rows.reshape(2, 128, 256)
    made = jnp.einsum("acwbi,doi->acdwbo", windows, taps_band, preferred_element_type=jnp.float32)
    real = made[:, 0, 0] - made[:, 1, 1]
    imag = made[:, 1, 0] + made[:, 0, 1]
    image = jnp.sum(real * real + imag * imag, axis=0) / waves
    image = image.reshape(width, lane_count * rows)
    blurred = jnp.einsum("wbi,oi->wbo", block_windows(image), row_taps, precision=highest)
    return jnp.dot(col_taps, blurred.reshape(width, lane_count * rows), precision=highest)


def local(potential, tilt_index, slice_order, tilt_table, fresnel_taps, ctf_taps, mtf_taps, owner):
    row_count, col_count = potential.shape[1:]
    lane_count = lax.axis_size("lat")
    total_rows = row_count * lane_count
    tile_cols = col_count // lane_count
    waves = tilt_index.shape[0]
    first_row = lax.axis_index("lat") * row_count
    steps = col_count // STEP

    def neighbour(value, offset):
        pairs = [(i, i + offset) for i in range(lane_count) if 0 <= i + offset < lane_count]
        return lax.ppermute(value, "lat", pairs)

    def chosen(step, start, rows):
        return lax.dynamic_slice(
            potential, (slice_order[step], start, 0), (1, rows, col_count)
        )[0]

    whole = chosen(0, 0, row_count)
    up1, down1 = neighbour(whole, 1), neighbour(whole, -1)
    up2 = neighbour(chosen(0, row_count - HALO, HALO), 2)
    down2 = neighbour(chosen(0, 0, HALO), -2)
    whole = chosen(1, 0, row_count)
    second_up, second_down = neighbour(whole, 1), neighbour(whole, -1)
    third_up = neighbour(chosen(2, row_count - HALO, HALO), 1)
    third_down = neighbour(chosen(2, 0, HALO), -1)

    rows1, rows2, rows3 = (row_count + 2 * HALO * k for k in (3, 2, 1))

    def inside(halo_rows, count):
        at = first_row - halo_rows + jnp.arange(count, dtype=jnp.int32)
        return ((at >= 0) & (at < total_rows)).astype(jnp.float32), at

    tilts = jnp.take(tilt_table, tilt_index, axis=0)
    keep, at = inside(3 * HALO, rows1)
    angle = 2.0 * math.pi * tilts[:, 0, None] * (at.astype(jnp.float32) / total_rows)
    ex = jnp.stack([jnp.cos(angle), jnp.sin(angle)], axis=1).reshape(2 * waves, rows1) * keep
    ex = jnp.pad(ex.T, ((0, 0), (0, 128 - 2 * waves)))
    across = jnp.arange(col_count, dtype=jnp.float32) / col_count
    angle = 2.0 * math.pi * tilts[:, 1, None] * across
    ey = jnp.stack([jnp.cos(angle), jnp.sin(angle)], axis=1).reshape(2 * waves, col_count)
    ey = jnp.pad(ey, ((0, 8 - 2 * waves), (0, STEP)))

    band = column_band(fresnel_taps)
    wide_band = column_band(ctf_taps)
    full_rows = row_band(fresnel_taps, rows2, rows1, 1)

    def stacked(count, count_in, halo_rows):
        keep = inside(halo_rows, count)[0]
        cut = full_rows[:, :count, :count_in] * keep[None, :, None]
        return cut.reshape(2 * count, count_in).astype(jnp.bfloat16)

    band2 = stacked(rows2, rows1, 2 * HALO)
    band3 = stacked(rows3, rows2, HALO)
    band4 = stacked(row_count, rows3, 0)
    wide_rows = row_band(ctf_taps, 128, 256, 1).reshape(256, 256).astype(jnp.bfloat16)
    mtf_reach = (mtf_taps.shape[0] - 1) // 2
    at = jnp.arange(256, dtype=jnp.int32)
    row_taps = spread_taps(mtf_taps, at[None, :] - at[:128, None] - 64 + mtf_reach)
    at = jnp.arange(tile_cols, dtype=jnp.int32)
    col_taps = spread_taps(mtf_taps, at[None, :] - at[:, None] + mtf_reach)

    def clamp(g):
        return jnp.minimum(g, steps - 1)

    def piece(rows):
        return pl.BlockSpec((rows, STEP), lambda g, *_: (0, clamp(g)))

    def mine(step, start, rows):
        return pl.BlockSpec(
            (1, rows, STEP), lambda g, order, *_: (order[step], start // rows, clamp(g))
        )

    def fixed(*shape):
        return pl.BlockSpec(shape, lambda g, *_: (0,) * len(shape))

    def blocks(rows):
        return pl.BlockSpec((waves, rows, 512), lambda g, *_: (0, 0, g))

    params = pltpu.CompilerParams(
        dimension_semantics=("arbitrary",), vmem_limit_bytes=48 * 1024 * 1024
    )

    def cost(flops, count):
        return pl.CostEstimate(flops=flops, bytes_accessed=count, transcendentals=0)

    spread_cols = (steps + 1) * 512
    spread = pl.pallas_call(
        functools.partial(first_kernel, waves),
        name="first_step",
        out_shape=jax.ShapeDtypeStruct((waves, rows1, spread_cols), jnp.bfloat16),
        grid_spec=pltpu.PrefetchScalarGridSpec(
            num_scalar_prefetch=1,
            grid=(steps + 1,),
            in_specs=[
                piece(HALO),
                piece(row_count),
                mine(0, 0, row_count),
                piece(row_count),
                piece(HALO),
                fixed(rows1, 128),
                pl.BlockSpec((8, STEP), lambda g, *_: (0, g)),
                fixed(512, 256),
            ],
            out_specs=blocks(rows1),
            scratch_shapes=[pltpu.VMEM((waves, rows1, 768), jnp.bfloat16)],
        ),
        compiler_params=params,
        cost_estimate=cost(waves * rows1 * spread_cols * 1024, 12 << 20),
    )(slice_order, up2, up1, potential, down1, down2, ex, ey, band)

    spread = pl.pallas_call(
        functools.partial(second_kernel, waves, col_count),
        name="second_step",
        out_shape=jax.ShapeDtypeStruct((waves, rows2, spread_cols), jnp.bfloat16),
        grid_spec=pltpu.PrefetchScalarGridSpec(
            num_scalar_prefetch=1,
            grid=(steps + 1,),
            in_specs=[
                piece(row_count),
                mine(1, 0, row_count),
                piece(row_count),
                blocks(rows1),
                fixed(2 * rows2, rows1),
                fixed(512, 256),
            ],
            out_specs=blocks(rows2),
            scratch_shapes=[
                pltpu.VMEM((waves, rows2, 768), jnp.bfloat16),
                pltpu.VMEM((rows2, 128), jnp.float32),
            ],
        ),
        compiler_params=params,
        cost_estimate=cost(waves * rows2 * spread_cols * 2048, 16 << 20),
    )(slice_order, second_up, potential, second_down, spread, band2, band)

    def done(g):
        return jnp.maximum(g - 1, 0)

    placed = tile_cols == STEP
    if placed:
        focused_shape = (lane_count, waves, 2, row_count, tile_cols)
        focused_spec = pl.BlockSpec(
            (1, waves, 2, row_count, tile_cols),
            lambda g, order, owner: (owner[done(g)], 0, 0, 0, 0),
        )
    else:
        focused_shape = (waves, 2, row_count, col_count)
        focused_spec = pl.BlockSpec(
            (waves, 2, row_count, STEP), lambda g, *_: (0, 0, 0, done(g))
        )
    exit_wave, focused = pl.pallas_call(
        functools.partial(third_kernel, waves, col_count),
        name="third_step",
        out_shape=(
            jax.ShapeDtypeStruct((waves, 2, row_count, col_count), jnp.float32),
            jax.ShapeDtypeStruct(focused_shape, jnp.bfloat16),
        ),
        grid_spec=pltpu.PrefetchScalarGridSpec(
            num_scalar_prefetch=2,
            grid=(steps + 1,),
            in_specs=[
                piece(HALO),
                mine(2, 0, row_count),
                piece(HALO),
                blocks(rows2),
                fixed(2 * rows3, rows2),
                fixed(512, 256),
                fixed(2 * row_count, rows3),
                fixed(512, 256),
            ],
            out_specs=(
                pl.BlockSpec((waves, 2, row_count, STEP), lambda g, *_: (0, 0, 0, done(g))),
                focused_spec,
            ),
            scratch_shapes=[
                pltpu.VMEM((waves, rows3, 768), jnp.bfloat16),
                pltpu.VMEM((rows3, 128), jnp.float32),
                pltpu.VMEM((waves, row_count, 768), jnp.bfloat16),
                pltpu.VMEM((waves, 2, row_count, 128), jnp.float32),
            ],
        ),
        compiler_params=params,
        cost_estimate=cost(waves * rows3 * spread_cols * 3072, 16 << 20),
    )(slice_order, owner, third_up, potential, third_down, spread, band3, band, band4, wide_band)

    if not placed:
        detector = narrow_tiles(focused, owner, wide_rows, row_taps, col_taps, lane_count)
        return exit_wave, detector[None]

    tile_wave = lax.all_to_all(focused, "lat", split_axis=0, concat_axis=0, tiled=True)
    detector = pl.pallas_call(
        functools.partial(detector_kernel, waves),
        name="detector",
        out_shape=jax.ShapeDtypeStruct((tile_cols, total_rows), jnp.float32),
        in_specs=[pl.BlockSpec(memory_space=pltpu.VMEM)] * 4,
        out_specs=pl.BlockSpec(memory_space=pltpu.VMEM),
        scratch_shapes=[pltpu.VMEM((total_rows + 128, tile_cols), jnp.float32)],
        compiler_params=pltpu.CompilerParams(vmem_limit_bytes=48 * 1024 * 1024),
        cost_estimate=cost(1 << 33, 4 << 20),
    )(tile_wave, wide_rows, row_taps, col_taps)
    return exit_wave, detector[None]


def solution(mesh):
    placed = (
        P(None, ("lamella", "lat"), None),
        P("lamella"),
        P("lamella"),
        P(),
        P(),
        P(),
        P(),
        P("lamella"),
    )
    return jax.shard_map(
        local,
        mesh=mesh,
        in_specs=placed,
        out_specs=(P(None, None, ("lamella", "lat"), None), P(("lamella", "lat"), None, None)),
        check_vma=False,
    )
```

profile of v0, /device:TPU:13, one launch (start us, length us, event | category | flops | bytes accessed | tf_op | source)
XLA Modules:
  0.0 189.3 jit_solution(7963900699373979750)
XLA Ops:
  0.7 1.4 fusion.32
  5.9 2.3 %dynamic-slice_bitcast_fusion = (bf16[64,4096]{1,0:T(8,128)(2,1)}, bf16[64,4096]{1,0:T(8,128)(2,1)}) fusion(bf16[6,64,4096]{2,1,0:T(8,128)(2,1)} %refs_1_.3, s32[]{:T(128)S(6)} %select_n.23, s32[]{:T(128)S(6)} %select_n.22), kind=kLoop, calls=%fused_computation.23 | loop fusion | bytes 2097160 | tf_op jit(solution)/shard_map/squeeze | solution.py:309
  8.2 3.8 %collective-permute-start.5 = (bf16[64,4096]{1,0:T(8,128)(2,1)}, bf16[64,4096]{1,0:T(8,128)(2,1)}, u32[]{:S(2)}, u32[]{:S(2)}) collective-permute-start(bf16[64,4096]{1,0:T(8,128)(2,1)} %get-tuple-element.12), channel_id=1, source_target_pairs={{0,1},{1,2},{2,3},{3,4},{4,5},{5,6},{6,7},{7,8},{8,9},{9,10},{10,1... | collective-permute-start | bytes 1572872 | tf_op jit(solution)/shard_map/ppermute | solution.py:306
  12.0 1.9 %collective-permute-start.6 = (bf16[64,4096]{1,0:T(8,128)(2,1)}, bf16[64,4096]{1,0:T(8,128)(2,1)}, u32[]{:S(2)}, u32[]{:S(2)}) collective-permute-start(bf16[64,4096]{1,0:T(8,128)(2,1)} %get-tuple-element.12), channel_id=1, source_target_pairs={{1,0},{2,1},{3,2},{4,3},{5,4},{6,5},{7,6},{8,7},{9,8},{10,9},{11,1... | collective-permute-start | bytes 1572872 | tf_op jit(solution)/shard_map/ppermute | solution.py:306
  13.9 4.5 %collective-permute-start.2 = (bf16[64,4096]{1,0:T(8,128)(2,1)}, bf16[64,4096]{1,0:T(8,128)(2,1)}, u32[]{:S(2)}, u32[]{:S(2)}) collective-permute-start(bf16[64,4096]{1,0:T(8,128)(2,1)} %get-tuple-element.13), channel_id=1, source_target_pairs={{0,1},{1,2},{2,3},{3,4},{4,5},{5,6},{6,7},{7,8},{8,9},{9,10},{10,1... | collective-permute-start | bytes 1572872 | tf_op jit(solution)/shard_map/ppermute | solution.py:306
  20.2 2.2 %dynamic-slice_bitcast_fusion.2 = (bf16[32,4096]{1,0:T(8,128)(2,1)}, bf16[32,4096]{1,0:T(8,128)(2,1)}, bf16[32,4096]{1,0:T(8,128)(2,1)}, bf16[32,4096]{1,0:T(8,128)(2,1)}) fusion(bf16[6,64,4096]{2,1,0:T(8,128)(2,1)} %refs_1_.3, s32[]{:T(128)S(6)} %select_n.23, s32[]{:T(128)S(6)} %select_n.21), kind=kLoop, calls=%fused_computation.35 | loop fusion | bytes 2097160 | tf_op jit(solution)/shard_map/squeeze | solution.py:309
  22.4 2.2 %collective-permute-start.4 = (bf16[32,4096]{1,0:T(8,128)(2,1)}, bf16[32,4096]{1,0:T(8,128)(2,1)}, u32[]{:S(2)}, u32[]{:S(2)}) collective-permute-start(bf16[32,4096]{1,0:T(8,128)(2,1)} %get-tuple-element.9), channel_id=1, source_target_pairs={{0,2},{1,3},{2,4},{3,5},{4,6},{5,7},{6,8},{7,9},{8,10},{9,11},{10,... | collective-permute-start | bytes 786440 | tf_op jit(solution)/shard_map/ppermute | solution.py:306
  24.6 3.0 %collective-permute-start.7 = (bf16[32,4096]{1,0:T(8,128)(2,1)}, bf16[32,4096]{1,0:T(8,128)(2,1)}, u32[]{:S(2)}, u32[]{:S(2)}) collective-permute-start(bf16[32,4096]{1,0:T(8,128)(2,1)} %get-tuple-element.8), channel_id=1, source_target_pairs={{2,0},{3,1},{4,2},{5,3},{6,4},{7,5},{8,6},{9,7},{10,8},{11,9},{12,... | collective-permute-start | bytes 786440 | tf_op jit(solution)/shard_map/ppermute | solution.py:306
  27.8 7.4 %fusion.13 = f32[2,256,128]{2,0,1:T(2,128)S(1)} fusion(s32[256,128]{1,0:T(8,128)S(1)} %fusion.17, f32[2,127]{1,0:T(2,128)S(1)} %copy-done.10), kind=kOutput, calls=%fused_computation.20 | convolution fusion | flops 20807934 | bytes 394232 | tf_op jit(solution)/shard_map/...k,iok->...io/dot_general | solution.py:38
  35.6 1.5 fusion.12
  40.2 1.0 copy.53
  41.2 1.0 copy.50
  42.2 3.1 %fusion.2 = f32[192,256,2]{1,2,0:T(2,128)S(1)} fusion(s32[192,256]{1,0:T(8,128)} %subtract_add_fusion.1, f32[2,63]{1,0:T(2,128)S(1)} %copy-done.9), kind=kOutput, calls=%fused_computation.6 | convolution fusion | flops 15483006 | bytes 590328 | tf_op jit(solution)/shard_map/...k,iok->...io/dot_general | solution.py:38
  46.9 1.1 multiply_cosine_fusion
  48.6 1.8 copy_bitcast_fusion.1
  50.4 1.0 fusion.16
  51.5 1.7 multiply_bitcast_fusion
  53.1 1.9 %collective-permute-start.3 = (bf16[64,4096]{1,0:T(8,128)(2,1)}, bf16[64,4096]{1,0:T(8,128)(2,1)}, u32[]{:S(2)}, u32[]{:S(2)}) collective-permute-start(bf16[64,4096]{1,0:T(8,128)(2,1)} %get-tuple-element.13), channel_id=1, source_target_pairs={{1,0},{2,1},{3,2},{4,3},{5,4},{6,5},{7,6},{8,7},{9,8},{10,9},{11,1... | collective-permute-start | bytes 1572872 | tf_op jit(solution)/shard_map/ppermute | solution.py:306
  55.1 1.5 fusion.19
  56.6 1.5 reshape.384
  59.9 4.5 %collective-permute-start = (bf16[32,4096]{1,0:T(8,128)(2,1)}, bf16[32,4096]{1,0:T(8,128)(2,1)S(1)}, u32[]{:S(2)}, u32[]{:S(2)}) collective-permute-start(bf16[32,4096]{1,0:T(8,128)(2,1)} %get-tuple-element.11), channel_id=1, source_target_pairs={{0,1},{1,2},{2,3},{3,4},{4,5},{5,6},{6,7},{7,8},{8,9},{9,10},{10,1... | collective-permute-start | bytes 786440 | tf_op jit(solution)/shard_map/ppermute | solution.py:306
  64.5 1.9 %collective-permute-start.1 = (bf16[32,4096]{1,0:T(8,128)(2,1)}, bf16[32,4096]{1,0:T(8,128)(2,1)S(1)}, u32[]{:S(2)}, u32[]{:S(2)}) collective-permute-start(bf16[32,4096]{1,0:T(8,128)(2,1)} %get-tuple-element.10), channel_id=1, source_target_pairs={{1,0},{2,1},{3,2},{4,3},{5,4},{6,5},{7,6},{8,7},{9,8},{10,9},{11,1... | collective-permute-start | bytes 786440 | tf_op jit(solution)/shard_map/ppermute | solution.py:306
  66.4 0.9 copy-done.2
  67.4 17.9 %first_step.1.refs_3_ = bf16[2,256,8704]{2,1,0:T(8,128)(2,1)} custom-call(s32[3]{0:T(128)S(1)} %copy-done.6, bf16[32,4096]{1,0:T(8,128)(2,1)} %collective-permute-done.4.refs_0_, bf16[64,4096]{1,0:T(8,128)(2,1)} %collective-permute-done.5.refs_1_, bf16[6,64,4096]{2,1,0:T(8,128)(2,1)S(1)} %copy-done.1, bf16[64,4096]{1,0:T(8,128)(2,1)} %collective-permute-done.6.refs_3_, ...), custom_call_target="tpu_custom_call" | custom-call | flops 4563402752 | bytes 12582912 | tf_op jit(solution)/shard_map/first_step/pallas_call | solution.py:382
  85.3 19.8 %second_step.1.refs_3_ = bf16[2,192,8704]{2,1,0:T(8,128)(2,1)} custom-call(s32[3]{0:T(128)S(1)} %copy-done.6, bf16[64,4096]{1,0:T(8,128)(2,1)} %collective-permute-done.2.refs_0_, bf16[6,64,4096]{2,1,0:T(8,128)(2,1)S(1)} %copy-done.1, bf16[64,4096]{1,0:T(8,128)(2,1)} %collective-permute-done.3.refs_2_, bf16[2,256,8704]{2,1,0:T(8,128)(2,1)} %first_step.1.refs_3_, ...), custom_call_target="tpu_custom_call" | custom-call | flops 6845104128 | bytes 16777216 | tf_op jit(solution)/shard_map/second_step/pallas_call | solution.py:406
  105.2 24.8 %third_step.1 = (f32[2,2,64,4096]{3,2,1,0:T(8,128)}, bf16[16,2,2,64,256]{4,3,2,1,0:T(8,128)(2,1)}) custom-call(s32[3]{0:T(128)S(1)} %copy-done.6, s32[16]{0:T(128)S(1)} %copy-done.7, bf16[32,4096]{1,0:T(8,128)(2,1)S(1)} %collective-permute-done.refs_0_, bf16[6,64,4096]{2,1,0:T(8,128)(2,1)} %refs_1_.3, bf16[32,4096]{1,0:T(8,128)(2,1)S(1)} %collective-permute-done.1.refs_2_, ...), custom_call_target="tpu_custom_call" | custom-call | flops 6845104128 | bytes 16777216 | tf_op jit(solution)/shard_map/third_step/pallas_call | solution.py:446
  130.0 6.4 %all-to-all-start = ((bf16[16,2,2,64,256]{4,3,2,1,0:T(8,128)(2,1)}), bf16[16,2,2,64,256]{4,3,2,1,0:T(8,128)(2,1)S(1)}, u32[]{:S(2)}, u32[]{:S(2)}) async-start(bf16[16,2,2,64,256]{4,3,2,1,0:T(8,128)(2,1)} %get-tuple-element.5), calls=%async_computation | async-start | bytes 4194304 | tf_op jit(solution)/shard_map/all_to_all | solution.py:485
  136.4 7.4 %fusion.15 = bf16[2,128,256]{2,0,1:T(2,128)(2,1)S(1)} fusion(s32[128,256]{1,0:T(8,128)S(1)} %subtract_add_fusion.3, f32[2,127]{1,0:T(2,128)S(1)} %copy-done.10), kind=kOutput, calls=%fused_computation.22 | convolution fusion | flops 20873470 | bytes 263160 | tf_op jit(solution)/shard_map/...k,iok->...io/dot_general | solution.py:38
  144.3 1.3 fusion.10
  146.3 2.5 %fusion.8 = f32[1,256,256]{2,0,1:T(1,128)S(1)} fusion(pred[256,256,15]{1,0,2:T(32,128)(4,1)S(1)} %iota_compare_fusion.8, f32[15]{0:T(128)S(1)} %copy-done), kind=kOutput, calls=%fused_computation.13 | convolution fusion | flops 11796480 | bytes 1245244 | tf_op jit(solution)/shard_map/...k,iok->...io/dot_general | solution.py:38
  148.7 35.1 %all-to-all-done.tile_wave = bf16[16,2,2,64,256]{4,3,2,1,0:T(8,128)(2,1)S(1)} async-done(((bf16[16,2,2,64,256]{4,3,2,1,0:T(8,128)(2,1)}), bf16[16,2,2,64,256]{4,3,2,1,0:T(8,128)(2,1)S(1)}, u32[]{:S(2)}, u32[]{:S(2)}) %all-to-all-start) | async-done | bytes 2097184 | tf_op jit(solution)/shard_map/all_to_all | solution.py:485
  183.8 5.4 %detector.1 = f32[256,1024]{1,0:T(8,128)} custom-call(bf16[16,2,2,64,256]{4,3,2,1,0:T(8,128)(2,1)S(1)} %all-to-all-done.tile_wave, bf16[256,256]{1,0:T(8,128)(2,1)S(1)} %bitcast.76, f32[128,256]{1,0:T(8,128)S(1)} %bitcast.77, f32[256,256]{1,0:T(8,128)S(1)} %bitcast.73), custom_call_target="tpu_custom_call" | custom-call | flops 8589934592 | bytes 4194304 | tf_op jit(solution)/shard_map/detector/pallas_call | solution.py:486
  (78 shorter events, 8.6 us)
Async XLA Ops:
  0.6 143.7 %copy-start = (f32[15]{0:T(128)S(1)}, f32[15]{0:T(128)}, u32[]{:S(2)}) copy-start(f32[15]{0:T(128)} %param.14) | copy-start | bytes 184
  0.6 27.0 %copy-start.11 = (s32[2]{0:T(128)S(1)}, s32[2]{0:T(128)}, u32[]{:S(2)}) copy-start(s32[2]{0:T(128)} %param.9) | copy-start | bytes 28
  0.7 27.1 %copy-start.10 = (f32[2,127]{1,0:T(2,128)S(1)}, f32[2,127]{1,0:T(2,128)}, u32[]{:S(2)}) copy-start(f32[2,127]{1,0:T(2,128)} %param.13) | copy-start | bytes 3052
  8.2 27.4 %copy-start.9 = (f32[2,63]{1,0:T(2,128)S(1)}, f32[2,63]{1,0:T(2,128)}, u32[]{:S(2)}) copy-start(f32[2,63]{1,0:T(2,128)} %param.12) | copy-start | bytes 1516
  8.2 56.3 %collective-permute-start.5 = (bf16[64,4096]{1,0:T(8,128)(2,1)}, bf16[64,4096]{1,0:T(8,128)(2,1)}, u32[]{:S(2)}, u32[]{:S(2)}) collective-permute-start(bf16[64,4096]{1,0:T(8,128)(2,1)} %get-tuple-element.12), channel_id=1, source_target_pairs={{0,1},{1,2},{2,3},{3,4},{4,5},{5,6},{6,7},{7,8},{8,9},{9,10},{10,1... | collective-permute-start | bytes 1572872 | tf_op jit(solution)/shard_map/ppermute | solution.py:306
  12.0 54.4 %collective-permute-start.6 = (bf16[64,4096]{1,0:T(8,128)(2,1)}, bf16[64,4096]{1,0:T(8,128)(2,1)}, u32[]{:S(2)}, u32[]{:S(2)}) collective-permute-start(bf16[64,4096]{1,0:T(8,128)(2,1)} %get-tuple-element.12), channel_id=1, source_target_pairs={{1,0},{2,1},{3,2},{4,3},{5,4},{6,5},{7,6},{8,7},{9,8},{10,9},{11,1... | collective-permute-start | bytes 1572872 | tf_op jit(solution)/shard_map/ppermute | solution.py:306
  13.9 71.3 %collective-permute-start.2 = (bf16[64,4096]{1,0:T(8,128)(2,1)}, bf16[64,4096]{1,0:T(8,128)(2,1)}, u32[]{:S(2)}, u32[]{:S(2)}) collective-permute-start(bf16[64,4096]{1,0:T(8,128)(2,1)} %get-tuple-element.13), channel_id=1, source_target_pairs={{0,1},{1,2},{2,3},{3,4},{4,5},{5,6},{6,7},{7,8},{8,9},{9,10},{10,1... | collective-permute-start | bytes 1572872 | tf_op jit(solution)/shard_map/ppermute | solution.py:306
  22.4 30.7 %collective-permute-start.4 = (bf16[32,4096]{1,0:T(8,128)(2,1)}, bf16[32,4096]{1,0:T(8,128)(2,1)}, u32[]{:S(2)}, u32[]{:S(2)}) collective-permute-start(bf16[32,4096]{1,0:T(8,128)(2,1)} %get-tuple-element.9), channel_id=1, source_target_pairs={{0,2},{1,3},{2,4},{3,5},{4,6},{5,7},{6,8},{7,9},{8,10},{9,11},{10,... | collective-permute-start | bytes 786440 | tf_op jit(solution)/shard_map/ppermute | solution.py:306
  24.6 35.3 %collective-permute-start.7 = (bf16[32,4096]{1,0:T(8,128)(2,1)}, bf16[32,4096]{1,0:T(8,128)(2,1)}, u32[]{:S(2)}, u32[]{:S(2)}) collective-permute-start(bf16[32,4096]{1,0:T(8,128)(2,1)} %get-tuple-element.8), channel_id=1, source_target_pairs={{2,0},{3,1},{4,2},{5,3},{6,4},{7,5},{8,6},{9,7},{10,8},{11,9},{12,... | collective-permute-start | bytes 786440 | tf_op jit(solution)/shard_map/ppermute | solution.py:306
  27.8 10.4 %copy-start.8 = (f32[41,2]{0,1:T(2,128)S(1)}, f32[41,2]{0,1:T(2,128)}, u32[]{:S(2)}) copy-start(f32[41,2]{0,1:T(2,128)} %param.11) | copy-start | bytes 988
  41.1 25.3 %copy-start.1 = (bf16[6,64,4096]{2,1,0:T(8,128)(2,1)S(1)}, bf16[6,64,4096]{2,1,0:T(8,128)(2,1)}, u32[]{:S(2)}) copy-start(bf16[6,64,4096]{2,1,0:T(8,128)(2,1)} %refs_1_.3) | copy-start | bytes 9437188
  41.2 25.3 %copy-start.6 = (s32[3]{0:T(128)S(1)}, s32[3]{0:T(128)}, u32[]{:S(2)}) copy-start(s32[3]{0:T(128)} %order.5) | copy-start | bytes 40
  53.1 32.1 %collective-permute-start.3 = (bf16[64,4096]{1,0:T(8,128)(2,1)}, bf16[64,4096]{1,0:T(8,128)(2,1)}, u32[]{:S(2)}, u32[]{:S(2)}) collective-permute-start(bf16[64,4096]{1,0:T(8,128)(2,1)} %get-tuple-element.13), channel_id=1, source_target_pairs={{1,0},{2,1},{3,2},{4,3},{5,4},{6,5},{7,6},{8,7},{9,8},{10,9},{11,1... | collective-permute-start | bytes 1572872 | tf_op jit(solution)/shard_map/ppermute | solution.py:306
  59.9 45.2 %collective-permute-start = (bf16[32,4096]{1,0:T(8,128)(2,1)}, bf16[32,4096]{1,0:T(8,128)(2,1)S(1)}, u32[]{:S(2)}, u32[]{:S(2)}) collective-permute-start(bf16[32,4096]{1,0:T(8,128)(2,1)} %get-tuple-element.11), channel_id=1, source_target_pairs={{0,1},{1,2},{2,3},{3,4},{4,5},{5,6},{6,7},{7,8},{8,9},{9,10},{10,1... | collective-permute-start | bytes 786440 | tf_op jit(solution)/shard_map/ppermute | solution.py:306
  64.5 40.7 %collective-permute-start.1 = (bf16[32,4096]{1,0:T(8,128)(2,1)}, bf16[32,4096]{1,0:T(8,128)(2,1)S(1)}, u32[]{:S(2)}, u32[]{:S(2)}) collective-permute-start(bf16[32,4096]{1,0:T(8,128)(2,1)} %get-tuple-element.10), channel_id=1, source_target_pairs={{1,0},{2,1},{3,2},{4,3},{5,4},{6,5},{7,6},{8,7},{9,8},{10,9},{11,1... | collective-permute-start | bytes 786440 | tf_op jit(solution)/shard_map/ppermute | solution.py:306
  66.4 1.0 copy-start.2
  67.4 17.9 %copy-start.4 = (bf16[2,192,256]{2,1,0:T(8,128)(2,1)S(1)}, bf16[2,192,256]{2,1,0:T(8,128)(2,1)}, u32[]{:S(2)}) copy-start(bf16[2,192,256]{2,1,0:T(8,128)(2,1)} %multiply_convert_fusion) | copy-start | bytes 589828
  85.3 19.9 %copy-start.3 = (bf16[512,256]{1,0:T(8,128)(2,1)S(1)}, bf16[512,256]{1,0:T(8,128)(2,1)}, u32[]{:S(2)}) copy-start(bf16[512,256]{1,0:T(8,128)(2,1)} %get-tuple-element.26.refs_7_.refs_5_) | copy-start | bytes 786436
  85.3 19.9 %copy-start.5 = (bf16[2,64,128]{2,1,0:T(8,128)(2,1)S(1)}, bf16[2,64,128]{2,1,0:T(8,128)(2,1)}, u32[]{:S(2)}) copy-start(bf16[2,64,128]{2,1,0:T(8,128)(2,1)} %fusion.19) | copy-start | bytes 98308
  85.3 19.9 %copy-start.7 = (s32[16]{0:T(128)S(1)}, s32[16]{0:T(128)}, u32[]{:S(2)}) copy-start(s32[16]{0:T(128)} %owner.1) | copy-start | bytes 196
  130.0 53.9 %all-to-all-start = ((bf16[16,2,2,64,256]{4,3,2,1,0:T(8,128)(2,1)}), bf16[16,2,2,64,256]{4,3,2,1,0:T(8,128)(2,1)S(1)}, u32[]{:S(2)}, u32[]{:S(2)}) async-start(bf16[16,2,2,64,256]{4,3,2,1,0:T(8,128)(2,1)} %get-tuple-element.5), calls=%async_computation | async-start | bytes 4194304 | tf_op jit(solution)/shard_map/all_to_all | solution.py:485
where the time goes:
time: 192 us; the launch traced here: 189 us
  Pallas kernels  67.9 us (35%)
  waiting for transfers between devices  35.1 us (18%)
  starting transfers between devices  30.4 us (16%)
  matrix products  23.1 us (12%)
  local copies, waits for them, and re-layouts  16.6 us (9%)
  other arithmetic  9.33 us (5%)
  between operations  6.76 us (4%)
    all_to_all x1, waiting for transfers between devices, local(): lax.all_to_all(focused, 'lat', split_axis=0, concat_axis=0, tiled=True)  35.1 us
    pallas_call x1, Pallas kernels, local(): pl.pallas_call(functools.partial(third_kernel, waves, col_count), name='t...  24.8 us
    ppermute x8, starting transfers between devices, neighbour(): return lax.ppermute(value, 'lat', pairs)  23.9 us
    dot_general x6, matrix products, spread_taps(): return jnp.einsum('...k,iok->...io', tap_list, onehot, precision=highest)  23.1 us
    pallas_call x1, Pallas kernels, local(): pl.pallas_call(functools.partial(second_kernel, waves, col_count), name='...  19.8 us
    pallas_call x1, Pallas kernels, local(): pl.pallas_call(functools.partial(first_kernel, waves), name='first_step',...  17.9 us
    all_to_all x1, starting transfers between devices, local(): lax.all_to_all(focused, 'lat', split_axis=0, concat_axis=0, tiled=True)  6.43 us
    pallas_call x1, Pallas kernels, local(): pl.pallas_call(functools.partial(detector_kernel, waves), name='detector'...  5.41 us
  transfers between devices with their start and end apart: 9, of which 1 were waited for; matrix products, arithmetic and copies ran while one was open for 23% of the time, Pallas kernels for 20%

commit v1 on v0

--- a/solution.py
+++ b/solution.py
@@ -27,37 +27,22 @@
     -25.967599868774414,
     6.528658390045166,
 )
+SIN_QUARTER = (
+    0.4204482138156891,
+    -0.004379667341709137,
+    1.3686111742572393e-05,
+    -2.0339173900651986e-08,
+    1.679661791598175e-11,
+)
+COS_QUARTER = (
+    1.6817927360534668,
+    -0.052555955946445465,
+    0.00027371387113817036,
+    -5.690624220733298e-07,
+    5.977824346636851e-10,
+)
 HALO = 32
 STEP = 256
-
-
-def spread_taps(tap_list, tap_index):
-    count = tap_list.shape[-1]
-    which = jnp.arange(count, dtype=jnp.int32)
-    onehot = (tap_index[..., None] == which).astype(jnp.float32)
-    return jnp.einsum("...k,iok->...io", tap_list, onehot, precision=highest)
-
-
-def short(tap_pair):
-    return tap_pair.astype(jnp.bfloat16).astype(jnp.float32)
-
-
-def column_band(tap_pair):
-    reach = (tap_pair.shape[1] - 1) // 2
-    inputs = jnp.arange(256, dtype=jnp.int32)[:, None]
-    outputs = jnp.arange(128, dtype=jnp.int32)[None, :]
-    real, imag = spread_taps(short(tap_pair), inputs - outputs - 64 + reach)
-    joined = jnp.stack(
-        [jnp.stack([real, imag], axis=1), jnp.stack([-imag, real], axis=1)], axis=0
-    )
-    joined = joined.reshape(2, 2, 128, 2, 128).transpose(1, 0, 2, 3, 4)
-    return joined.reshape(512, 256).astype(jnp.bfloat16)
-
-
-def row_band(tap_pair, rows_out, rows_in, offset):
-    outputs = jnp.arange(rows_out, dtype=jnp.int32)[:, None]
-    inputs = jnp.arange(rows_in, dtype=jnp.int32)[None, :]
-    return spread_taps(short(tap_pair), inputs - outputs - offset)
 
 
 def horner(coefs, z):
@@ -67,11 +52,18 @@
     return total
 
 
-def cos_sin(phase):
-    turns = phase * (1.0 / (2.0 * math.pi))
+def cos_sin_turns(turns):
     rest = turns - jnp.round(turns)
     z = rest * rest
     return horner(COS_TURN, z), horner(SIN_TURN, z) * rest
+
+
+def cos_sin(phase):
+    z = phase * phase
+    quarter_sin = horner(SIN_QUARTER, z) * phase
+    half_sin = quarter_sin * horner(COS_QUARTER, z)
+    half_cos = math.sqrt(2.0) - quarter_sin * quarter_sin
+    return 1.0 - half_sin * half_sin, half_sin * half_cos
 
 
 def dot(a, b):
@@ -90,6 +82,88 @@
 def lanes_inside(block, shift, col_count):
     cols = block * 128 - shift + lax.broadcasted_iota(jnp.int32, (1, 128), 1)
     return ((cols >= 0) & (cols < col_count)).astype(jnp.float32)
+
+
+def pick_kernel(halo, order, potential, *refs):
+    outs, sems = refs[:-1], refs[-1]
+    rows = potential.shape[1]
+    whole, low, high = pl.ds(0, rows), pl.ds(0, halo), pl.ds(rows - halo, halo)
+    picks = ((0, whole), (0, high), (0, low), (1, whole), (2, high), (2, low))
+    copies = []
+    for i, (step, part) in enumerate(picks):
+        copy = pltpu.make_async_copy(potential.at[order[step], part], outs[i], sems.at[i])
+        copy.start()
+        copies.append(copy)
+    for copy in copies:
+        copy.wait()
+
+
+def toeplitz(row, count, shift):
+    wide = jnp.broadcast_to(row, (count, 256))
+    return pltpu.roll(wide, shift % 256, 1, stride=1, stride_axis=0)
+
+
+def inside_rows(first, count, total):
+    at = first + lax.broadcasted_iota(jnp.int32, (count, 1), 0)
+    return ((at >= 0) & (at < total)).astype(jnp.float32)
+
+
+def prepare_kernel(
+    waves, rows, total_rows, col_count, tilt_index, first_row, tilt_table, fresnel, ctf, mtf,
+    band, wide_band, band2, band3, band4, wide_rows, row_taps, col_taps, ex, ey, line,
+):
+    line[...] = jnp.zeros_like(line)
+    line[0:2, : fresnel.shape[1]] = fresnel[...].astype(jnp.bfloat16).astype(jnp.float32)
+    line[2:4, : ctf.shape[1]] = ctf[...].astype(jnp.bfloat16).astype(jnp.float32)
+    line[4:5, : mtf.shape[1]] = mtf[...]
+    first = first_row[0]
+
+    def columns(target, at, shift):
+        for part in range(2):
+            made = toeplitz(line[at + part : at + part + 1], 128, shift)
+            for k in range(2):
+                turned = jnp.transpose(made[:, 128 * k : 128 * k + 128])
+                up, down = 256 * k, 256 * k + 128
+                if part == 0:
+                    target[up:down, :128] = turned.astype(jnp.bfloat16)
+                    target[down : down + 128, 128:] = turned.astype(jnp.bfloat16)
+                else:
+                    target[up:down, 128:] = turned.astype(jnp.bfloat16)
+                    target[down : down + 128, :128] = (-turned).astype(jnp.bfloat16)
+
+    columns(band, 0, 65 - (fresnel.shape[1] + 1) // 2)
+    columns(wide_band, 2, 65 - (ctf.shape[1] + 1) // 2)
+    for target, halo in ((band2, 2 * HALO), (band3, HALO), (band4, 0)):
+        count, count_in = target.shape[0] // 2, target.shape[1]
+        keep = inside_rows(first - halo, count, total_rows)
+        for part in range(2):
+            made = toeplitz(line[part : part + 1], count, HALO - (fresnel.shape[1] - 1) // 2) * keep
+            target[count * part : count * part + count] = made[:, :count_in].astype(jnp.bfloat16)
+    for part in range(2):
+        made = toeplitz(line[2 + part : 3 + part], 128, 65 - (ctf.shape[1] + 1) // 2)
+        wide_rows[128 * part : 128 * part + 128] = made.astype(jnp.bfloat16)
+    reach = (mtf.shape[1] - 1) // 2
+    row_taps[...] = toeplitz(line[4:5], 128, 64 - reach)
+    width = col_taps.shape[0]
+    off = lax.broadcasted_iota(jnp.int32, (width, 256), 1) - lax.broadcasted_iota(
+        jnp.int32, (width, 256), 0
+    )
+    made = jnp.where(jnp.abs(off) <= reach, toeplitz(line[4:5], width, -reach), 0.0)
+    col_taps[...] = made[:, :width]
+    count = ex.shape[1]
+    at = first - 3 * HALO + lax.broadcasted_iota(jnp.int32, (count, 128), 0)
+    keep = ((at >= 0) & (at < total_rows)).astype(jnp.float32)
+    at = at.astype(jnp.float32) * (1.0 / total_rows)
+    across = lax.broadcasted_iota(jnp.int32, (1, ey.shape[1]), 1)
+    keep_cols = (across < col_count).astype(jnp.float32)
+    across = across.astype(jnp.float32) * (1.0 / col_count)
+    for w in range(waves):
+        cosine, sine = cos_sin_turns(at * tilt_table[tilt_index[w], 0])
+        ex[2 * w] = cosine * keep
+        ex[2 * w + 1] = sine * keep
+        cosine, sine = cos_sin_turns(across * tilt_table[tilt_index[w], 1])
+        ey[2 * w : 2 * w + 1] = cosine * keep_cols
+        ey[2 * w + 1 : 2 * w + 2] = sine * keep_cols
 
 
 def first_kernel(waves, order, *refs):
@@ -113,8 +187,8 @@
                 for w in range(waves):
                     yr, yi = ey[2 * w : 2 * w + 1, lanes], ey[2 * w + 1 : 2 * w + 2, lanes]
                     ur, ui = cosine * yr - sine * yi, cosine * yi + sine * yr
-                    xr = ex[pl.ds(row, 32), 2 * w : 2 * w + 1]
-                    xi = ex[pl.ds(row, 32), 2 * w + 1 : 2 * w + 2]
+                    xr = ex[2 * w, pl.ds(row, 32)]
+                    xi = ex[2 * w + 1, pl.ds(row, 32)]
                     to = 256 * (blk + 1)
                     ring[w, pl.ds(row, 32), to : to + 128] = (ur * xr - ui * xi).astype(jnp.bfloat16)
                     ring[w, pl.ds(row, 32), to + 128 : to + 256] = (ur * xi + ui * xr).astype(
@@ -305,54 +379,51 @@
         pairs = [(i, i + offset) for i in range(lane_count) if 0 <= i + offset < lane_count]
         return lax.ppermute(value, "lat", pairs)
 
-    def chosen(step, start, rows):
-        return lax.dynamic_slice(
-            potential, (slice_order[step], start, 0), (1, rows, col_count)
-        )[0]
-
-    whole = chosen(0, 0, row_count)
+    rows1, rows2, rows3 = (row_count + 2 * HALO * k for k in (3, 2, 1))
+    anywhere = pl.BlockSpec(memory_space=pl.ANY)
+    in_vmem = pl.BlockSpec(memory_space=pltpu.VMEM)
+    in_smem = pl.BlockSpec(memory_space=pltpu.SMEM)
+    picked = pl.pallas_call(
+        functools.partial(pick_kernel, HALO),
+        name="pick_rows",
+        out_shape=[
+            jax.ShapeDtypeStruct((rows, col_count), potential.dtype)
+            for rows in (row_count, HALO, HALO, row_count, HALO, HALO)
+        ],
+        in_specs=[in_smem, anywhere],
+        out_specs=[anywhere] * 6,
+        scratch_shapes=[pltpu.SemaphoreType.DMA((6,))],
+        cost_estimate=pl.CostEstimate(flops=0, bytes_accessed=4 << 20, transcendentals=0),
+    )(slice_order, potential)
+    whole, high, low, second, third_high, third_low = picked
     up1, down1 = neighbour(whole, 1), neighbour(whole, -1)
-    up2 = neighbour(chosen(0, row_count - HALO, HALO), 2)
-    down2 = neighbour(chosen(0, 0, HALO), -2)
-    whole = chosen(1, 0, row_count)
-    second_up, second_down = neighbour(whole, 1), neighbour(whole, -1)
-    third_up = neighbour(chosen(2, row_count - HALO, HALO), 1)
-    third_down = neighbour(chosen(2, 0, HALO), -1)
-
-    rows1, rows2, rows3 = (row_count + 2 * HALO * k for k in (3, 2, 1))
-
-    def inside(halo_rows, count):
-        at = first_row - halo_rows + jnp.arange(count, dtype=jnp.int32)
-        return ((at >= 0) & (at < total_rows)).astype(jnp.float32), at
-
-    tilts = jnp.take(tilt_table, tilt_index, axis=0)
-    keep, at = inside(3 * HALO, rows1)
-    angle = 2.0 * math.pi * tilts[:, 0, None] * (at.astype(jnp.float32) / total_rows)
-    ex = jnp.stack([jnp.cos(angle), jnp.sin(angle)], axis=1).reshape(2 * waves, rows1) * keep
-    ex = jnp.pad(ex.T, ((0, 0), (0, 128 - 2 * waves)))
-    across = jnp.arange(col_count, dtype=jnp.float32) / col_count
-    angle = 2.0 * math.pi * tilts[:, 1, None] * across
-    ey = jnp.stack([jnp.cos(angle), jnp.sin(angle)], axis=1).reshape(2 * waves, col_count)
-    ey = jnp.pad(ey, ((0, 8 - 2 * waves), (0, STEP)))
-
-    band = column_band(fresnel_taps)
-    wide_band = column_band(ctf_taps)
-    full_rows = row_band(fresnel_taps, rows2, rows1, 1)
-
-    def stacked(count, count_in, halo_rows):
-        keep = inside(halo_rows, count)[0]
-        cut = full_rows[:, :count, :count_in] * keep[None, :, None]
-        return cut.reshape(2 * count, count_in).astype(jnp.bfloat16)
-
-    band2 = stacked(rows2, rows1, 2 * HALO)
-    band3 = stacked(rows3, rows2, HALO)
-    band4 = stacked(row_count, rows3, 0)
-    wide_rows = row_band(ctf_taps, 128, 256, 1).reshape(256, 256).astype(jnp.bfloat16)
-    mtf_reach = (mtf_taps.shape[0] - 1) // 2
-    at = jnp.arange(256, dtype=jnp.int32)
-    row_taps = spread_taps(mtf_taps, at[None, :] - at[:128, None] - 64 + mtf_reach)
-    at = jnp.arange(tile_cols, dtype=jnp.int32)
-    col_taps = spread_taps(mtf_taps, at[None, :] - at[:, None] + mtf_reach)
+    up2, down2 = neighbour(high, 2), neighbour(low, -2)
+    second_up, second_down = neighbour(second, 1), neighbour(second, -1)
+    third_up, third_down = neighbour(third_high, 1), neighbour(third_low, -1)
+
+    def made(shape, dtype):
+        return jax.ShapeDtypeStruct(shape, dtype)
+
+    band, wide_band, band2, band3, band4, wide_rows, row_taps, col_taps, ex, ey = pl.pallas_call(
+        functools.partial(prepare_kernel, waves, row_count, total_rows, col_count),
+        name="prepare",
+        out_shape=[
+            made((512, 256), jnp.bfloat16),
+            made((512, 256), jnp.bfloat16),
+            made((2 * rows2, rows1), jnp.bfloat16),
+            made((2 * rows3, rows2), jnp.bfloat16),
+            made((2 * row_count, rows3), jnp.bfloat16),
+            made((256, 256), jnp.bfloat16),
+            made((128, 256), jnp.float32),
+            made((tile_cols, tile_cols), jnp.float32),
+            made((2 * waves, rows1, 128), jnp.float32),
+            made((2 * waves, col_count + STEP), jnp.float32),
+        ],
+        in_specs=[in_smem] * 3 + [in_vmem] * 3,
+        out_specs=[in_vmem] * 10,
+        scratch_shapes=[pltpu.VMEM((8, 256), jnp.float32)],
+        cost_estimate=pl.CostEstimate(flops=1 << 31, bytes_accessed=2 << 20, transcendentals=0),
+    )(tilt_index, first_row[None], tilt_table, fresnel_taps, ctf_taps, mtf_taps[None])
 
     def clamp(g):
         return jnp.minimum(g, steps - 1)
@@ -392,8 +463,8 @@
                 mine(0, 0, row_count),
                 piece(row_count),
                 piece(HALO),
-                fixed(rows1, 128),
-                pl.BlockSpec((8, STEP), lambda g, *_: (0, g)),
+                fixed(2 * waves, rows1, 128),
+                pl.BlockSpec((2 * waves, STEP), lambda g, *_: (0, g)),
                 fixed(512, 256),
             ],
             out_specs=blocks(rows1),

time: 192 us -> 236 us (1.23)
  Pallas kernels: 67.9 us -> 134 us
  blocking collectives: 0 us -> 53.3 us
  matrix products: 23.1 us -> 0 us
  waiting for transfers between devices: 35.1 us -> 19 us
  local copies, waits for them, and re-layouts: 16.6 us -> 4.29 us
  starting transfers between devices: 30.4 us -> 20.7 us
  other arithmetic: 9.33 us -> 0 us
  between operations: 6.76 us -> 0.86 us
    pallas_call x0 -> x2, Pallas kernels: none -> 68.6 us  [the longest x1 65.4 us: local(): pl.pallas_call(functools.partial(pick_kernel, HALO), name='pick_rows', ou...]
    all_to_all x0 -> x1, blocking collectives: none -> 53.3 us  [local(): lax.all_to_all(focused, 'lat', split_axis=0, concat_axis=0, tiled=True)]
    all_to_all x1 -> x0, waiting for transfers between devices: 35.1 us -> none  [local(): lax.all_to_all(focused, 'lat', split_axis=0, concat_axis=0, tiled=True)]
    dot_general x6 -> x0, matrix products: 23.1 us -> none  [spread_taps(): return jnp.einsum('...k,iok->...io', tap_list, onehot, precision=highest)]
    ppermute x8, waiting for transfers between devices: 0.02 us -> 19 us  [neighbour(): return lax.ppermute(value, 'lat', pairs)]
    all_to_all x1 -> x0, starting transfers between devices: 6.43 us -> none  [local(): lax.all_to_all(focused, 'lat', split_axis=0, concat_axis=0, tiled=True)]
    squeeze x2 -> x0, local copies, waits for them, and re-layouts: 4.45 us -> none  [chosen(): lax.dynamic_slice(potential, (slice_order[step], start, 0), (1, rows, col...]
    convert_element_type x4 -> x0, local copies, waits for them, and re-layouts: 3.74 us -> none  [the longest x3 3.72 us: column_band(): return joined.reshape(512, 256).astype(jnp.bfloat16)]
  transfers between devices with their start and end apart: 9 -> 8, of which waited for: 1 -> 1; matrix products, arithmetic and copies ran while one was open for 23% -> 1% of each run, Pallas kernels for 20% -> 17%
where the time goes in v1:
time: 236 us; the launch traced here: 232 us
  Pallas kernels  134 us (57%)
  blocking collectives  53.3 us (23%)
  starting transfers between devices  20.7 us (9%)
  waiting for transfers between devices  19 us (8%)
  local copies, waits for them, and re-layouts  4.29 us (2%)
    pallas_call x1, Pallas kernels, local(): pl.pallas_call(functools.partial(pick_kernel, HALO), name='pick_rows', ou...  65.4 us
    all_to_all x1, blocking collectives, local(): lax.all_to_all(focused, 'lat', split_axis=0, concat_axis=0, tiled=True)  53.3 us
    pallas_call x1, Pallas kernels, local(): pl.pallas_call(functools.partial(third_kernel, waves, col_count), name='t...  24.4 us
    ppermute x8, starting transfers between devices, neighbour(): return lax.ppermute(value, 'lat', pairs)  20.7 us
    pallas_call x1, Pallas kernels, local(): pl.pallas_call(functools.partial(second_kernel, waves, col_count), name='...  19.6 us
    ppermute x8, waiting for transfers between devices, neighbour(): return lax.ppermute(value, 'lat', pairs)  19 us
    pallas_call x1, Pallas kernels, local(): pl.pallas_call(functools.partial(first_kernel, waves), name='first_step',...  16.4 us
    pallas_call x1, Pallas kernels, local(): pl.pallas_call(functools.partial(detector_kernel, waves), name='detector'...  5.28 us
  transfers between devices with their start and end apart: 8, of which 1 were waited for; matrix products, arithmetic and copies ran while one was open for 1% of the time, Pallas kernels for 17%

profile of v1, /device:TPU:13, one launch (start us, length us, event | category | flops | bytes accessed | tf_op | source)
XLA Modules:
  0.0 232.3 jit_solution(5732869202518950924)
XLA Ops:
  0.6 65.4 %pick_rows.1 = (bf16[64,4096]{1,0:T(8,128)(2,1)}, bf16[32,4096]{1,0:T(8,128)(2,1)}, bf16[32,4096]{1,0:T(8,128)(2,1)}, bf16[64,4096]{1,0:T(8,128)(2,1)}, bf16[32,...) custom-call(s32[3]{0:T(128)} %order.7, bf16[6,64,4096]{2,1,0:T(8,128)(2,1)} %refs_1_.3), custom_call_target="tpu_custom_call" | custom-call | bytes 4194304 | tf_op jit(solution)/shard_map/pick_rows/pallas_call | solution.py:386
  66.0 0.0 copy-start
  66.0 0.0 copy-start.1
  66.0 2.8 %collective-permute-start.6 = (bf16[64,4096]{1,0:T(8,128)(2,1)}, bf16[64,4096]{1,0:T(8,128)(2,1)}, u32[]{:S(2)}, u32[]{:S(2)}) collective-permute-start(bf16[64,4096]{1,0:T(8,128)(2,1)} %get-tuple-element.24), channel_id=1, source_target_pairs={{1,0},{2,1},{3,2},{4,3},{5,4},{6,5},{7,6},{8,7},{9,8},{10,9},{11,1... | collective-permute-start | bytes 1572872 | tf_op jit(solution)/shard_map/ppermute | solution.py:380
  68.9 3.9 %collective-permute-start.5 = (bf16[64,4096]{1,0:T(8,128)(2,1)}, bf16[64,4096]{1,0:T(8,128)(2,1)}, u32[]{:S(2)}, u32[]{:S(2)}) collective-permute-start(bf16[64,4096]{1,0:T(8,128)(2,1)} %get-tuple-element.24), channel_id=1, source_target_pairs={{0,1},{1,2},{2,3},{3,4},{4,5},{5,6},{6,7},{7,8},{8,9},{9,10},{10,1... | collective-permute-start | bytes 1572872 | tf_op jit(solution)/shard_map/ppermute | solution.py:380
  72.8 2.3 collective-permute-start.4
  75.1 3.0 %collective-permute-start.7 = (bf16[32,4096]{1,0:T(8,128)(2,1)}, bf16[32,4096]{1,0:T(8,128)(2,1)}, u32[]{:S(2)}, u32[]{:S(2)}) collective-permute-start(bf16[32,4096]{1,0:T(8,128)(2,1)} %get-tuple-element.25), channel_id=1, source_target_pairs={{2,0},{3,1},{4,2},{5,3},{6,4},{7,5},{8,6},{9,7},{10,8},{11,9},{12,... | collective-permute-start | bytes 786440 | tf_op jit(solution)/shard_map/ppermute | solution.py:380
  78.1 1.9 collective-permute-start.3
  80.0 1.4 copy.10.tilt_table
  81.4 19.0 %collective-permute-done.4.refs_0_ = bf16[32,4096]{1,0:T(8,128)(2,1)S(1)} collective-permute-done((bf16[32,4096]{1,0:T(8,128)(2,1)}, bf16[32,4096]{1,0:T(8,128)(2,1)S(1)}, u32[]{:S(2)}, u32[]{:S(2)}) %collective-permute-start.4) | collective-permute-done | bytes 262176 | tf_op jit(solution)/shard_map/ppermute | solution.py:380
  100.4 1.9 collective-permute-start.2
  102.3 3.2 %prepare.1 = (bf16[512,256]{1,0:T(8,128)(2,1)}, bf16[512,256]{1,0:T(8,128)(2,1)}, bf16[384,256]{1,0:T(8,128)(2,1)}, bf16[256,192]{1,0:T(8,128)(2,1)}, bf16[128,1...) custom-call(s32[2]{0:T(128)} %tilt_index.1, ...), custom_call_target="tpu_custom_call" | custom-call | flops 2147483648 | bytes 2097152 | tf_op jit(solution)/shard_map/prepare/pallas_call | solution.py:407
  105.5 0.0 collective-permute-done.7.refs_4_
  105.5 3.0 %collective-permute-start = (bf16[32,4096]{1,0:T(8,128)(2,1)}, bf16[32,4096]{1,0:T(8,128)(2,1)S(1)}, u32[]{:S(2)}, u32[]{:S(2)}) collective-permute-start(bf16[32,4096]{1,0:T(8,128)(2,1)} %get-tuple-element.20), channel_id=1, source_target_pairs={{0,1},{1,2},{2,3},{3,4},{4,5},{5,6},{6,7},{7,8},{8,9},{9,10},{10,1... | collective-permute-start | bytes 786440 | tf_op jit(solution)/shard_map/ppermute | solution.py:380
  108.5 0.0 collective-permute-done.6.refs_3_
  108.5 1.9 collective-permute-start.1
  110.4 0.0 collective-permute-done.5.refs_1_
  110.4 0.0 copy-done
  110.4 0.0 copy-done.1
  110.5 1.0 copy-done.3
  111.5 0.9 copy-done.4
  112.4 0.9 copy-done.6
  113.3 16.4 %first_step.1.refs_3_ = bf16[2,256,8704]{2,1,0:T(8,128)(2,1)} custom-call(s32[3]{0:T(128)S(1)} %copy-done.1, bf16[32,4096]{1,0:T(8,128)(2,1)S(1)} %collective-permute-done.4.refs_0_, bf16[64,4096]{1,0:T(8,128)(2,1)} %collective-permute-done.5.refs_1_, bf16[6,64,4096]{2,1,0:T(8,128)(2,1)S(1)} %copy-done, bf16[64,4096]{1,0:T(8,128)(2,1)} %collective-permute-done.6.refs_3_, ...), custom_call_target="tpu_custom_call" | custom-call | flops 4563402752 | bytes 12582912 | tf_op jit(solution)/shard_map/first_step/pallas_call | solution.py:453
  129.7 0.0 collective-permute-done.3.refs_2_
  129.7 0.0 collective-permute-done.2.refs_0_
  129.7 0.0 copy-start.2
  129.8 19.6 %second_step.1.refs_3_ = bf16[2,192,8704]{2,1,0:T(8,128)(2,1)} custom-call(s32[3]{0:T(128)S(1)} %copy-done.1, bf16[64,4096]{1,0:T(8,128)(2,1)} %collective-permute-done.2.refs_0_, bf16[6,64,4096]{2,1,0:T(8,128)(2,1)S(1)} %copy-done, bf16[64,4096]{1,0:T(8,128)(2,1)} %collective-permute-done.3.refs_2_, bf16[2,256,8704]{2,1,0:T(8,128)(2,1)} %first_step.1.refs_3_, ...), custom_call_target="tpu_custom_call" | custom-call | flops 6845104128 | bytes 16777216 | tf_op jit(solution)/shard_map/second_step/pallas_call | solution.py:477
  149.3 0.0 collective-permute-done.refs_0_
  149.3 0.0 collective-permute-done.1.refs_2_
  149.4 24.4 %third_step.1 = (f32[2,2,64,4096]{3,2,1,0:T(8,128)}, bf16[16,2,2,64,256]{4,3,2,1,0:T(8,128)(2,1)S(1)}) custom-call(s32[3]{0:T(128)S(1)} %copy-done.1, s32[16]{0:T(128)S(1)} %copy-done.2, bf16[32,4096]{1,0:T(8,128)(2,1)S(1)} %collective-permute-done.refs_0_, bf16[6,64,4096]{2,1,0:T(8,128)(2,1)} %refs_1_.3, ...), custom_call_target="tpu_custom_call" | custom-call | flops 6845104128 | bytes 16777216 | tf_op jit(solution)/shard_map/third_step/pallas_call | solution.py:517
  173.8 53.3 %all_to_all.5.tile_wave = bf16[16,2,2,64,256]{4,3,2,1,0:T(8,128)(2,1)S(1)} all-to-all(bf16[16,2,2,64,256]{4,3,2,1,0:T(8,128)(2,1)S(1)} %get-tuple-element.34), channel_id=1, replica_groups=mesh['lamella'=2,'lat'=16] {'lat'}, dimensions={0} | all-to-all | bytes 4194304 | tf_op jit(solution)/shard_map/all_to_all | solution.py:556
  227.1 5.3 %detector.1 = f32[256,1024]{1,0:T(8,128)} custom-call(bf16[16,2,2,64,256]{4,3,2,1,0:T(8,128)(2,1)S(1)} %all_to_all.5.tile_wave, bf16[256,256]{1,0:T(8,128)(2,1)S(1)} %copy-done.10, f32[128,256]{1,0:T(8,128)S(1)} %copy-done.11, f32[256,256]{1,0:T(8,128)S(1)} %copy-done.8), custom_call_target="tpu_custom_call" | custom-call | flops 8589934592 | bytes 4194304 | tf_op jit(solution)/shard_map/detector/pallas_call | solution.py:557
  (20 shorter events, 0.0 us)
Async XLA Ops:
  66.0 44.4 %copy-start = (bf16[6,64,4096]{2,1,0:T(8,128)(2,1)S(1)}, bf16[6,64,4096]{2,1,0:T(8,128)(2,1)}, u32[]{:S(2)}) copy-start(bf16[6,64,4096]{2,1,0:T(8,128)(2,1)} %refs_1_.3) | copy-start | bytes 9437188
  66.0 44.4 %copy-start.1 = (s32[3]{0:T(128)S(1)}, s32[3]{0:T(128)}, u32[]{:S(2)}) copy-start(s32[3]{0:T(128)} %order.7) | copy-start | bytes 40
  66.0 42.5 %collective-permute-start.6 = (bf16[64,4096]{1,0:T(8,128)(2,1)}, bf16[64,4096]{1,0:T(8,128)(2,1)}, u32[]{:S(2)}, u32[]{:S(2)}) collective-permute-start(bf16[64,4096]{1,0:T(8,128)(2,1)} %get-tuple-element.24), channel_id=1, source_target_pairs={{1,0},{2,1},{3,2},{4,3},{5,4},{6,5},{7,6},{8,7},{9,8},{10,9},{11,1... | collective-permute-start | bytes 1572872 | tf_op jit(solution)/shard_map/ppermute | solution.py:380
  68.9 41.5 %collective-permute-start.5 = (bf16[64,4096]{1,0:T(8,128)(2,1)}, bf16[64,4096]{1,0:T(8,128)(2,1)}, u32[]{:S(2)}, u32[]{:S(2)}) collective-permute-start(bf16[64,4096]{1,0:T(8,128)(2,1)} %get-tuple-element.24), channel_id=1, source_target_pairs={{0,1},{1,2},{2,3},{3,4},{4,5},{5,6},{6,7},{7,8},{8,9},{9,10},{10,1... | collective-permute-start | bytes 1572872 | tf_op jit(solution)/shard_map/ppermute | solution.py:380
  72.8 27.6 %collective-permute-start.4 = (bf16[32,4096]{1,0:T(8,128)(2,1)}, bf16[32,4096]{1,0:T(8,128)(2,1)S(1)}, u32[]{:S(2)}, u32[]{:S(2)}) collective-permute-start(bf16[32,4096]{1,0:T(8,128)(2,1)} %get-tuple-element.23), channel_id=1, source_target_pairs={{0,2},{1,3},{2,4},{3,5},{4,6},{5,7},{6,8},{7,9},{8,10},{9,11},{10,... | collective-permute-start | bytes 786440 | tf_op jit(solution)/shard_map/ppermute | solution.py:380
  75.1 30.4 %collective-permute-start.7 = (bf16[32,4096]{1,0:T(8,128)(2,1)}, bf16[32,4096]{1,0:T(8,128)(2,1)}, u32[]{:S(2)}, u32[]{:S(2)}) collective-permute-start(bf16[32,4096]{1,0:T(8,128)(2,1)} %get-tuple-element.25), channel_id=1, source_target_pairs={{2,0},{3,1},{4,2},{5,3},{6,4},{7,5},{8,6},{9,7},{10,8},{11,9},{12,... | collective-permute-start | bytes 786440 | tf_op jit(solution)/shard_map/ppermute | solution.py:380
  78.1 51.6 %collective-permute-start.3 = (bf16[64,4096]{1,0:T(8,128)(2,1)}, bf16[64,4096]{1,0:T(8,128)(2,1)}, u32[]{:S(2)}, u32[]{:S(2)}) collective-permute-start(bf16[64,4096]{1,0:T(8,128)(2,1)} %get-tuple-element.22), channel_id=1, source_target_pairs={{1,0},{2,1},{3,2},{4,3},{5,4},{6,5},{7,6},{8,7},{9,8},{10,9},{11,1... | collective-permute-start | bytes 1572872 | tf_op jit(solution)/shard_map/ppermute | solution.py:380
  100.4 29.3 %collective-permute-start.2 = (bf16[64,4096]{1,0:T(8,128)(2,1)}, bf16[64,4096]{1,0:T(8,128)(2,1)}, u32[]{:S(2)}, u32[]{:S(2)}) collective-permute-start(bf16[64,4096]{1,0:T(8,128)(2,1)} %get-tuple-element.22), channel_id=1, source_target_pairs={{0,1},{1,2},{2,3},{3,4},{4,5},{5,6},{6,7},{7,8},{8,9},{9,10},{10,1... | collective-permute-start | bytes 1572872 | tf_op jit(solution)/shard_map/ppermute | solution.py:380
  105.5 43.8 %collective-permute-start = (bf16[32,4096]{1,0:T(8,128)(2,1)}, bf16[32,4096]{1,0:T(8,128)(2,1)S(1)}, u32[]{:S(2)}, u32[]{:S(2)}) collective-permute-start(bf16[32,4096]{1,0:T(8,128)(2,1)} %get-tuple-element.20), channel_id=1, source_target_pairs={{0,1},{1,2},{2,3},{3,4},{4,5},{5,6},{6,7},{7,8},{8,9},{9,10},{10,1... | collective-permute-start | bytes 786440 | tf_op jit(solution)/shard_map/ppermute | solution.py:380
  108.5 40.8 %collective-permute-start.1 = (bf16[32,4096]{1,0:T(8,128)(2,1)}, bf16[32,4096]{1,0:T(8,128)(2,1)S(1)}, u32[]{:S(2)}, u32[]{:S(2)}) collective-permute-start(bf16[32,4096]{1,0:T(8,128)(2,1)} %get-tuple-element.21), channel_id=1, source_target_pairs={{1,0},{2,1},{3,2},{4,3},{5,4},{6,5},{7,6},{8,7},{9,8},{10,9},{11,1... | collective-permute-start | bytes 786440 | tf_op jit(solution)/shard_map/ppermute | solution.py:380
  110.4 1.0 copy-start.3
  111.5 0.9 copy-start.4
  112.4 0.9 copy-start.6
  113.3 16.4 %copy-start.5 = (bf16[512,256]{1,0:T(8,128)(2,1)S(1)}, bf16[512,256]{1,0:T(8,128)(2,1)}, u32[]{:S(2)}) copy-start(bf16[512,256]{1,0:T(8,128)(2,1)} %get-tuple-element.28.refs_7_.refs_5_) | copy-start | bytes 786436
  113.3 16.4 %copy-start.7 = (bf16[384,256]{1,0:T(8,128)(2,1)S(1)}, bf16[384,256]{1,0:T(8,128)(2,1)}, u32[]{:S(2)}) copy-start(bf16[384,256]{1,0:T(8,128)(2,1)} %get-tuple-element.29.refs_4_) | copy-start | bytes 589828
  129.7 19.6 %copy-start.2 = (s32[16]{0:T(128)S(1)}, s32[16]{0:T(128)}, u32[]{:S(2)}) copy-start(s32[16]{0:T(128)} %owner.1) | copy-start | bytes 196
  129.7 19.6 %copy-start.9 = (bf16[512,256]{1,0:T(8,128)(2,1)S(1)}, bf16[512,256]{1,0:T(8,128)(2,1)}, u32[]{:S(2)}) copy-start(bf16[512,256]{1,0:T(8,128)(2,1)} %get-tuple-element.32.refs_7_) | copy-start | bytes 786436
  129.7 19.6 %copy-start.12 = (bf16[256,192]{1,0:T(8,128)(2,1)S(1)}, bf16[256,192]{1,0:T(8,128)(2,1)}, u32[]{:S(2)}) copy-start(bf16[256,192]{1,0:T(8,128)(2,1)} %get-tuple-element.30.refs_4_) | copy-start | bytes 294916
  129.7 19.6 %copy-start.13 = (bf16[128,128]{1,0:T(8,128)(2,1)S(1)}, bf16[128,128]{1,0:T(8,128)(2,1)}, u32[]{:S(2)}) copy-start(bf16[128,128]{1,0:T(8,128)(2,1)} %get-tuple-element.31.refs_6_) | copy-start | bytes 98308
  173.8 53.3 %copy-start.8 = (f32[256,256]{1,0:T(8,128)S(1)}, f32[256,256]{1,0:T(8,128)}, u32[]{:S(2)}) copy-start(f32[256,256]{1,0:T(8,128)} %get-tuple-element.37.col_taps) | copy-start | bytes 786436
  173.8 53.3 %copy-start.10 = (bf16[256,256]{1,0:T(8,128)(2,1)S(1)}, bf16[256,256]{1,0:T(8,128)(2,1)}, u32[]{:S(2)}) copy-start(bf16[256,256]{1,0:T(8,128)(2,1)} %get-tuple-element.35.taps_band) | copy-start | bytes 393220
  173.8 53.3 %copy-start.11 = (f32[128,256]{1,0:T(8,128)S(1)}, f32[128,256]{1,0:T(8,128)}, u32[]{:S(2)}) copy-start(f32[128,256]{1,0:T(8,128)} %get-tuple-element.36.row_taps) | copy-start | bytes 393220

commit v2 on v1

--- a/solution.py
+++ b/solution.py
@@ -84,20 +84,6 @@
     return ((cols >= 0) & (cols < col_count)).astype(jnp.float32)
 
 
-def pick_kernel(halo, order, potential, *refs):
-    outs, sems = refs[:-1], refs[-1]
-    rows = potential.shape[1]
-    whole, low, high = pl.ds(0, rows), pl.ds(0, halo), pl.ds(rows - halo, halo)
-    picks = ((0, whole), (0, high), (0, low), (1, whole), (2, high), (2, low))
-    copies = []
-    for i, (step, part) in enumerate(picks):
-        copy = pltpu.make_async_copy(potential.at[order[step], part], outs[i], sems.at[i])
-        copy.start()
-        copies.append(copy)
-    for copy in copies:
-        copy.wait()
-
-
 def toeplitz(row, count, shift):
     wide = jnp.broadcast_to(row, (count, 256))
     return pltpu.roll(wide, shift % 256, 1, stride=1, stride_axis=0)
@@ -166,137 +152,179 @@
         ey[2 * w + 1 : 2 * w + 2] = sine * keep_cols
 
 
-def first_kernel(waves, order, *refs):
-    pieces, (ex, ey, band, out, ring) = refs[:5], refs[5:]
-
-    @pl.when(pl.program_id(0) == 0)
-    def _():
+def rows_of(piece, start, count, lanes):
+    if len(piece.shape) == 3:
+        found = piece[0, pl.ds(start, count), lanes]
+    else:
+        found = piece[pl.ds(start, count), lanes]
+    return found.astype(jnp.float32)
+
+
+def chunks(pieces, size):
+    row = 0
+    for piece in pieces:
+        for start in range(0, piece.shape[-2], size):
+            yield piece, start, row
+            row += size
+
+
+def columns_pass(ring, band):
+    waves, rows = ring.shape[:2]
+    pairs = [(w, blk) for w in range(waves) for blk in range(2)]
+    windows = [ring[w, :, 256 * blk : 256 * blk + 512] for w, blk in pairs]
+    result = dot(jnp.concatenate(windows, axis=0), band[...])
+    for w in range(waves):
+        ring[w, :, :256] = ring[w, :, 512:768]
+    return {pair: result[rows * i : rows * i + rows] for i, pair in enumerate(pairs)}
+
+
+def store_spread(spread, result):
+    for (w, blk), value in result.items():
+        spread[w, :, 256 * blk : 256 * blk + 256] = value.astype(jnp.bfloat16)
+
+
+def start_wave(pieces, ex, ey, ring, waves):
+    for piece, start, row in chunks(pieces, 32):
+        for blk in range(2):
+            lanes = pl.ds(128 * blk, 128)
+            cosine, sine = cos_sin(rows_of(piece, start, 32, lanes))
+            to = 256 * (blk + 1)
+            for w in range(waves):
+                yr, yi = ey[2 * w : 2 * w + 1, lanes], ey[2 * w + 1 : 2 * w + 2, lanes]
+                ur, ui = cosine * yr - sine * yi, cosine * yi + sine * yr
+                xr, xi = ex[2 * w, pl.ds(row, 32)], ex[2 * w + 1, pl.ds(row, 32)]
+                ring[w, pl.ds(row, 32), to : to + 128] = (ur * xr - ui * xi).astype(jnp.bfloat16)
+                ring[w, pl.ds(row, 32), to + 128 : to + 256] = (ur * xi + ui * xr).astype(
+                    jnp.bfloat16
+                )
+
+
+def transmit(pieces, product, ring, last, masks, turn):
+    waves, rows = ring.shape[:2]
+    low = lax.broadcasted_iota(jnp.int32, (32, 128), 1) < 64
+    for piece, start, row in chunks(pieces, 32):
+        here = pl.ds(row, 32)
+        found = [rows_of(piece, start, 32, pl.ds(128 * blk, 128)) for blk in range(2)]
+        if turn:
+            found = [pltpu.roll(value, 64, 1) for value in found]
+            phases = [jnp.where(low, last[here], found[0]), jnp.where(low, found[0], found[1])]
+        else:
+            phases = [last[here], found[0]]
+        last[here] = found[1]
+        for blk in range(2):
+            cosine, sine = cos_sin(phases[blk])
+            cosine, sine = cosine * masks[blk], sine * masks[blk]
+            to = 256 * (blk + 1)
+            for w in range(waves):
+                top = product[w, here, 256 * blk : 256 * blk + 256]
+                under = product[w, pl.ds(rows + row, 32), 256 * blk : 256 * blk + 256]
+                real, imag = top[:, :128] - under[:, 128:], top[:, 128:] + under[:, :128]
+                ring[w, here, to : to + 128] = (real * cosine - imag * sine).astype(jnp.bfloat16)
+                ring[w, here, to + 128 : to + 256] = (real * sine + imag * cosine).astype(
+                    jnp.bfloat16
+                )
+
+
+def steps_kernel(
+    waves, col_count, lag, order, owner, *refs
+):
+    first, second, third = refs[:5], refs[5:8], refs[8:11]
+    ex, ey, band, band2, band3, band4, wide_band, exit_wave, focused = refs[11:20]
+    ring1, ring2, ring3, spread1, spread2, product2, product3, waved, last2, last3, turned = refs[20:]
+    g = pl.program_id(0)
+
+    def clear(ring):
         ring[:, :, :256] = jnp.zeros((waves, ring.shape[1], 256), jnp.bfloat16)
-
-    for blk in range(2):
-        lanes = pl.ds(128 * blk, 128)
-        row = 0
-        for piece in pieces:
-            rows = piece.shape[-2]
-            for start in range(0, rows, 32):
-                if len(piece.shape) == 3:
-                    phase = piece[0, pl.ds(start, 32), lanes]
-                else:
-                    phase = piece[pl.ds(start, 32), lanes]
-                cosine, sine = cos_sin(phase.astype(jnp.float32))
-                for w in range(waves):
-                    yr, yi = ey[2 * w : 2 * w + 1, lanes], ey[2 * w + 1 : 2 * w + 2, lanes]
-                    ur, ui = cosine * yr - sine * yi, cosine * yi + sine * yr
-                    xr = ex[2 * w, pl.ds(row, 32)]
-                    xi = ex[2 * w + 1, pl.ds(row, 32)]
-                    to = 256 * (blk + 1)
-                    ring[w, pl.ds(row, 32), to : to + 128] = (ur * xr - ui * xi).astype(jnp.bfloat16)
-                    ring[w, pl.ds(row, 32), to + 128 : to + 256] = (ur * xi + ui * xr).astype(
-                        jnp.bfloat16
-                    )
-                row += 32
-    for w in range(waves):
-        for blk in range(2):
-            lanes = pl.ds(256 * blk, 256)
-            out[w, :, lanes] = dot(ring[w, :, 256 * blk : 256 * blk + 512], band[...]).astype(
-                jnp.bfloat16
-            )
-        ring[w, :, :256] = ring[w, :, 512:768]
-
-
-def gather_rows(pieces, lanes):
-    found = []
-    for piece in pieces:
-        if len(piece.shape) == 3:
-            found.append(piece[0, :, lanes])
-        else:
-            found.append(piece[:, lanes])
-    return jnp.concatenate(found, axis=0).astype(jnp.float32)
-
-
-def transmit(ring, product, phases, masks, waves, rows):
-    factors = []
-    for phase, mask in zip(phases, masks):
-        cosine, sine = cos_sin(phase)
-        factors.append((cosine * mask, sine * mask))
-    for w in range(waves):
-        for blk, (real, imag) in enumerate(split_parts(product[w], rows)):
-            cosine, sine = factors[blk]
-            to = 256 * (blk + 1)
-            ring[w, :, to : to + 128] = (real * cosine - imag * sine).astype(jnp.bfloat16)
-            ring[w, :, to + 128 : to + 256] = (real * sine + imag * cosine).astype(jnp.bfloat16)
-
-
-def second_kernel(waves, col_count, order, *refs):
-    pieces, (spread, rows_band, band, out, ring, last) = refs[:3], refs[3:]
-    g = pl.program_id(0)
 
     @pl.when(g == 0)
     def _():
-        ring[:, :, :256] = jnp.zeros((waves, ring.shape[1], 256), jnp.bfloat16)
-        last[...] = jnp.zeros_like(last)
-
-    rows = ring.shape[1]
-    low = lax.broadcasted_iota(jnp.int32, (rows, 128), 1) < 64
-    turned = [last[...]]
-    for blk in range(2):
-        turned.append(pltpu.roll(gather_rows(pieces, pl.ds(128 * blk, 128)), 64, 1))
-    last[...] = turned[2]
-    phases = [jnp.where(low, turned[0], turned[1]), jnp.where(low, turned[1], turned[2])]
-    masks = [lanes_inside(2 * g, 64, col_count), lanes_inside(2 * g + 1, 64, col_count)]
-    product = [dot(rows_band[...], spread[w]) for w in range(waves)]
-    transmit(ring, product, phases, masks, waves, rows)
-    for w in range(waves):
-        for blk in range(2):
-            out[w, :, 256 * blk : 256 * (blk + 1)] = dot(
-                ring[w, :, 256 * blk : 256 * blk + 512], band[...]
-            ).astype(jnp.bfloat16)
-        ring[w, :, :256] = ring[w, :, 512:768]
-
-
-def third_kernel(waves, col_count, order, owner, *refs):
-    pieces = refs[:3]
-    spread, rows_band, band, last_band, wide_band, exit_wave, focused, ring, last, waved, turned = refs[3:]
-    g = pl.program_id(0)
-
-    @pl.when(g == 0)
+        clear(ring1)
+
+    @pl.when(g == lag)
     def _():
-        ring[:, :, :256] = jnp.zeros((waves, ring.shape[1], 256), jnp.bfloat16)
-        waved[:, :, :256] = jnp.zeros((waves, waved.shape[1], 256), jnp.bfloat16)
+        clear(ring2)
+        last2[...] = jnp.zeros_like(last2)
+
+    @pl.when(g == 2 * lag)
+    def _():
+        clear(ring3)
+        clear(waved)
+        last3[...] = jnp.zeros_like(last3)
         turned[...] = jnp.zeros_like(turned)
-        last[...] = jnp.zeros_like(last)
-
-    rows, kept = ring.shape[1], waved.shape[1]
-    phases = [last[...], gather_rows(pieces, pl.ds(0, 128))]
-    last[...] = gather_rows(pieces, pl.ds(128, 128))
-    masks = [lanes_inside(2 * g - 1, 0, col_count), lanes_inside(2 * g, 0, col_count)]
-    product = [dot(rows_band[...], spread[w]) for w in range(waves)]
-    transmit(ring, product, phases, masks, waves, rows)
-    low = lax.broadcasted_iota(jnp.int32, (kept, 128), 1) < 64
-    masks = [lanes_inside(2 * g - 1, 64, col_count), lanes_inside(2 * g, 64, col_count)]
-    for w in range(waves):
-        for blk in range(2):
-            made = dot(ring[w, :, 256 * blk : 256 * blk + 512], band[...]).astype(jnp.bfloat16)
-            ((real, imag),) = split_parts(dot(last_band[...], made), kept)
-            to = 256 * (blk + 1)
-            for part, value in enumerate((real, imag)):
-                waved[w, :, to + 128 * part : to + 128 * part + 128] = (value * masks[blk]).astype(
-                    jnp.bfloat16
-                )
-                rolled = pltpu.roll(value, 64, 1)
-                exit_wave[w, part, :, 128 * blk : 128 * blk + 128] = jnp.where(
-                    low, turned[w, part], rolled
-                )
-                turned[w, part] = rolled
-            made = dot(waved[w, :, 256 * blk : 256 * blk + 512], wide_band[...]).astype(jnp.bfloat16)
+
+    def stage1():
+        start_wave(first, ex, ey, ring1, waves)
+        store_spread(spread1, columns_pass(ring1, band))
+
+    def stage2():
+        at = g - lag
+        masks = [lanes_inside(2 * at, 64, col_count), lanes_inside(2 * at + 1, 64, col_count)]
+        for w in range(waves):
+            product2[w] = dot(band2[...], spread1[w])
+        transmit(second, product2, ring2, last2, masks, True)
+        store_spread(spread2, columns_pass(ring2, band))
+
+    def stage3():
+        at = g - 2 * lag
+        masks = [lanes_inside(2 * at - 1, 0, col_count), lanes_inside(2 * at, 0, col_count)]
+        for w in range(waves):
+            product3[w] = dot(band3[...], spread2[w])
+        transmit(third, product3, ring3, last3, masks, False)
+        result = columns_pass(ring3, band)
+        kept = waved.shape[1]
+        low = lax.broadcasted_iota(jnp.int32, (kept, 128), 1) < 64
+        masks = [lanes_inside(2 * at - 1, 64, col_count), lanes_inside(2 * at, 64, col_count)]
+        for w in range(waves):
+            made = jnp.concatenate([result[w, 0], result[w, 1]], axis=1).astype(jnp.bfloat16)
+            for blk, parts in enumerate(split_parts(dot(band4[...], made), kept)):
+                to = 256 * (blk + 1)
+                for part, value in enumerate(parts):
+                    at_lane = to + 128 * part
+                    waved[w, :, at_lane : at_lane + 128] = (value * masks[blk]).astype(jnp.bfloat16)
+                    rolled = pltpu.roll(value, 64, 1)
+                    exit_wave[w, part, :, 128 * blk : 128 * blk + 128] = jnp.where(
+                        low, turned[w, part], rolled
+                    )
+                    turned[w, part] = rolled
+        for (w, blk), value in columns_pass(waved, wide_band).items():
             for part in range(2):
-                block = made[:, 128 * part : 128 * part + 128]
+                block = value[:, 128 * part : 128 * part + 128].astype(jnp.bfloat16)
                 if len(focused.shape) == 5:
                     focused[0, w, part, :, 128 * blk : 128 * blk + 128] = block
                 else:
                     focused[w, part, :, 128 * blk : 128 * blk + 128] = block
-        ring[w, :, :256] = ring[w, :, 512:768]
-        waved[w, :, :256] = waved[w, :, 512:768]
+
+    for stage in (stage1, stage2, stage3) if lag == 0 else (stage3, stage2, stage1):
+        stage()
+
+
+def pick_kernel(halo, order, potential, *refs):
+    outs, held, load_sems, sems = refs[:-3], refs[-3], refs[-2], refs[-1]
+    rows = potential.shape[1]
+    whole, low, high = pl.ds(0, rows), pl.ds(0, halo), pl.ds(rows - halo, halo)
+    both1, up2, down2, up_rest, down_rest = outs
+    after, beside = pl.ds(rows, halo), pl.ds(0, rows)
+    picks = (
+        (0, whole, both1, None), (0, high, up2, None), (0, low, down2, None),
+        (1, whole, up_rest, beside), (1, whole, down_rest, beside),
+        (2, high, up_rest, after), (2, low, down_rest, after),
+    )
+    loads = []
+    for step in range(3):
+        load = pltpu.make_async_copy(potential.at[order[step]], held.at[step], load_sems.at[step])
+        load.start()
+        loads.append(load)
+    copies = []
+    for i, (step, part, target, where) in enumerate(picks):
+        if loads[step] is not None:
+            loads[step].wait()
+            loads[step] = None
+        target = target if where is None else target.at[where]
+        copy = pltpu.make_async_copy(held.at[step, part], target, sems.at[i])
+        copy.start()
+        copies.append(copy)
+    for copy in copies:
+        copy.wait()
 
 
 def detector_kernel(waves, tile_wave, taps_band, row_taps, col_taps, out, padded):
@@ -388,18 +416,21 @@
         name="pick_rows",
         out_shape=[
             jax.ShapeDtypeStruct((rows, col_count), potential.dtype)
-            for rows in (row_count, HALO, HALO, row_count, HALO, HALO)
+            for rows in (row_count, HALO, HALO, row_count + HALO, row_count + HALO)
         ],
         in_specs=[in_smem, anywhere],
-        out_specs=[anywhere] * 6,
-        scratch_shapes=[pltpu.SemaphoreType.DMA((6,))],
+        out_specs=[anywhere] * 5,
+        scratch_shapes=[
+            pltpu.VMEM((3, row_count, col_count), potential.dtype),
+            pltpu.SemaphoreType.DMA((3,)),
+            pltpu.SemaphoreType.DMA((7,)),
+        ],
         cost_estimate=pl.CostEstimate(flops=0, bytes_accessed=4 << 20, transcendentals=0),
     )(slice_order, potential)
-    whole, high, low, second, third_high, third_low = picked
+    whole, high, low, rest_high, rest_low = picked
     up1, down1 = neighbour(whole, 1), neighbour(whole, -1)
     up2, down2 = neighbour(high, 2), neighbour(low, -2)
-    second_up, second_down = neighbour(second, 1), neighbour(second, -1)
-    third_up, third_down = neighbour(third_high, 1), neighbour(third_low, -1)
+    up_rest, down_rest = neighbour(rest_high, 1), neighbour(rest_low, -1)
 
     def made(shape, dtype):
         return jax.ShapeDtypeStruct(shape, dtype)
@@ -425,82 +456,24 @@
         cost_estimate=pl.CostEstimate(flops=1 << 31, bytes_accessed=2 << 20, transcendentals=0),
     )(tilt_index, first_row[None], tilt_table, fresnel_taps, ctf_taps, mtf_taps[None])
 
+    lag = 1
+
     def clamp(g):
-        return jnp.minimum(g, steps - 1)
-
-    def piece(rows):
-        return pl.BlockSpec((rows, STEP), lambda g, *_: (0, clamp(g)))
-
-    def mine(step, start, rows):
+        return jnp.clip(g, 0, steps - 1)
+
+    def piece(step, start, rows):
+        return pl.BlockSpec((rows, STEP), lambda g, *_: (start // rows, clamp(g - step * lag)))
+
+    def mine(step):
         return pl.BlockSpec(
-            (1, rows, STEP), lambda g, order, *_: (order[step], start // rows, clamp(g))
+            (1, row_count, STEP), lambda g, order, *_: (order[step], 0, clamp(g - step * lag))
         )
 
     def fixed(*shape):
         return pl.BlockSpec(shape, lambda g, *_: (0,) * len(shape))
 
-    def blocks(rows):
-        return pl.BlockSpec((waves, rows, 512), lambda g, *_: (0, 0, g))
-
-    params = pltpu.CompilerParams(
-        dimension_semantics=("arbitrary",), vmem_limit_bytes=48 * 1024 * 1024
-    )
-
-    def cost(flops, count):
-        return pl.CostEstimate(flops=flops, bytes_accessed=count, transcendentals=0)
-
-    spread_cols = (steps + 1) * 512
-    spread = pl.pallas_call(
-        functools.partial(first_kernel, waves),
-        name="first_step",
-        out_shape=jax.ShapeDtypeStruct((waves, rows1, spread_cols), jnp.bfloat16),
-        grid_spec=pltpu.PrefetchScalarGridSpec(
-            num_scalar_prefetch=1,
-            grid=(steps + 1,),
-            in_specs=[
-                piece(HALO),
-                piece(row_count),
-                mine(0, 0, row_count),
-                piece(row_count),
-                piece(HALO),
-                fixed(2 * waves, rows1, 128),
-                pl.BlockSpec((2 * waves, STEP), lambda g, *_: (0, g)),
-                fixed(512, 256),
-            ],
-            out_specs=blocks(rows1),
-            scratch_shapes=[pltpu.VMEM((waves, rows1, 768), jnp.bfloat16)],
-        ),
-        compiler_params=params,
-        cost_estimate=cost(waves * rows1 * spread_cols * 1024, 12 << 20),
-    )(slice_order, up2, up1, potential, down1, down2, ex, ey, band)
-
-    spread = pl.pallas_call(
-        functools.partial(second_kernel, waves, col_count),
-        name="second_step",
-        out_shape=jax.ShapeDtypeStruct((waves, rows2, spread_cols), jnp.bfloat16),
-        grid_spec=pltpu.PrefetchScalarGridSpec(
-            num_scalar_prefetch=1,
-            grid=(steps + 1,),
-            in_specs=[
-                piece(row_count),
-                mine(1, 0, row_count),
-                piece(row_count),
-                blocks(rows1),
-                fixed(2 * rows2, rows1),
-                fixed(512, 256),
-            ],
-            out_specs=blocks(rows2),
-            scratch_shapes=[
-                pltpu.VMEM((waves, rows2, 768), jnp.bfloat16),
-                pltpu.VMEM((rows2, 128), jnp.float32),
-            ],
-        ),
-        compiler_params=params,
-        cost_estimate=cost(waves * rows2 * spread_cols * 2048, 16 << 20),
-    )(slice_order, second_up, potential, second_down, spread, band2, band)
-
     def done(g):
-        return jnp.maximum(g - 1, 0)
+        return clamp(g - 1 - 2 * lag)
 
     placed = tile_cols == STEP
     if placed:
@@ -511,26 +484,38 @@
         )
     else:
         focused_shape = (waves, 2, row_count, col_count)
-        focused_spec = pl.BlockSpec(
-            (waves, 2, row_count, STEP), lambda g, *_: (0, 0, 0, done(g))
-        )
+        focused_spec = pl.BlockSpec((waves, 2, row_count, STEP), lambda g, *_: (0, 0, 0, done(g)))
+
+    def rings(rows, lanes, dtype=jnp.bfloat16):
+        return pltpu.VMEM((waves, rows, lanes), dtype)
+
     exit_wave, focused = pl.pallas_call(
-        functools.partial(third_kernel, waves, col_count),
-        name="third_step",
+        functools.partial(steps_kernel, waves, col_count, lag),
+        name="steps",
         out_shape=(
-            jax.ShapeDtypeStruct((waves, 2, row_count, col_count), jnp.float32),
-            jax.ShapeDtypeStruct(focused_shape, jnp.bfloat16),
+            made((waves, 2, row_count, col_count), jnp.float32),
+            made(focused_shape, jnp.bfloat16),
         ),
         grid_spec=pltpu.PrefetchScalarGridSpec(
             num_scalar_prefetch=2,
-            grid=(steps + 1,),
+            grid=(steps + 1 + 2 * lag,),
             in_specs=[
-                piece(HALO),
-                mine(2, 0, row_count),
-                piece(HALO),
-                blocks(rows2),
+                piece(0, 0, HALO),
+                piece(0, 0, row_count),
+                mine(0),
+                piece(0, 0, row_count),
+                piece(0, 0, HALO),
+                piece(1, 0, row_count),
+                mine(1),
+                piece(1, 0, row_count),
+                piece(2, row_count, HALO),
+                mine(2),
+                piece(2, row_count, HALO),
+                fixed(2 * waves, rows1, 128),
+                pl.BlockSpec((2 * waves, STEP), lambda g, *_: (0, jnp.minimum(g, steps))),
+                fixed(512, 256),
+                fixed(2 * rows2, rows1),
                 fixed(2 * rows3, rows2),
-                fixed(512, 256),
                 fixed(2 * row_count, rows3),
                 fixed(512, 256),
             ],
@@ -539,15 +524,32 @@
                 focused_spec,
             ),
             scratch_shapes=[
-                pltpu.VMEM((waves, rows3, 768), jnp.bfloat16),
+                rings(rows1, 768),
+                rings(rows2, 768),
+                rings(rows3, 768),
+                rings(rows1, 512),
+                rings(rows2, 512),
+                rings(2 * rows2, 512, jnp.float32),
+                rings(2 * rows3, 512, jnp.float32),
+                rings(row_count, 768),
+                pltpu.VMEM((rows2, 128), jnp.float32),
                 pltpu.VMEM((rows3, 128), jnp.float32),
-                pltpu.VMEM((waves, row_count, 768), jnp.bfloat16),
                 pltpu.VMEM((waves, 2, row_count, 128), jnp.float32),
             ],
         ),
-        compiler_params=params,
-        cost_estimate=cost(waves * rows3 * spread_cols * 3072, 16 << 20),
-    )(slice_order, owner, third_up, potential, third_down, spread, band3, band, band4, wide_band)
+        compiler_params=pltpu.CompilerParams(
+            dimension_semantics=("arbitrary",), vmem_limit_bytes=40 * 1024 * 1024
+        ),
+        cost_estimate=pl.CostEstimate(
+            flops=1 << 34, bytes_accessed=12 << 20, transcendentals=0
+        ),
+    )(
+        slice_order, owner,
+        up2, up1, potential, down1, down2,
+        up_rest, potential, down_rest,
+        up_rest, potential, down_rest,
+        ex, ey, band, band2, band3, band4, wide_band,
+    )
 
     if not placed:
         detector = narrow_tiles(focused, owner, wide_rows, row_taps, col_taps, lane_count)
@@ -562,7 +564,9 @@
         out_specs=pl.BlockSpec(memory_space=pltpu.VMEM),
         scratch_shapes=[pltpu.VMEM((total_rows + 128, tile_cols), jnp.float32)],
         compiler_params=pltpu.CompilerParams(vmem_limit_bytes=48 * 1024 * 1024),
-        cost_estimate=cost(1 << 33, 4 << 20),
+        cost_estimate=pl.CostEstimate(
+            flops=1 << 33, bytes_accessed=4 << 20, transcendentals=0
+        ),
     )(tile_wave, wide_rows, row_taps, col_taps)
     return exit_wave, detector[None]
 

time: 236 us -> 162 us (0.69)
  Pallas kernels: 134 us -> 58.5 us
  starting transfers between devices: 20.7 us -> 17.2 us
  blocking collectives: 53.3 us -> 56.3 us
  local copies, waits for them, and re-layouts: 4.29 us -> 7.13 us
    pallas_call x1, Pallas kernels: 65.4 us -> 3.78 us  [local(): pl.pallas_call(functools.partial(pick_kernel, HALO), name='pick_rows', ou...]
    pallas_call x3 -> x1, Pallas kernels: 60.3 us -> 46.2 us  [local(): pl.pallas_call(functools.partial(steps_kernel, waves, col_count, lag), na...]
    ppermute x8 -> x6, starting transfers between devices: 20.7 us -> 17.2 us  [neighbour(): return lax.ppermute(value, 'lat', pairs)]
    all_to_all x1, blocking collectives: 53.3 us -> 56.3 us  [local(): lax.all_to_all(focused, 'lat', split_axis=0, concat_axis=0, tiled=True)]
    unnamed x29, local copies, waits for them, and re-layouts: 4.29 us -> 7.13 us
    ppermute x8 -> x6, waiting for transfers between devices: 19 us -> 20.8 us  [neighbour(): return lax.ppermute(value, 'lat', pairs)]
  transfers between devices with their start and end apart: 8 -> 6, of which waited for: 1 -> 2; matrix products, arithmetic and copies ran while one was open for 1% -> 0% of each run, Pallas kernels for 17% -> 2%
where the time goes in v2:
time: 162 us; the launch traced here: 161 us
  Pallas kernels  58.5 us (36%)
  blocking collectives  56.3 us (35%)
  waiting for transfers between devices  20.8 us (13%)
  starting transfers between devices  17.2 us (11%)
  local copies, waits for them, and re-layouts  7.13 us (4%)
    all_to_all x1, blocking collectives, local(): lax.all_to_all(focused, 'lat', split_axis=0, concat_axis=0, tiled=True)  56.3 us
    pallas_call x1, Pallas kernels, local(): pl.pallas_call(functools.partial(steps_kernel, waves, col_count, lag), na...  46.2 us
    ppermute x6, waiting for transfers between devices, neighbour(): return lax.ppermute(value, 'lat', pairs)  20.8 us
    ppermute x6, starting transfers between devices, neighbour(): return lax.ppermute(value, 'lat', pairs)  17.2 us
    unnamed x29, local copies, waits for them, and re-layouts  7.13 us
    pallas_call x1, Pallas kernels, local(): pl.pallas_call(functools.partial(detector_kernel, waves), name='detector'...  5.28 us
    pallas_call x1, Pallas kernels, local(): pl.pallas_call(functools.partial(pick_kernel, HALO), name='pick_rows', ou...  3.78 us
  transfers between devices with their start and end apart: 6, of which 2 were waited for; matrix products, arithmetic and copies ran while one was open for 0% of the time, Pallas kernels for 2%

profile of v2, /device:TPU:13, one launch (start us, length us, event | category | flops | bytes accessed | tf_op | source)
XLA Modules:
  0.0 160.7 jit_solution(12405386630943310633)
XLA Ops:
  0.6 0.0 copy-start.13
  0.6 3.8 %pick_rows.1 = (bf16[64,4096]{1,0:T(8,128)(2,1)}, bf16[32,4096]{1,0:T(8,128)(2,1)}, bf16[32,4096]{1,0:T(8,128)(2,1)}, bf16[96,4096]{1,0:T(8,128)(2,1)}, bf16[96,4096]{1,0:T(8,128)(2,1)}) custom-call(s32[3]{0:T(128)} %order.3, bf16[6,64,4096]{2,1,0:T(8,128)(2,1)} %refs_9_.1), custom_call_target="tpu_custom_call" | custom-call | bytes 4194304 | tf_op jit(solution)/shard_map/pick_rows/pallas_call | solution.py:414
  4.4 3.7 %collective-permute-start.4 = (bf16[96,4096]{1,0:T(8,128)(2,1)}, bf16[96,4096]{1,0:T(8,128)(2,1)}, u32[]{:S(2)}, u32[]{:S(2)}) collective-permute-start(bf16[96,4096]{1,0:T(8,128)(2,1)} %get-tuple-element.22), channel_id=1, source_target_pairs={{0,1},{1,2},{2,3},{3,4},{4,5},{5,6},{6,7},{7,8},{8,9},{9,10},{10,1... | collective-permute-start | bytes 2359304 | tf_op jit(solution)/shard_map/ppermute | solution.py:408
  8.1 1.9 %collective-permute-start.5 = (bf16[96,4096]{1,0:T(8,128)(2,1)}, bf16[96,4096]{1,0:T(8,128)(2,1)}, u32[]{:S(2)}, u32[]{:S(2)}) collective-permute-start(bf16[96,4096]{1,0:T(8,128)(2,1)} %get-tuple-element.23), channel_id=1, source_target_pairs={{1,0},{2,1},{3,2},{4,3},{5,4},{6,5},{7,6},{8,7},{9,8},{10,9},{11,1... | collective-permute-start | bytes 2359304 | tf_op jit(solution)/shard_map/ppermute | solution.py:408
  10.1 3.1 %collective-permute-start = (bf16[32,4096]{1,0:T(8,128)(2,1)}, bf16[32,4096]{1,0:T(8,128)(2,1)S(1)}, u32[]{:S(2)}, u32[]{:S(2)}) collective-permute-start(bf16[32,4096]{1,0:T(8,128)(2,1)} %get-tuple-element.19), channel_id=1, source_target_pairs={{0,2},{1,3},{2,4},{3,5},{4,6},{5,7},{6,8},{7,9},{8,10},{9,11},{10,... | collective-permute-start | bytes 786440 | tf_op jit(solution)/shard_map/ppermute | solution.py:408
  13.2 3.7 %collective-permute-start.2 = (bf16[64,4096]{1,0:T(8,128)(2,1)}, bf16[64,4096]{1,0:T(8,128)(2,1)}, u32[]{:S(2)}, u32[]{:S(2)}) collective-permute-start(bf16[64,4096]{1,0:T(8,128)(2,1)} %get-tuple-element.20), channel_id=1, source_target_pairs={{1,0},{2,1},{3,2},{4,3},{5,4},{6,5},{7,6},{8,7},{9,8},{10,9},{11,1... | collective-permute-start | bytes 1572872 | tf_op jit(solution)/shard_map/ppermute | solution.py:408
  16.9 2.8 %collective-permute-start.1 = (bf16[64,4096]{1,0:T(8,128)(2,1)}, bf16[64,4096]{1,0:T(8,128)(2,1)}, u32[]{:S(2)}, u32[]{:S(2)}) collective-permute-start(bf16[64,4096]{1,0:T(8,128)(2,1)} %get-tuple-element.20), channel_id=1, source_target_pairs={{0,1},{1,2},{2,3},{3,4},{4,5},{5,6},{6,7},{7,8},{8,9},{9,10},{10,1... | collective-permute-start | bytes 1572872 | tf_op jit(solution)/shard_map/ppermute | solution.py:408
  19.7 17.9 %collective-permute-done.refs_0_ = bf16[32,4096]{1,0:T(8,128)(2,1)S(1)} collective-permute-done((bf16[32,4096]{1,0:T(8,128)(2,1)}, bf16[32,4096]{1,0:T(8,128)(2,1)S(1)}, u32[]{:S(2)}, u32[]{:S(2)}) %collective-permute-start) | collective-permute-done | bytes 262176 | tf_op jit(solution)/shard_map/ppermute | solution.py:408
  37.6 1.9 %collective-permute-start.3 = (bf16[32,4096]{1,0:T(8,128)(2,1)}, bf16[32,4096]{1,0:T(8,128)(2,1)}, u32[]{:S(2)}, u32[]{:S(2)}) collective-permute-start(bf16[32,4096]{1,0:T(8,128)(2,1)} %get-tuple-element.21), channel_id=1, source_target_pairs={{2,0},{3,1},{4,2},{5,3},{6,4},{7,5},{8,6},{9,7},{10,8},{11,9},{12,... | collective-permute-start | bytes 786440 | tf_op jit(solution)/shard_map/ppermute | solution.py:408
  39.5 0.0 copy-done.13
  39.5 0.7 copy.10.tilt_table
  40.2 3.2 %prepare.1 = (bf16[512,256]{1,0:T(8,128)(2,1)}, bf16[512,256]{1,0:T(8,128)(2,1)}, bf16[384,256]{1,0:T(8,128)(2,1)}, bf16[256,192]{1,0:T(8,128)(2,1)}, bf16[128,1...) custom-call(s32[2]{0:T(128)} %tilt_index.1, ...), custom_call_target="tpu_custom_call" | custom-call | flops 2147483648 | bytes 2097152 | tf_op jit(solution)/shard_map/prepare/pallas_call | solution.py:438
  43.4 2.9 %collective-permute-done.3.refs_4_ = bf16[32,4096]{1,0:T(8,128)(2,1)} collective-permute-done((bf16[32,4096]{1,0:T(8,128)(2,1)}, bf16[32,4096]{1,0:T(8,128)(2,1)}, u32[]{:S(2)}, u32[]{:S(2)}) %collective-permute-start.3) | collective-permute-done | bytes 262176 | tf_op jit(solution)/shard_map/ppermute | solution.py:408
  46.4 0.0 collective-permute-done.2.refs_3_
  46.4 0.0 collective-permute-done.1.refs_1_
  46.4 0.0 collective-permute-done.4.refs_5_.refs_8_
  46.4 0.0 collective-permute-done.5.refs_7_.refs_10_
  46.4 0.0 copy-done
  46.4 0.0 copy-done.1
  46.4 0.0 copy-done.2
  46.4 1.0 copy-done.3
  47.5 0.9 copy-done.5
  48.4 0.9 copy-done.6
  49.4 0.9 copy-done.7
  50.3 0.9 copy-done.10
  51.2 0.9 copy-done.11
  52.1 0.8 copy-done.12
  52.8 46.2 %steps.1 = (f32[2,2,64,4096]{3,2,1,0:T(8,128)}, bf16[16,2,2,64,256]{4,3,2,1,0:T(8,128)(2,1)S(1)}) custom-call(s32[3]{0:T(128)S(1)} %copy-done.1, s32[16]{0:T(128)S(1)} %copy-done.2, bf16[32,4096]{1,0:T(8,128)(2,1)S(1)} %collective-permute-done.refs_0_, bf16[64,4096]{1,0:T(8,128)(2,1)} %collective-permute-done.1.refs_1_, bf16[6,64,4096]{2,1,0:T(8,128)(2,1)S(1)} %copy-done, ...), custom_call_target="tpu_custom_call" | custom-call | flops 17179869184 | bytes 12582912 | tf_op jit(solution)/shard_map/steps/pallas_call | solution.py:492
  99.1 56.3 %all_to_all.5.tile_wave = bf16[16,2,2,64,256]{4,3,2,1,0:T(8,128)(2,1)S(1)} all-to-all(bf16[16,2,2,64,256]{4,3,2,1,0:T(8,128)(2,1)S(1)} %get-tuple-element.32), channel_id=1, replica_groups=mesh['lamella'=2,'lat'=16] {'lat'}, dimensions={0} | all-to-all | bytes 4194304 | tf_op jit(solution)/shard_map/all_to_all | solution.py:558
  155.4 0.0 copy-done.4
  155.4 0.0 copy-done.9
  155.4 5.3 %detector.1 = f32[256,1024]{1,0:T(8,128)} custom-call(bf16[16,2,2,64,256]{4,3,2,1,0:T(8,128)(2,1)S(1)} %all_to_all.5.tile_wave, bf16[256,256]{1,0:T(8,128)(2,1)S(1)} %copy-done.8, f32[128,256]{1,0:T(8,128)S(1)} %copy-done.9, f32[256,256]{1,0:T(8,128)S(1)} %copy-done.4), custom_call_target="tpu_custom_call" | custom-call | flops 8589934592 | bytes 4194304 | tf_op jit(solution)/shard_map/detector/pallas_call | solution.py:559
  (14 shorter events, 0.0 us)
Async XLA Ops:
  0.6 38.9 %copy-start.13 = (f32[41,2]{0,1:T(2,128)S(1)}, f32[41,2]{0,1:T(2,128)}, u32[]{:S(2)}) copy-start(f32[41,2]{0,1:T(2,128)} %param.11) | copy-start | bytes 988
  4.4 41.9 %collective-permute-start.4 = (bf16[96,4096]{1,0:T(8,128)(2,1)}, bf16[96,4096]{1,0:T(8,128)(2,1)}, u32[]{:S(2)}, u32[]{:S(2)}) collective-permute-start(bf16[96,4096]{1,0:T(8,128)(2,1)} %get-tuple-element.22), channel_id=1, source_target_pairs={{0,1},{1,2},{2,3},{3,4},{4,5},{5,6},{6,7},{7,8},{8,9},{9,10},{10,1... | collective-permute-start | bytes 2359304 | tf_op jit(solution)/shard_map/ppermute | solution.py:408
  8.1 38.2 %collective-permute-start.5 = (bf16[96,4096]{1,0:T(8,128)(2,1)}, bf16[96,4096]{1,0:T(8,128)(2,1)}, u32[]{:S(2)}, u32[]{:S(2)}) collective-permute-start(bf16[96,4096]{1,0:T(8,128)(2,1)} %get-tuple-element.23), channel_id=1, source_target_pairs={{1,0},{2,1},{3,2},{4,3},{5,4},{6,5},{7,6},{8,7},{9,8},{10,9},{11,1... | collective-permute-start | bytes 2359304 | tf_op jit(solution)/shard_map/ppermute | solution.py:408
  10.1 27.5 %collective-permute-start = (bf16[32,4096]{1,0:T(8,128)(2,1)}, bf16[32,4096]{1,0:T(8,128)(2,1)S(1)}, u32[]{:S(2)}, u32[]{:S(2)}) collective-permute-start(bf16[32,4096]{1,0:T(8,128)(2,1)} %get-tuple-element.19), channel_id=1, source_target_pairs={{0,2},{1,3},{2,4},{3,5},{4,6},{5,7},{6,8},{7,9},{8,10},{9,11},{10,... | collective-permute-start | bytes 786440 | tf_op jit(solution)/shard_map/ppermute | solution.py:408
  13.2 33.1 %collective-permute-start.2 = (bf16[64,4096]{1,0:T(8,128)(2,1)}, bf16[64,4096]{1,0:T(8,128)(2,1)}, u32[]{:S(2)}, u32[]{:S(2)}) collective-permute-start(bf16[64,4096]{1,0:T(8,128)(2,1)} %get-tuple-element.20), channel_id=1, source_target_pairs={{1,0},{2,1},{3,2},{4,3},{5,4},{6,5},{7,6},{8,7},{9,8},{10,9},{11,1... | collective-permute-start | bytes 1572872 | tf_op jit(solution)/shard_map/ppermute | solution.py:408
  16.9 29.4 %collective-permute-start.1 = (bf16[64,4096]{1,0:T(8,128)(2,1)}, bf16[64,4096]{1,0:T(8,128)(2,1)}, u32[]{:S(2)}, u32[]{:S(2)}) collective-permute-start(bf16[64,4096]{1,0:T(8,128)(2,1)} %get-tuple-element.20), channel_id=1, source_target_pairs={{0,1},{1,2},{2,3},{3,4},{4,5},{5,6},{6,7},{7,8},{8,9},{9,10},{10,1... | collective-permute-start | bytes 1572872 | tf_op jit(solution)/shard_map/ppermute | solution.py:408
  37.6 8.8 %collective-permute-start.3 = (bf16[32,4096]{1,0:T(8,128)(2,1)}, bf16[32,4096]{1,0:T(8,128)(2,1)}, u32[]{:S(2)}, u32[]{:S(2)}) collective-permute-start(bf16[32,4096]{1,0:T(8,128)(2,1)} %get-tuple-element.21), channel_id=1, source_target_pairs={{2,0},{3,1},{4,2},{5,3},{6,4},{7,5},{8,6},{9,7},{10,8},{11,9},{12,... | collective-permute-start | bytes 786440 | tf_op jit(solution)/shard_map/ppermute | solution.py:408
  40.2 6.2 %copy-start = (bf16[6,64,4096]{2,1,0:T(8,128)(2,1)S(1)}, bf16[6,64,4096]{2,1,0:T(8,128)(2,1)}, u32[]{:S(2)}) copy-start(bf16[6,64,4096]{2,1,0:T(8,128)(2,1)} %refs_9_.1) | copy-start | bytes 9437188
  40.2 6.2 %copy-start.1 = (s32[3]{0:T(128)S(1)}, s32[3]{0:T(128)}, u32[]{:S(2)}) copy-start(s32[3]{0:T(128)} %order.3) | copy-start | bytes 40
  40.2 6.2 %copy-start.2 = (s32[16]{0:T(128)S(1)}, s32[16]{0:T(128)}, u32[]{:S(2)}) copy-start(s32[16]{0:T(128)} %owner.1) | copy-start | bytes 196
  46.4 1.0 copy-start.3
  47.5 0.9 copy-start.5
  48.4 0.9 copy-start.6
  49.4 0.9 copy-start.7
  50.3 0.9 copy-start.10
  51.2 0.9 copy-start.11
  52.1 0.8 copy-start.12
  99.0 56.3 %copy-start.4 = (f32[256,256]{1,0:T(8,128)S(1)}, f32[256,256]{1,0:T(8,128)}, u32[]{:S(2)}) copy-start(f32[256,256]{1,0:T(8,128)} %get-tuple-element.35.col_taps) | copy-start | bytes 786436
  99.0 56.4 %copy-start.8 = (bf16[256,256]{1,0:T(8,128)(2,1)S(1)}, bf16[256,256]{1,0:T(8,128)(2,1)}, u32[]{:S(2)}) copy-start(bf16[256,256]{1,0:T(8,128)(2,1)} %get-tuple-element.33.taps_band) | copy-start | bytes 393220
  99.0 56.3 %copy-start.9 = (f32[128,256]{1,0:T(8,128)S(1)}, f32[128,256]{1,0:T(8,128)}, u32[]{:S(2)}) copy-start(f32[128,256]{1,0:T(8,128)} %get-tuple-element.34.row_taps) | copy-start | bytes 393220

commit v3 on v2

v3 whole, which is shorter than its diff:
```python
import functools
import math

import jax
import jax.numpy as jnp
from jax import lax
from jax.experimental import pallas as pl
from jax.experimental.pallas import tpu as pltpu
from jax.sharding import PartitionSpec as P

highest = lax.Precision.HIGHEST
SIN_TURN = (
    6.2831854820251465,
    -41.34170150756836,
    81.60513305664062,
    -76.70301818847656,
    42.02592849731445,
    -14.899847030639648,
    3.2381374835968018,
)
COS_TURN = (
    1.0,
    -19.73920440673828,
    64.93911743164062,
    -85.45014190673828,
    60.16762924194336,
    -25.967599868774414,
    6.528658390045166,
)
SIN_QUARTER = (
    0.4204482138156891,
    -0.004379667341709137,
    1.3686111742572393e-05,
    -2.0339173900651986e-08,
    1.679661791598175e-11,
)
COS_QUARTER = (
    1.6817927360534668,
    -0.052555955946445465,
    0.00027371387113817036,
    -5.690624220733298e-07,
    5.977824346636851e-10,
)
HALO = 32
STEP = 256


def horner(coefs, z):
    total = coefs[-1] * z + coefs[-2]
    for coef in coefs[-3::-1]:
        total = total * z + coef
    return total


def cos_sin_turns(turns):
    rest = turns - jnp.round(turns)
    z = rest * rest
    return horner(COS_TURN, z), horner(SIN_TURN, z) * rest


def cos_sin(phase):
    z = phase * phase
    quarter_sin = horner(SIN_QUARTER, z) * phase
    half_sin = quarter_sin * horner(COS_QUARTER, z)
    half_cos = math.sqrt(2.0) - quarter_sin * quarter_sin
    return 1.0 - half_sin * half_sin, half_sin * half_cos


def dot(a, b):
    return jnp.dot(a, b, preferred_element_type=jnp.float32)


def lanes_inside(block, shift, col_count):
    cols = block * 128 - shift + lax.broadcasted_iota(jnp.int32, (1, 128), 1)
    return ((cols >= 0) & (cols < col_count)).astype(jnp.float32)


def rows_of(ref, lead, start, count, lanes):
    if lead is None:
        found = ref[pl.ds(start, count), lanes]
    else:
        found = ref[lead, pl.ds(start, count), lanes]
    return found.astype(jnp.float32)


def chunks(pieces, size):
    row = 0
    for ref, lead, first, rows in pieces:
        for start in range(0, rows, size):
            yield ref, lead, first + start, row
            row += size


def columns_tasks(ring, band, store):
    waves = ring.shape[0]

    def task(w, blk):
        store(w, blk, dot(ring[w, :, 256 * blk : 256 * blk + 512], band[...]))
        if blk == 1:
            ring[w, :, :256] = ring[w, :, 512:768]

    return [functools.partial(task, w, blk) for w in range(waves) for blk in range(2)]


def spread_store(spread):
    rows = spread.shape[1] // 2

    def store(w, blk, value):
        lanes = pl.ds(128 * blk, 128)
        spread[w, :rows, lanes] = value[:, :128].astype(jnp.bfloat16)
        spread[w, rows:, lanes] = value[:, 128:].astype(jnp.bfloat16)

    return store


def rows_tasks(product, rows_band, spread):
    def task(w):
        product[w] = dot(rows_band[...], spread[w])

    return [functools.partial(task, w) for w in range(spread.shape[0])]


def run(*lists):
    for tasks in lists:
        for task in tasks:
            task()


def start_tasks(pieces, ex, ey, first_lane, ring):
    waves = ring.shape[0]

    def task(ref, lead, start, row):
        for blk in range(2):
            lanes = pl.ds(128 * blk, 128)
            cosine, sine = cos_sin(rows_of(ref, lead, start, 32, lanes))
            to = 256 * (blk + 1)
            for w in range(waves):
                at = pl.ds(first_lane + 128 * blk, 128)
                yr, yi = ey[2 * w : 2 * w + 1, at], ey[2 * w + 1 : 2 * w + 2, at]
                ur, ui = cosine * yr - sine * yi, cosine * yi + sine * yr
                xr, xi = ex[2 * w, pl.ds(row, 32)], ex[2 * w + 1, pl.ds(row, 32)]
                ring[w, pl.ds(row, 32), to : to + 128] = (ur * xr - ui * xi).astype(jnp.bfloat16)
                ring[w, pl.ds(row, 32), to + 128 : to + 256] = (ur * xi + ui * xr).astype(
                    jnp.bfloat16
                )

    return [functools.partial(task, *chunk) for chunk in chunks(pieces, 32)]


def transmit_tasks(pieces, product, ring, last, masks, turn):
    waves, rows = ring.shape[:2]

    def task(ref, lead, start, row):
        here = pl.ds(row, 32)
        found = [rows_of(ref, lead, start, 32, pl.ds(128 * blk, 128)) for blk in range(2)]
        if turn:
            low = lax.broadcasted_iota(jnp.int32, (32, 128), 1) < 64
            found = [pltpu.roll(value, 64, 1) for value in found]
            phases = [jnp.where(low, last[here], found[0]), jnp.where(low, found[0], found[1])]
        else:
            phases = [last[here], found[0]]
        last[here] = found[1]
        for blk in range(2):
            cosine, sine = cos_sin(phases[blk])
            cosine, sine = cosine * masks[blk], sine * masks[blk]
            to = 256 * (blk + 1)
            for w in range(waves):
                real = product[w, here, 128 * blk : 128 * blk + 128]
                imag = product[w, pl.ds(rows + row, 32), 128 * blk : 128 * blk + 128]
                ring[w, here, to : to + 128] = (real * cosine - imag * sine).astype(jnp.bfloat16)
                ring[w, here, to + 128 : to + 256] = (real * sine + imag * cosine).astype(
                    jnp.bfloat16
                )

    return [functools.partial(task, *chunk) for chunk in chunks(pieces, 32)]


def steps_kernel(waves, rows, col_count, begin, count, resumed, handed, order, owner, *refs):
    up2, up, own, down, down2, ex, ey, mats = refs[:8]
    refs = refs[8:]
    given, refs = (refs[:7], refs[9:]) if resumed else (None, refs)
    exit_wave, focused = refs[:2]
    given_on, refs = (refs[2:9], refs[9:]) if handed else (None, refs[2:])
    ring1, ring2, ring3, waved, last2, last3, turned = carried = refs[:7]
    spread1, spread2, spread3, product2, product3 = refs[7:]
    g = pl.program_id(0) + begin
    rings = carried[:4]

    @pl.when(g == begin)
    def _():
        for i, ref in enumerate(carried):
            if given is None:
                if i < 4:
                    ref[:, :, :256] = jnp.zeros((waves, ref.shape[1], 256), jnp.bfloat16)
                else:
                    ref[...] = jnp.zeros_like(ref)
            elif i < 4:
                ref[:, :, :256] = given[i][...]
            else:
                ref[...] = given[i][...]

    sizes = [ring.shape[1] for ring in rings]
    band2 = mats.at[pl.ds(0, 2 * sizes[1]), pl.ds(0, 2 * sizes[0])]
    at = 2 * sizes[1]
    band3 = mats.at[pl.ds(at, 2 * sizes[2]), pl.ds(0, 2 * sizes[1])]
    at += 2 * sizes[2]
    band4 = mats.at[pl.ds(at, 2 * sizes[3]), pl.ds(0, 2 * sizes[2])]
    at += 2 * sizes[3]
    band = mats.at[pl.ds(at, 512), pl.ds(0, 256)]
    wide_band = mats.at[pl.ds(at, 512), pl.ds(256, 256)]
    first = (
        (up2, None, 0, HALO), (up, None, 0, rows), (own, order[0], 0, rows),
        (down, None, 0, rows), (down2, None, 0, HALO),
    )
    second = ((up, None, rows, rows), (own, order[1], 0, rows), (down, None, rows, rows))
    third = (
        (up, None, 2 * rows, HALO), (own, order[2], 0, rows), (down, None, 2 * rows, HALO)
    )
    masks2 = [lanes_inside(2 * g + blk, 64, col_count) for blk in range(2)]
    masks3 = [lanes_inside(2 * g - 1 + blk, 0, col_count) for blk in range(2)]
    masks4 = [lanes_inside(2 * g - 1 + blk, 64, col_count) for blk in range(2)]
    kept = waved.shape[1]
    low = lax.broadcasted_iota(jnp.int32, (kept, 128), 1) < 64

    def exit_task(w):
        product = dot(band4[...], spread3[w])
        for blk in range(2):
            for part in range(2):
                value = product[kept * part : kept * part + kept, 128 * blk : 128 * blk + 128]
                lane = 256 * (blk + 1) + 128 * part
                waved[w, :, lane : lane + 128] = (value * masks4[blk]).astype(jnp.bfloat16)
                rolled = pltpu.roll(value, 64, 1)
                exit_wave[w, part, :, 128 * blk : 128 * blk + 128] = jnp.where(
                    low, turned[w, part], rolled
                )
                turned[w, part] = rolled

    def focused_store(w, blk, value):
        for part in range(2):
            block = value[:, 128 * part : 128 * part + 128].astype(jnp.bfloat16)
            if len(focused.shape) == 5:
                focused[0, w, part, :, 128 * blk : 128 * blk + 128] = block
            else:
                focused[w, part, :, 128 * blk : 128 * blk + 128] = block

    first_lane = pl.multiple_of(g * STEP, STEP)
    start = start_tasks(first, ex, ey, first_lane, ring1)
    run(start, columns_tasks(ring1, band, spread_store(spread1)))
    run(rows_tasks(product2, band2, spread1))
    run(transmit_tasks(second, product2, ring2, last2, masks2, True))
    run(columns_tasks(ring2, band, spread_store(spread2)))
    run(rows_tasks(product3, band3, spread2))
    run(transmit_tasks(third, product3, ring3, last3, masks3, False))
    run(columns_tasks(ring3, band, spread_store(spread3)))
    run([functools.partial(exit_task, w) for w in range(waves)])
    run(columns_tasks(waved, wide_band, focused_store))

    if handed:

        @pl.when(g == begin + count - 1)
        def _():
            for i, ref in enumerate(carried):
                given_on[i][...] = ref[:, :, :256] if i < 4 else ref[...]


def pick_kernel(halo, edges, order, potential, *refs):
    outs, held, load_sems, sems = refs[:-3], refs[-3], refs[-2], refs[-1]
    rows = potential.shape[1]
    loads = []
    for step in range(3):
        load = pltpu.make_async_copy(potential.at[order[step]], held.at[step], load_sems.at[step])
        load.start()
        loads.append(load)
    for load in loads:
        load.wait()
    copies = []
    for i, (left, right) in enumerate(zip(edges[:-1], edges[1:])):
        lanes = pl.ds(left, right - left)
        up, down, up2, down2 = outs[4 * i : 4 * i + 4]
        high, low = pl.ds(rows - halo, halo), pl.ds(0, halo)
        after = pl.ds(2 * rows, halo)
        pairs = []
        for target, part in ((up, high), (down, low)):
            for step in range(2):
                pairs.append((held.at[step, :, lanes], target.at[pl.ds(rows * step, rows)]))
            pairs.append((held.at[2, part, lanes], target.at[after]))
        pairs += [(held.at[0, high, lanes], up2), (held.at[0, low, lanes], down2)]
        for source, target in pairs:
            copy = pltpu.make_async_copy(source, target, sems.at[len(copies)])
            copy.start()
            copies.append(copy)
    for copy in copies:
        copy.wait()


def toeplitz(row, count, shift):
    wide = jnp.broadcast_to(row, (count, 256))
    return pltpu.roll(wide, shift % 256, 1, stride=1, stride_axis=0)


def inside_rows(first, count, total):
    at = first + lax.broadcasted_iota(jnp.int32, (count, 1), 0)
    return ((at >= 0) & (at < total)).astype(jnp.float32)


def prepare_kernel(
    waves, rows, total_rows, col_count, tilt_index, first_row, tilt_table, fresnel, ctf, mtf,
    mats, wide_rows, row_taps, col_taps, ex, ey, line,
):
    rows3, rows2, rows1 = (rows + 2 * HALO * k for k in (1, 2, 3))
    mats[...] = jnp.zeros_like(mats)
    at = 2 * rows2 + 2 * rows3 + 2 * rows
    band, wide_band = (mats.at[pl.ds(at, 512), pl.ds(256 * i, 256)] for i in range(2))
    band2 = mats.at[pl.ds(0, 2 * rows2), pl.ds(0, 2 * rows1)]
    band3 = mats.at[pl.ds(2 * rows2, 2 * rows3), pl.ds(0, 2 * rows2)]
    band4 = mats.at[pl.ds(2 * rows2 + 2 * rows3, 2 * rows), pl.ds(0, 2 * rows3)]
    line[...] = jnp.zeros_like(line)
    line[0:2, : fresnel.shape[1]] = fresnel[...].astype(jnp.bfloat16).astype(jnp.float32)
    line[2:4, : ctf.shape[1]] = ctf[...].astype(jnp.bfloat16).astype(jnp.float32)
    line[4:5, : mtf.shape[1]] = mtf[...]
    first = first_row[0]

    def columns(target, at, shift):
        for part in range(2):
            made = toeplitz(line[at + part : at + part + 1], 128, shift)
            for k in range(2):
                turned = jnp.transpose(made[:, 128 * k : 128 * k + 128])
                up, down = 256 * k, 256 * k + 128
                if part == 0:
                    target[up:down, :128] = turned.astype(jnp.bfloat16)
                    target[down : down + 128, 128:] = turned.astype(jnp.bfloat16)
                else:
                    target[up:down, 128:] = turned.astype(jnp.bfloat16)
                    target[down : down + 128, :128] = (-turned).astype(jnp.bfloat16)

    columns(band, 0, 65 - (fresnel.shape[1] + 1) // 2)
    columns(wide_band, 2, 65 - (ctf.shape[1] + 1) // 2)
    for target, halo in ((band2, 2 * HALO), (band3, HALO), (band4, 0)):
        count, count_in = target.shape[0] // 2, target.shape[1] // 2
        keep = inside_rows(first - halo, count, total_rows)
        for part in range(2):
            made = toeplitz(line[part : part + 1], count, HALO - (fresnel.shape[1] - 1) // 2) * keep
            made = made[:, :count_in].astype(jnp.bfloat16)
            if part == 0:
                target[:count, :count_in] = made
                target[count:, count_in:] = made
            else:
                target[:count, count_in:] = -made
                target[count:, :count_in] = made
    for part in range(2):
        made = toeplitz(line[2 + part : 3 + part], 128, 65 - (ctf.shape[1] + 1) // 2)
        wide_rows[128 * part : 128 * part + 128] = made.astype(jnp.bfloat16)
    reach = (mtf.shape[1] - 1) // 2
    row_taps[...] = toeplitz(line[4:5], 128, 64 - reach)
    width = col_taps.shape[0]
    off = lax.broadcasted_iota(jnp.int32, (width, 256), 1) - lax.broadcasted_iota(
        jnp.int32, (width, 256), 0
    )
    made = jnp.where(jnp.abs(off) <= reach, toeplitz(line[4:5], width, -reach), 0.0)
    col_taps[...] = made[:, :width]
    count = ex.shape[1]
    at = first - 3 * HALO + lax.broadcasted_iota(jnp.int32, (count, 128), 0)
    keep = ((at >= 0) & (at < total_rows)).astype(jnp.float32)
    at = at.astype(jnp.float32) * (1.0 / total_rows)
    across = lax.broadcasted_iota(jnp.int32, (1, ey.shape[1]), 1)
    keep_cols = (across < col_count).astype(jnp.float32)
    across = across.astype(jnp.float32) * (1.0 / col_count)
    for w in range(waves):
        cosine, sine = cos_sin_turns(at * tilt_table[tilt_index[w], 0])
        ex[2 * w] = cosine * keep
        ex[2 * w + 1] = sine * keep
        cosine, sine = cos_sin_turns(across * tilt_table[tilt_index[w], 1])
        ey[2 * w : 2 * w + 1] = cosine * keep_cols
        ey[2 * w + 1 : 2 * w + 2] = sine * keep_cols


def detector_kernel(waves, tile_wave, taps_band, row_taps, col_taps, out, padded):
    sources, rows, width = tile_wave.shape[0], tile_wave.shape[3], tile_wave.shape[4]
    total = sources * rows
    edge = jnp.zeros((64, width), jnp.float32)
    padded[:64] = edge
    padded[64 + total :] = edge
    for b in range(total // 128):
        image = None
        for w in range(waves):
            parts = []
            for part in range(2):
                window = []
                for k in range(2 * b - 1, 2 * b + 3):
                    if 0 <= k < total // 64:
                        window.append(tile_wave[k, w, part])
                    else:
                        window.append(jnp.zeros((64, width), jnp.bfloat16))
                parts.append(jnp.concatenate(window, axis=0))
            real, imag = dot(taps_band[...], parts[0]), dot(taps_band[...], parts[1])
            re = real[:128] - imag[128:]
            im = imag[:128] + real[128:]
            term = re * re + im * im
            image = term if image is None else image + term
        padded[64 + 128 * b : 192 + 128 * b] = image / waves
    for b in range(total // 128):
        rows_done = jnp.dot(
            row_taps[...],
            padded[128 * b : 128 * b + 256],
            precision=highest,
            preferred_element_type=jnp.float32,
        )
        out[:, 128 * b : 128 * b + 128] = lax.dot_general(
            col_taps[...],
            rows_done,
            (((1,), (1,)), ((), ())),
            precision=highest,
            preferred_element_type=jnp.float32,
        )


def block_windows(values):
    length = values.shape[-1]
    padded = jnp.pad(values, [(0, 0)] * (values.ndim - 1) + [(64, 64)])
    blocks = padded.reshape(values.shape[:-1] + (length // 128 + 1, 128))
    return jnp.concatenate([blocks[..., :-1, :], blocks[..., 1:, :]], axis=-1)


def narrow_tiles(focused, owner, wide_rows, row_taps, col_taps, lane_count):
    waves, _, rows, col_count = focused.shape
    width = col_count // lane_count
    slots = jnp.arange(lane_count, dtype=jnp.int32)
    placing = (owner[None, :] == slots[:, None]).astype(jnp.bfloat16)
    focused = focused.reshape(waves, 2, rows, lane_count, width)
    focused = jnp.einsum("jl,acrlk->jackr", placing, focused, preferred_element_type=jnp.float32)
    sent = focused.astype(jnp.bfloat16)
    tile_wave = lax.all_to_all(sent, "lat", split_axis=0, concat_axis=4, tiled=True)[0]
    windows = block_windows(tile_wave)
    taps_band = wide_rows.reshape(2, 128, 256)
    made = jnp.einsum("acwbi,doi->acdwbo", windows, taps_band, preferred_element_type=jnp.float32)
    real = made[:, 0, 0] - made[:, 1, 1]
    imag = made[:, 1, 0] + made[:, 0, 1]
    image = jnp.sum(real * real + imag * imag, axis=0) / waves
    image = image.reshape(width, lane_count * rows)
    blurred = jnp.einsum("wbi,oi->wbo", block_windows(image), row_taps, precision=highest)
    return jnp.dot(col_taps, blurred.reshape(width, lane_count * rows), precision=highest)


def local(potential, tilt_index, slice_order, tilt_table, fresnel_taps, ctf_taps, mtf_taps, owner):
    row_count, col_count = potential.shape[1:]
    lane_count = lax.axis_size("lat")
    total_rows = row_count * lane_count
    tile_cols = col_count // lane_count
    waves = tilt_index.shape[0]
    first_row = lax.axis_index("lat") * row_count
    steps = col_count // STEP

    def neighbour(value, offset):
        pairs = [(i, i + offset) for i in range(lane_count) if 0 <= i + offset < lane_count]
        return lax.ppermute(value, "lat", pairs)

    rows1, rows2, rows3 = (row_count + 2 * HALO * k for k in (3, 2, 1))
    anywhere = pl.BlockSpec(memory_space=pl.ANY)
    in_vmem = pl.BlockSpec(memory_space=pltpu.VMEM)
    in_smem = pl.BlockSpec(memory_space=pltpu.SMEM)
    widths = [steps // 2, steps - steps // 2]
    edges = [STEP * sum(widths[:i]) for i in range(len(widths) + 1)]
    sent_rows = (2 * row_count + HALO, 2 * row_count + HALO, HALO, HALO)
    picked = pl.pallas_call(
        functools.partial(pick_kernel, HALO, edges),
        name="pick_rows",
        out_shape=[
            jax.ShapeDtypeStruct((rows, STEP * width), potential.dtype)
            for width in widths
            for rows in sent_rows
        ],
        in_specs=[in_smem, anywhere],
        out_specs=[anywhere] * (4 * len(widths)),
        scratch_shapes=[
            pltpu.VMEM((3, row_count, col_count), potential.dtype),
            pltpu.SemaphoreType.DMA((3,)),
            pltpu.SemaphoreType.DMA((8 * len(widths),)),
        ],
        cost_estimate=pl.CostEstimate(flops=0, bytes_accessed=4 << 20, transcendentals=0),
    )(slice_order, potential)
    halos = [
        [neighbour(value, offset) for value, offset in zip(picked[4 * i : 4 * i + 4], (1, -1, 2, -2))]
        for i in range(len(widths))
    ]

    mats_shape = (2 * rows2 + 2 * rows3 + 2 * row_count + 512, 2 * rows1)

    def made(shape, dtype):
        return jax.ShapeDtypeStruct(shape, dtype)

    mats, wide_rows, row_taps, col_taps, ex, ey = pl.pallas_call(
        functools.partial(prepare_kernel, waves, row_count, total_rows, col_count),
        name="prepare",
        out_shape=[
            made(mats_shape, jnp.bfloat16),
            made((256, 256), jnp.bfloat16),
            made((128, 256), jnp.float32),
            made((tile_cols, tile_cols), jnp.float32),
            made((2 * waves, rows1, 128), jnp.float32),
            made((2 * waves, col_count + STEP), jnp.float32),
        ],
        in_specs=[in_smem] * 3 + [in_vmem] * 3,
        out_specs=[in_vmem] * 6,
        scratch_shapes=[pltpu.VMEM((8, 256), jnp.float32)],
        cost_estimate=pl.CostEstimate(flops=1 << 31, bytes_accessed=2 << 20, transcendentals=0),
    )(tilt_index, first_row[None], tilt_table, fresnel_taps, ctf_taps, mtf_taps[None])

    def clamp(g):
        return jnp.clip(g, 0, steps - 1)

    def fixed(*shape):
        return pl.BlockSpec(shape, lambda g, *_: (0,) * len(shape))

    placed = tile_cols == STEP
    if placed:
        focused_shape = (lane_count, waves, 2, row_count, tile_cols)
    else:
        focused_shape = (waves, 2, row_count, col_count)
    carried = [((waves, rows, 256), jnp.bfloat16) for rows in (rows1, rows2, rows3, row_count)]
    carried += [
        ((rows2, 128), jnp.float32),
        ((rows3, 128), jnp.float32),
        ((waves, 2, row_count, 128), jnp.float32),
    ]

    def ring(rows, lanes, dtype=jnp.bfloat16):
        return pltpu.VMEM((waves, rows, lanes), dtype)

    outputs = [
        made((waves, 2, row_count, col_count), jnp.float32),
        made(focused_shape, jnp.bfloat16),
    ]
    given = None
    for i, width in enumerate(widths):
        begin, last_call = edges[i] // STEP, i + 1 == len(widths)
        count = width + 1 if last_call else width

        def piece(rows, width=width):
            return pl.BlockSpec((rows, STEP), lambda g, *_: (0, jnp.minimum(g, width - 1)))

        def done(g, begin=begin):
            return clamp(g + begin - 1)

        if placed:
            focused_spec = pl.BlockSpec(
                (1, waves, 2, row_count, tile_cols),
                lambda g, order, owner, done=done: (owner[done(g)], 0, 0, 0, 0),
            )
        else:
            focused_spec = pl.BlockSpec(
                (waves, 2, row_count, STEP), lambda g, *_, done=done: (0, 0, 0, done(g))
            )
        up, down, up2, down2 = halos[i]
        args = [slice_order, owner, up2, up, potential, down, down2, ex, ey, mats]
        in_specs = [
            piece(HALO),
            piece(2 * row_count + HALO),
            pl.BlockSpec(
                (potential.shape[0], row_count, STEP),
                lambda g, *_, begin=begin: (0, 0, clamp(g + begin)),
            ),
            piece(2 * row_count + HALO),
            piece(HALO),
            fixed(*ex.shape),
            fixed(*ey.shape),
            fixed(*mats.shape),
        ]
        aliases = {}
        if given is not None:
            args += given
            in_specs += [fixed(*shape) for shape, _ in carried] + [anywhere, anywhere]
            aliases = {len(args) - 2: 0, len(args) - 1: 1}
        out_shape = list(outputs)
        out_specs = [
            pl.BlockSpec((waves, 2, row_count, STEP), lambda g, *_, done=done: (0, 0, 0, done(g))),
            focused_spec,
        ]
        if not last_call:
            out_shape += [made(shape, dtype) for shape, dtype in carried]
            out_specs += [fixed(*shape) for shape, _ in carried]
        results = pl.pallas_call(
            functools.partial(
                steps_kernel, waves, row_count, col_count, begin, count, given is not None, not last_call
            ),
            name="steps",
            out_shape=out_shape,
            grid_spec=pltpu.PrefetchScalarGridSpec(
                num_scalar_prefetch=2,
                grid=(count,),
                in_specs=in_specs,
                out_specs=out_specs,
                scratch_shapes=[ring(rows, 768) for rows in (rows1, rows2, rows3, row_count)]
                + [pltpu.VMEM(shape, dtype) for shape, dtype in carried[4:]]
                + [ring(2 * rows, 256) for rows in (rows1, rows2, rows3)]
                + [ring(2 * rows, 256, jnp.float32) for rows in (rows2, rows3)],
            ),
            input_output_aliases=aliases,
            compiler_params=pltpu.CompilerParams(
                dimension_semantics=("arbitrary",), vmem_limit_bytes=24 * 1024 * 1024
            ),
            cost_estimate=pl.CostEstimate(
                flops=count * (1 << 30), bytes_accessed=count << 19, transcendentals=0
            ),
        )(*args)
        given = list(results[2:]) + list(results[:2])
    exit_wave, focused = results[:2]

    if not placed:
        detector = narrow_tiles(focused, owner, wide_rows, row_taps, col_taps, lane_count)
        return exit_wave, detector[None]

    tile_wave = lax.all_to_all(focused, "lat", split_axis=0, concat_axis=0, tiled=True)
    detector = pl.pallas_call(
        functools.partial(detector_kernel, waves),
        name="detector",
        out_shape=jax.ShapeDtypeStruct((tile_cols, total_rows), jnp.float32),
        in_specs=[pl.BlockSpec(memory_space=pltpu.VMEM)] * 4,
        out_specs=pl.BlockSpec(memory_space=pltpu.VMEM),
        scratch_shapes=[pltpu.VMEM((total_rows + 128, tile_cols), jnp.float32)],
        compiler_params=pltpu.CompilerParams(vmem_limit_bytes=48 * 1024 * 1024),
        cost_estimate=pl.CostEstimate(
            flops=1 << 33, bytes_accessed=4 << 20, transcendentals=0
        ),
    )(tile_wave, wide_rows, row_taps, col_taps)
    return exit_wave, detector[None]


def solution(mesh):
    placed = (
        P(None, ("lamella", "lat"), None),
        P("lamella"),
        P("lamella"),
        P(),
        P(),
        P(),
        P(),
        P("lamella"),
    )
    return jax.shard_map(
        local,
        mesh=mesh,
        in_specs=placed,
        out_specs=(P(None, None, ("lamella", "lat"), None), P(("lamella", "lat"), None, None)),
        check_vma=False,
    )
```

time: 162 us -> 149 us (0.920)
  waiting for transfers between devices: 20.8 us -> 9.26 us
  starting transfers between devices: 17.2 us -> 20.8 us
  local copies, waits for them, and re-layouts: 7.13 us -> 3.98 us
    ppermute x6 -> x8, waiting for transfers between devices: 20.8 us -> 9.26 us  [neighbour(): return lax.ppermute(value, 'lat', pairs)]
    ppermute x6 -> x8, starting transfers between devices: 17.2 us -> 20.8 us  [neighbour(): return lax.ppermute(value, 'lat', pairs)]
    unnamed x29 -> x21, local copies, waits for them, and re-layouts: 7.13 us -> 3.98 us
    pallas_call x2 -> x3, Pallas kernels: 50 us -> 49.3 us  [the longest x2 45.3 us: local(): pl.pallas_call(functools.partial(steps_kernel, waves, row_count, col_coun...]
  transfers between devices with their start and end apart: 6 -> 8, of which waited for: 2 -> 1; matrix products, arithmetic and copies ran while one was open for 0% -> 0% of each run, Pallas kernels for 2% -> 17%
where the time goes in v3:
time: 149 us; the launch traced here: 148 us
  Pallas kernels  58 us (39%)
  blocking collectives  54.9 us (37%)
  starting transfers between devices  20.8 us (14%)
  waiting for transfers between devices  9.26 us (6%)
  local copies, waits for them, and re-layouts  3.98 us (3%)
    all_to_all x1, blocking collectives, local(): lax.all_to_all(focused, 'lat', split_axis=0, concat_axis=0, tiled=True)  54.9 us
    pallas_call x2, Pallas kernels, local(): pl.pallas_call(functools.partial(steps_kernel, waves, row_count, col_coun...  45.3 us
    ppermute x8, starting transfers between devices, neighbour(): return lax.ppermute(value, 'lat', pairs)  20.8 us
    ppermute x8, waiting for transfers between devices, neighbour(): return lax.ppermute(value, 'lat', pairs)  9.26 us
    pallas_call x1, Pallas kernels, local(): pl.pallas_call(functools.partial(detector_kernel, waves), name='detector'...  5.28 us
    unnamed x21, local copies, waits for them, and re-layouts  3.98 us
    pallas_call x1, Pallas kernels, local(): pl.pallas_call(functools.partial(pick_kernel, HALO, edges), name='pick_ro...  3.96 us
    pallas_call x1, Pallas kernels, local(): pl.pallas_call(functools.partial(prepare_kernel, waves, row_count, total_...  3.47 us
  transfers between devices with their start and end apart: 8, of which 1 were waited for; matrix products, arithmetic and copies ran while one was open for 0% of the time, Pallas kernels for 17%

profile of v3, /device:TPU:13, one launch (start us, length us, event | category | flops | bytes accessed | tf_op | source)
XLA Modules:
  0.0 147.7 jit_solution(10012246546421474784)
XLA Ops:
  0.6 0.0 copy-start.9
  0.6 4.0 %pick_rows.1 = (bf16[160,2048]{1,0:T(8,128)(2,1)}, bf16[160,2048]{1,0:T(8,128)(2,1)}, bf16[32,2048]{1,0:T(8,128)(2,1)}, bf16[32,2048]{1,0:T(8,128)(2,1)}, bf16[1...) custom-call(s32[3]{0:T(128)} %order.5, ...), custom_call_target="tpu_custom_call" | custom-call | bytes 4194304 | tf_op jit(solution)/shard_map/pick_rows/pallas_call | solution.py:464
  4.6 3.7 %collective-permute-start.5 = (bf16[160,2048]{1,0:T(8,128)(2,1)}, bf16[160,2048]{1,0:T(8,128)(2,1)}, u32[]{:S(2)}, u32[]{:S(2)}) collective-permute-start(bf16[160,2048]{1,0:T(8,128)(2,1)} %get-tuple-element.35), channel_id=1, source_target_pairs={{0,1},{1,2},{2,3},{3,4},{4,5},{5,6},{6,7},{7,8},{8,9},{9,10},{10,1... | collective-permute-start | bytes 1966088 | tf_op jit(solution)/shard_map/ppermute | solution.py:455
  8.3 1.9 %collective-permute-start.6 = (bf16[160,2048]{1,0:T(8,128)(2,1)}, bf16[160,2048]{1,0:T(8,128)(2,1)}, u32[]{:S(2)}, u32[]{:S(2)}) collective-permute-start(bf16[160,2048]{1,0:T(8,128)(2,1)} %get-tuple-element.36), channel_id=1, source_target_pairs={{1,0},{2,1},{3,2},{4,3},{5,4},{6,5},{7,6},{8,7},{9,8},{10,9},{11,1... | collective-permute-start | bytes 1966088 | tf_op jit(solution)/shard_map/ppermute | solution.py:455
  10.3 3.1 %collective-permute-start = (bf16[32,2048]{1,0:T(8,128)(2,1)}, bf16[32,2048]{1,0:T(8,128)(2,1)S(1)}, u32[]{:S(2)}, u32[]{:S(2)}) collective-permute-start(bf16[32,2048]{1,0:T(8,128)(2,1)} %get-tuple-element.27), channel_id=1, source_target_pairs={{0,2},{1,3},{2,4},{3,5},{4,6},{5,7},{6,8},{7,9},{8,10},{9,11},{10,... | collective-permute-start | bytes 393224 | tf_op jit(solution)/shard_map/ppermute | solution.py:455
  13.4 3.1 %collective-permute-start.4 = (bf16[32,2048]{1,0:T(8,128)(2,1)}, bf16[32,2048]{1,0:T(8,128)(2,1)S(1)}, u32[]{:S(2)}, u32[]{:S(2)}) collective-permute-start(bf16[32,2048]{1,0:T(8,128)(2,1)} %get-tuple-element.34), channel_id=1, source_target_pairs={{0,2},{1,3},{2,4},{3,5},{4,6},{5,7},{6,8},{7,9},{8,10},{9,11},{10,... | collective-permute-start | bytes 393224 | tf_op jit(solution)/shard_map/ppermute | solution.py:455
  16.6 2.1 %collective-permute-start.7 = (bf16[32,2048]{1,0:T(8,128)(2,1)}, bf16[32,2048]{1,0:T(8,128)(2,1)S(1)}, u32[]{:S(2)}, u32[]{:S(2)}) collective-permute-start(bf16[32,2048]{1,0:T(8,128)(2,1)} %get-tuple-element.37), channel_id=1, source_target_pairs={{2,0},{3,1},{4,2},{5,3},{6,4},{7,5},{8,6},{9,7},{10,8},{11,9},{12,... | collective-permute-start | bytes 393224 | tf_op jit(solution)/shard_map/ppermute | solution.py:455
  18.7 0.7 copy.12.tilt_table
  19.4 3.5 %prepare.1 = (bf16[1280,512]{1,0:T(8,128)(2,1)}, bf16[256,256]{1,0:T(8,128)(2,1)}, f32[128,256]{1,0:T(8,128)}, f32[256,256]{1,0:T(8,128)}, f32[4,256,128]{2,1,0:T(8,128)}, /*index=5*/f32[4,4352]{1,0:T(4,128)}) custom-call(s32[2]{0:T(128)} %tilt_index.1, s32[1]{0:T(128)} %bitcast.first_row, f32[41,2]{1,0:T(8,128)} %copy.12.tilt_table, f32[2,63]{1,0:T(2,128)} %fresnel.1, ...), custom_call_target="tpu_custom_call" | custom-call | flops 2147483648 | bytes 2097152 | tf_op jit(solution)/shard_map/prepare/pallas_call | solution.py:491
  22.9 9.2 %collective-permute-done.4.refs_0_ = bf16[32,2048]{1,0:T(8,128)(2,1)S(1)} collective-permute-done((bf16[32,2048]{1,0:T(8,128)(2,1)}, bf16[32,2048]{1,0:T(8,128)(2,1)S(1)}, u32[]{:S(2)}, u32[]{:S(2)}) %collective-permute-start.4) | collective-permute-done | bytes 131104 | tf_op jit(solution)/shard_map/ppermute | solution.py:455
  32.2 1.9 %collective-permute-start.3 = (bf16[32,2048]{1,0:T(8,128)(2,1)}, bf16[32,2048]{1,0:T(8,128)(2,1)S(1)}, u32[]{:S(2)}, u32[]{:S(2)}) collective-permute-start(bf16[32,2048]{1,0:T(8,128)(2,1)} %get-tuple-element.30), channel_id=1, source_target_pairs={{2,0},{3,1},{4,2},{5,3},{6,4},{7,5},{8,6},{9,7},{10,8},{11,9},{12,... | collective-permute-start | bytes 393224 | tf_op jit(solution)/shard_map/ppermute | solution.py:455
  34.1 0.0 collective-permute-done.7.refs_4_
  34.1 2.9 %collective-permute-start.1 = (bf16[160,2048]{1,0:T(8,128)(2,1)}, bf16[160,2048]{1,0:T(8,128)(2,1)S(1)}, u32[]{:S(2)}, u32[]{:S(2)}) collective-permute-start(bf16[160,2048]{1,0:T(8,128)(2,1)} %get-tuple-element.28), channel_id=1, source_target_pairs={{0,1},{1,2},{2,3},{3,4},{4,5},{5,6},{6,7},{7,8},{8,9},{9,10},{10,1... | collective-permute-start | bytes 1966088 | tf_op jit(solution)/shard_map/ppermute | solution.py:455
  37.0 0.0 collective-permute-done.5.refs_1_
  37.0 1.9 %collective-permute-start.2 = (bf16[160,2048]{1,0:T(8,128)(2,1)}, bf16[160,2048]{1,0:T(8,128)(2,1)S(1)}, u32[]{:S(2)}, u32[]{:S(2)}) collective-permute-start(bf16[160,2048]{1,0:T(8,128)(2,1)} %get-tuple-element.29), channel_id=1, source_target_pairs={{1,0},{2,1},{3,2},{4,3},{5,4},{6,5},{7,6},{8,7},{9,8},{10,9},{11,1... | collective-permute-start | bytes 1966088 | tf_op jit(solution)/shard_map/ppermute | solution.py:455
  38.9 0.0 collective-permute-done.6.refs_3_
  38.9 0.0 copy-done
  38.9 0.0 copy-done.1
  38.9 0.0 copy-done.2
  39.0 0.0 copy-start.3
  39.0 1.3 copy-done.3
  40.3 1.0 copy-done.4
  41.3 0.9 copy-done.8
  42.2 21.8 %steps.2 = (f32[2,2,64,4096]{3,2,1,0:T(8,128)}, bf16[16,2,2,64,256]{4,3,2,1,0:T(8,128)(2,1)S(1)}, bf16[2,256,256]{2,1,0:T(8,128)(2,1)S(1)}, bf16[2,192,256]{2,1,...) custom-call(s32[3]{0:T(128)S(1)} %copy-done.1, ...), custom_call_target="tpu_custom_call" | custom-call | flops 8589934592 | bytes 4194304 | tf_op jit(solution)/shard_map/steps/pallas_call | solution.py:581
  64.0 0.0 collective-permute-done.refs_0_
  64.0 0.0 collective-permute-done.3.refs_4_
  64.0 0.0 collective-permute-done.1.refs_1_
  64.0 0.0 collective-permute-done.2.refs_3_
  64.1 23.5 %steps.3 = (f32[2,2,64,4096]{3,2,1,0:T(8,128)}, bf16[16,2,2,64,256]{4,3,2,1,0:T(8,128)(2,1)S(1)}) custom-call(s32[3]{0:T(128)S(1)} %copy-done.1, s32[16]{0:T(128)S(1)} %copy-done.2, bf16[32,2048]{1,0:T(8,128)(2,1)S(1)} %collective-permute-done.refs_0_, ...), custom_call_target="tpu_custom_call", output_to_operand_aliasing={{0}: (17, {}), {1}: (18, {})} | custom-call | flops 9663676416 | bytes 4718592 | tf_op jit(solution)/shard_map/steps/pallas_call | solution.py:581
  87.6 54.9 %all_to_all.5.tile_wave = bf16[16,2,2,64,256]{4,3,2,1,0:T(8,128)(2,1)S(1)} all-to-all(bf16[16,2,2,64,256]{4,3,2,1,0:T(8,128)(2,1)S(1)} %get-tuple-element.48), channel_id=1, replica_groups=mesh['lamella'=2,'lat'=16] {'lat'}, dimensions={0} | all-to-all | bytes 4194304 | tf_op jit(solution)/shard_map/all_to_all | solution.py:612
  142.4 0.0 copy-done.5
  142.4 5.3 %detector.1 = f32[256,1024]{1,0:T(8,128)} custom-call(bf16[16,2,2,64,256]{4,3,2,1,0:T(8,128)(2,1)S(1)} %all_to_all.5.tile_wave, bf16[256,256]{1,0:T(8,128)(2,1)S(1)} %copy-done.6, f32[128,256]{1,0:T(8,128)S(1)} %copy-done.7, f32[256,256]{1,0:T(8,128)S(1)} %copy-done.5), custom_call_target="tpu_custom_call" | custom-call | flops 8589934592 | bytes 4194304 | tf_op jit(solution)/shard_map/detector/pallas_call | solution.py:613
  (11 shorter events, 0.0 us)
Async XLA Ops:
  0.6 18.1 %copy-start.9 = (f32[41,2]{0,1:T(2,128)S(1)}, f32[41,2]{0,1:T(2,128)}, u32[]{:S(2)}) copy-start(f32[41,2]{0,1:T(2,128)} %param.11) | copy-start | bytes 988
  4.6 32.4 %collective-permute-start.5 = (bf16[160,2048]{1,0:T(8,128)(2,1)}, bf16[160,2048]{1,0:T(8,128)(2,1)}, u32[]{:S(2)}, u32[]{:S(2)}) collective-permute-start(bf16[160,2048]{1,0:T(8,128)(2,1)} %get-tuple-element.35), channel_id=1, source_target_pairs={{0,1},{1,2},{2,3},{3,4},{4,5},{5,6},{6,7},{7,8},{8,9},{9,10},{10,1... | collective-permute-start | bytes 1966088 | tf_op jit(solution)/shard_map/ppermute | solution.py:455
  8.3 30.6 %collective-permute-start.6 = (bf16[160,2048]{1,0:T(8,128)(2,1)}, bf16[160,2048]{1,0:T(8,128)(2,1)}, u32[]{:S(2)}, u32[]{:S(2)}) collective-permute-start(bf16[160,2048]{1,0:T(8,128)(2,1)} %get-tuple-element.36), channel_id=1, source_target_pairs={{1,0},{2,1},{3,2},{4,3},{5,4},{6,5},{7,6},{8,7},{9,8},{10,9},{11,1... | collective-permute-start | bytes 1966088 | tf_op jit(solution)/shard_map/ppermute | solution.py:455
  10.3 53.8 %collective-permute-start = (bf16[32,2048]{1,0:T(8,128)(2,1)}, bf16[32,2048]{1,0:T(8,128)(2,1)S(1)}, u32[]{:S(2)}, u32[]{:S(2)}) collective-permute-start(bf16[32,2048]{1,0:T(8,128)(2,1)} %get-tuple-element.27), channel_id=1, source_target_pairs={{0,2},{1,3},{2,4},{3,5},{4,6},{5,7},{6,8},{7,9},{8,10},{9,11},{10,... | collective-permute-start | bytes 393224 | tf_op jit(solution)/shard_map/ppermute | solution.py:455
  13.4 18.7 %collective-permute-start.4 = (bf16[32,2048]{1,0:T(8,128)(2,1)}, bf16[32,2048]{1,0:T(8,128)(2,1)S(1)}, u32[]{:S(2)}, u32[]{:S(2)}) collective-permute-start(bf16[32,2048]{1,0:T(8,128)(2,1)} %get-tuple-element.34), channel_id=1, source_target_pairs={{0,2},{1,3},{2,4},{3,5},{4,6},{5,7},{6,8},{7,9},{8,10},{9,11},{10,... | collective-permute-start | bytes 393224 | tf_op jit(solution)/shard_map/ppermute | solution.py:455
  16.6 17.5 %collective-permute-start.7 = (bf16[32,2048]{1,0:T(8,128)(2,1)}, bf16[32,2048]{1,0:T(8,128)(2,1)S(1)}, u32[]{:S(2)}, u32[]{:S(2)}) collective-permute-start(bf16[32,2048]{1,0:T(8,128)(2,1)} %get-tuple-element.37), channel_id=1, source_target_pairs={{2,0},{3,1},{4,2},{5,3},{6,4},{7,5},{8,6},{9,7},{10,8},{11,9},{12,... | collective-permute-start | bytes 393224 | tf_op jit(solution)/shard_map/ppermute | solution.py:455
  19.4 19.5 %copy-start = (bf16[6,64,4096]{2,1,0:T(8,128)(2,1)S(1)}, bf16[6,64,4096]{2,1,0:T(8,128)(2,1)}, u32[]{:S(2)}) copy-start(bf16[6,64,4096]{2,1,0:T(8,128)(2,1)} %refs_2_.3) | copy-start | bytes 9437188
  19.4 19.5 %copy-start.1 = (s32[3]{0:T(128)S(1)}, s32[3]{0:T(128)}, u32[]{:S(2)}) copy-start(s32[3]{0:T(128)} %order.5) | copy-start | bytes 40
  19.4 19.5 %copy-start.2 = (s32[16]{0:T(128)S(1)}, s32[16]{0:T(128)}, u32[]{:S(2)}) copy-start(s32[16]{0:T(128)} %owner.3) | copy-start | bytes 196
  32.2 31.9 %collective-permute-start.3 = (bf16[32,2048]{1,0:T(8,128)(2,1)}, bf16[32,2048]{1,0:T(8,128)(2,1)S(1)}, u32[]{:S(2)}, u32[]{:S(2)}) collective-permute-start(bf16[32,2048]{1,0:T(8,128)(2,1)} %get-tuple-element.30), channel_id=1, source_target_pairs={{2,0},{3,1},{4,2},{5,3},{6,4},{7,5},{8,6},{9,7},{10,8},{11,9},{12,... | collective-permute-start | bytes 393224 | tf_op jit(solution)/shard_map/ppermute | solution.py:455
  34.1 29.9 %collective-permute-start.1 = (bf16[160,2048]{1,0:T(8,128)(2,1)}, bf16[160,2048]{1,0:T(8,128)(2,1)S(1)}, u32[]{:S(2)}, u32[]{:S(2)}) collective-permute-start(bf16[160,2048]{1,0:T(8,128)(2,1)} %get-tuple-element.28), channel_id=1, source_target_pairs={{0,1},{1,2},{2,3},{3,4},{4,5},{5,6},{6,7},{7,8},{8,9},{9,10},{10,1... | collective-permute-start | bytes 1966088 | tf_op jit(solution)/shard_map/ppermute | solution.py:455
  37.0 27.1 %collective-permute-start.2 = (bf16[160,2048]{1,0:T(8,128)(2,1)}, bf16[160,2048]{1,0:T(8,128)(2,1)S(1)}, u32[]{:S(2)}, u32[]{:S(2)}) collective-permute-start(bf16[160,2048]{1,0:T(8,128)(2,1)} %get-tuple-element.29), channel_id=1, source_target_pairs={{1,0},{2,1},{3,2},{4,3},{5,4},{6,5},{7,6},{8,7},{9,8},{10,9},{11,1... | collective-permute-start | bytes 1966088 | tf_op jit(solution)/shard_map/ppermute | solution.py:455
  39.0 1.3 copy-start.3
  40.3 1.0 copy-start.4
  41.3 0.9 copy-start.8
  87.6 54.9 %copy-start.5 = (f32[256,256]{1,0:T(8,128)S(1)}, f32[256,256]{1,0:T(8,128)}, u32[]{:S(2)}) copy-start(f32[256,256]{1,0:T(8,128)} %get-tuple-element.51.col_taps) | copy-start | bytes 786436
  87.6 54.9 %copy-start.6 = (bf16[256,256]{1,0:T(8,128)(2,1)S(1)}, bf16[256,256]{1,0:T(8,128)(2,1)}, u32[]{:S(2)}) copy-start(bf16[256,256]{1,0:T(8,128)(2,1)} %get-tuple-element.49.taps_band) | copy-start | bytes 393220
  87.6 54.9 %copy-start.7 = (f32[128,256]{1,0:T(8,128)S(1)}, f32[128,256]{1,0:T(8,128)}, u32[]{:S(2)}) copy-start(f32[128,256]{1,0:T(8,128)} %get-tuple-element.50.row_taps) | copy-start | bytes 393220

commit v4 on v3

--- a/solution.py
+++ b/solution.py
@@ -126,7 +126,7 @@
             task()
 
 
-def start_tasks(pieces, ex, ey, first_lane, ring):
+def start_tasks(pieces, ex, ey, first_lane, first_wave, ring):
     waves = ring.shape[0]
 
     def task(ref, lead, start, row):
@@ -136,9 +136,10 @@
             to = 256 * (blk + 1)
             for w in range(waves):
                 at = pl.ds(first_lane + 128 * blk, 128)
-                yr, yi = ey[2 * w : 2 * w + 1, at], ey[2 * w + 1 : 2 * w + 2, at]
+                v = 2 * (w + first_wave)
+                yr, yi = ey[v : v + 1, at], ey[v + 1 : v + 2, at]
                 ur, ui = cosine * yr - sine * yi, cosine * yi + sine * yr
-                xr, xi = ex[2 * w, pl.ds(row, 32)], ex[2 * w + 1, pl.ds(row, 32)]
+                xr, xi = ex[v, pl.ds(row, 32)], ex[v + 1, pl.ds(row, 32)]
                 ring[w, pl.ds(row, 32), to : to + 128] = (ur * xr - ui * xi).astype(jnp.bfloat16)
                 ring[w, pl.ds(row, 32), to + 128 : to + 256] = (ur * xi + ui * xr).astype(
                     jnp.bfloat16
@@ -175,10 +176,13 @@
     return [functools.partial(task, *chunk) for chunk in chunks(pieces, 32)]
 
 
-def steps_kernel(waves, rows, col_count, begin, count, resumed, handed, order, owner, *refs):
+def steps_kernel(
+    waves, first_wave, rows, col_count, begin, count, kept_outputs, resumed, handed, order, owner, *refs
+):
     up2, up, own, down, down2, ex, ey, mats = refs[:8]
     refs = refs[8:]
-    given, refs = (refs[:7], refs[9:]) if resumed else (None, refs)
+    given, refs = (refs[:7], refs[7:]) if resumed else (None, refs)
+    refs = refs[kept_outputs:]
     exit_wave, focused = refs[:2]
     given_on, refs = (refs[2:9], refs[9:]) if handed else (None, refs[2:])
     ring1, ring2, ring3, waved, last2, last3, turned = carried = refs[:7]
@@ -244,7 +248,7 @@
                 focused[w, part, :, 128 * blk : 128 * blk + 128] = block
 
     first_lane = pl.multiple_of(g * STEP, STEP)
-    start = start_tasks(first, ex, ey, first_lane, ring1)
+    start = start_tasks(first, ex, ey, first_lane, first_wave, ring1)
     run(start, columns_tasks(ring1, band, spread_store(spread1)))
     run(rows_tasks(product2, band2, spread1))
     run(transmit_tasks(second, product2, ring2, last2, masks2, True))
@@ -273,22 +277,19 @@
         loads.append(load)
     for load in loads:
         load.wait()
-    copies = []
+    high, low = pl.ds(rows - halo, halo), pl.ds(0, halo)
+    pairs = [(held.at[0, high], outs[0]), (held.at[0, low], outs[1])]
     for i, (left, right) in enumerate(zip(edges[:-1], edges[1:])):
         lanes = pl.ds(left, right - left)
-        up, down, up2, down2 = outs[4 * i : 4 * i + 4]
-        high, low = pl.ds(rows - halo, halo), pl.ds(0, halo)
-        after = pl.ds(2 * rows, halo)
-        pairs = []
-        for target, part in ((up, high), (down, low)):
+        for target, part in ((outs[2 + 2 * i], high), (outs[3 + 2 * i], low)):
             for step in range(2):
                 pairs.append((held.at[step, :, lanes], target.at[pl.ds(rows * step, rows)]))
-            pairs.append((held.at[2, part, lanes], target.at[after]))
-        pairs += [(held.at[0, high, lanes], up2), (held.at[0, low, lanes], down2)]
-        for source, target in pairs:
-            copy = pltpu.make_async_copy(source, target, sems.at[len(copies)])
-            copy.start()
-            copies.append(copy)
+            pairs.append((held.at[2, part, lanes], target.at[pl.ds(2 * rows, halo)]))
+    copies = []
+    for source, target in pairs:
+        copy = pltpu.make_async_copy(source, target, sems.at[len(copies)])
+        copy.start()
+        copies.append(copy)
     for copy in copies:
         copy.wait()
 
@@ -374,30 +375,43 @@
         ey[2 * w + 1 : 2 * w + 2] = sine * keep_cols
 
 
-def detector_kernel(waves, tile_wave, taps_band, row_taps, col_taps, out, padded):
-    sources, rows, width = tile_wave.shape[0], tile_wave.shape[3], tile_wave.shape[4]
-    total = sources * rows
+def add_intensity(tile_wave, taps_band, store):
+    total = tile_wave.shape[0] * tile_wave.shape[3]
+    for b in range(total // 128):
+        parts = []
+        for part in range(2):
+            window = []
+            for k in range(2 * b - 1, 2 * b + 3):
+                if 0 <= k < total // 64:
+                    window.append(tile_wave[k, 0, part])
+                else:
+                    window.append(jnp.zeros((64, tile_wave.shape[4]), jnp.bfloat16))
+            parts.append(jnp.concatenate(window, axis=0))
+        real, imag = dot(taps_band[...], parts[0]), dot(taps_band[...], parts[1])
+        re = real[:128] - imag[128:]
+        im = imag[:128] + real[128:]
+        store(b, re * re + im * im)
+
+
+def intensity_kernel(tile_wave, before, taps_band, out):
+    def store(b, value):
+        at = pl.ds(128 * b, 128)
+        out[at] = value if before is None else before[at] + value
+
+    add_intensity(tile_wave, taps_band, store)
+
+
+def detector_kernel(waves, tile_wave, before, taps_band, row_taps, col_taps, out, padded):
+    total, width = before.shape
     edge = jnp.zeros((64, width), jnp.float32)
     padded[:64] = edge
     padded[64 + total :] = edge
-    for b in range(total // 128):
-        image = None
-        for w in range(waves):
-            parts = []
-            for part in range(2):
-                window = []
-                for k in range(2 * b - 1, 2 * b + 3):
-                    if 0 <= k < total // 64:
-                        window.append(tile_wave[k, w, part])
-                    else:
-                        window.append(jnp.zeros((64, width), jnp.bfloat16))
-                parts.append(jnp.concatenate(window, axis=0))
-            real, imag = dot(taps_band[...], parts[0]), dot(taps_band[...], parts[1])
-            re = real[:128] - imag[128:]
-            im = imag[:128] + real[128:]
-            term = re * re + im * im
-            image = term if image is None else image + term
-        padded[64 + 128 * b : 192 + 128 * b] = image / waves
+
+    def store(b, value):
+        at = pl.ds(128 * b, 128)
+        padded[64 + 128 * b : 192 + 128 * b] = (before[at] + value) / waves
+
+    add_intensity(tile_wave, taps_band, store)
     for b in range(total // 128):
         rows_done = jnp.dot(
             row_taps[...],
@@ -460,26 +474,28 @@
     in_smem = pl.BlockSpec(memory_space=pltpu.SMEM)
     widths = [steps // 2, steps - steps // 2]
     edges = [STEP * sum(widths[:i]) for i in range(len(widths) + 1)]
-    sent_rows = (2 * row_count + HALO, 2 * row_count + HALO, HALO, HALO)
+    sent_rows = 2 * row_count + HALO
     picked = pl.pallas_call(
         functools.partial(pick_kernel, HALO, edges),
         name="pick_rows",
-        out_shape=[
-            jax.ShapeDtypeStruct((rows, STEP * width), potential.dtype)
+        out_shape=[jax.ShapeDtypeStruct((HALO, col_count), potential.dtype)] * 2
+        + [
+            jax.ShapeDtypeStruct((sent_rows, STEP * width), potential.dtype)
             for width in widths
-            for rows in sent_rows
+            for _ in range(2)
         ],
         in_specs=[in_smem, anywhere],
-        out_specs=[anywhere] * (4 * len(widths)),
+        out_specs=[anywhere] * (2 + 2 * len(widths)),
         scratch_shapes=[
             pltpu.VMEM((3, row_count, col_count), potential.dtype),
             pltpu.SemaphoreType.DMA((3,)),
-            pltpu.SemaphoreType.DMA((8 * len(widths),)),
+            pltpu.SemaphoreType.DMA((2 + 6 * len(widths),)),
         ],
         cost_estimate=pl.CostEstimate(flops=0, bytes_accessed=4 << 20, transcendentals=0),
     )(slice_order, potential)
+    up2, down2 = neighbour(picked[0], 2), neighbour(picked[1], -2)
     halos = [
-        [neighbour(value, offset) for value, offset in zip(picked[4 * i : 4 * i + 4], (1, -1, 2, -2))]
+        (neighbour(picked[2 + 2 * i], 1), neighbour(picked[3 + 2 * i], -1))
         for i in range(len(widths))
     ]
 
@@ -513,115 +529,145 @@
 
     placed = tile_cols == STEP
     if placed:
-        focused_shape = (lane_count, waves, 2, row_count, tile_cols)
+        focused_shape = (lane_count, 1, 2, row_count, tile_cols)
     else:
-        focused_shape = (waves, 2, row_count, col_count)
-    carried = [((waves, rows, 256), jnp.bfloat16) for rows in (rows1, rows2, rows3, row_count)]
+        focused_shape = (1, 2, row_count, col_count)
+    carried = [((1, rows, 256), jnp.bfloat16) for rows in (rows1, rows2, rows3, row_count)]
     carried += [
         ((rows2, 128), jnp.float32),
         ((rows3, 128), jnp.float32),
-        ((waves, 2, row_count, 128), jnp.float32),
+        ((1, 2, row_count, 128), jnp.float32),
     ]
 
     def ring(rows, lanes, dtype=jnp.bfloat16):
-        return pltpu.VMEM((waves, rows, lanes), dtype)
+        return pltpu.VMEM((1, rows, lanes), dtype)
 
     outputs = [
         made((waves, 2, row_count, col_count), jnp.float32),
         made(focused_shape, jnp.bfloat16),
     ]
-    given = None
-    for i, width in enumerate(widths):
-        begin, last_call = edges[i] // STEP, i + 1 == len(widths)
-        count = width + 1 if last_call else width
-
-        def piece(rows, width=width):
-            return pl.BlockSpec((rows, STEP), lambda g, *_: (0, jnp.minimum(g, width - 1)))
-
-        def done(g, begin=begin):
-            return clamp(g + begin - 1)
-
-        if placed:
-            focused_spec = pl.BlockSpec(
-                (1, waves, 2, row_count, tile_cols),
-                lambda g, order, owner, done=done: (owner[done(g)], 0, 0, 0, 0),
-            )
-        else:
-            focused_spec = pl.BlockSpec(
-                (waves, 2, row_count, STEP), lambda g, *_, done=done: (0, 0, 0, done(g))
-            )
-        up, down, up2, down2 = halos[i]
-        args = [slice_order, owner, up2, up, potential, down, down2, ex, ey, mats]
-        in_specs = [
-            piece(HALO),
-            piece(2 * row_count + HALO),
-            pl.BlockSpec(
-                (potential.shape[0], row_count, STEP),
-                lambda g, *_, begin=begin: (0, 0, clamp(g + begin)),
+    exit_wave, focused = None, [None] * waves
+    for first_wave in range(waves):
+        given = []
+        for i, width in enumerate(widths):
+            begin, last_call = edges[i] // STEP, i + 1 == len(widths)
+            count = width + 1 if last_call else width
+
+            def piece(width=width):
+                return pl.BlockSpec((sent_rows, STEP), lambda g, *_: (0, jnp.minimum(g, width - 1)))
+
+            def far(begin=begin):
+                return pl.BlockSpec((HALO, STEP), lambda g, *_: (0, clamp(g + begin)))
+
+            def done(g, begin=begin):
+                return clamp(g + begin - 1)
+
+            up, down = halos[i]
+            args = [slice_order, owner, up2, up, potential, down, down2, ex, ey, mats]
+            in_specs = [
+                far(),
+                piece(),
+                pl.BlockSpec(
+                    (potential.shape[0], row_count, STEP),
+                    lambda g, *_, begin=begin: (0, 0, clamp(g + begin)),
+                ),
+                piece(),
+                far(),
+                fixed(*ex.shape),
+                fixed(*ey.shape),
+                fixed(*mats.shape),
+            ]
+            args += given
+            in_specs += [fixed(*shape) for shape, _ in carried[: len(given)]]
+            aliases = {}
+            for at, kept in enumerate((exit_wave, focused[first_wave])):
+                if kept is not None:
+                    aliases[len(args)] = at
+                    args.append(kept)
+                    in_specs.append(anywhere)
+            if placed:
+                focused_spec = pl.BlockSpec(
+                    (1, 1, 2, row_count, tile_cols),
+                    lambda g, order, owner, done=done: (owner[done(g)], 0, 0, 0, 0),
+                )
+            else:
+                focused_spec = pl.BlockSpec(
+                    (1, 2, row_count, STEP), lambda g, *_, done=done: (0, 0, 0, done(g))
+                )
+            out_shape = list(outputs)
+            out_specs = [
+                pl.BlockSpec(
+                    (1, 2, row_count, STEP),
+                    lambda g, *_, done=done, first_wave=first_wave: (first_wave, 0, 0, done(g)),
+                ),
+                focused_spec,
+            ]
+            if not last_call:
+                out_shape += [made(shape, dtype) for shape, dtype in carried]
+                out_specs += [fixed(*shape) for shape, _ in carried]
+            exit_wave, focused[first_wave], *given = pl.pallas_call(
+                functools.partial(
+                    steps_kernel, 1, first_wave, row_count, col_count, begin, count,
+                    len(aliases), i > 0, not last_call,
+                ),
+                name="steps",
+                out_shape=out_shape,
+                grid_spec=pltpu.PrefetchScalarGridSpec(
+                    num_scalar_prefetch=2,
+                    grid=(count,),
+                    in_specs=in_specs,
+                    out_specs=out_specs,
+                    scratch_shapes=[ring(rows, 768) for rows in (rows1, rows2, rows3, row_count)]
+                    + [pltpu.VMEM(shape, dtype) for shape, dtype in carried[4:]]
+                    + [ring(2 * rows, 256) for rows in (rows1, rows2, rows3)]
+                    + [ring(2 * rows, 256, jnp.float32) for rows in (rows2, rows3)],
+                ),
+                input_output_aliases=aliases,
+                compiler_params=pltpu.CompilerParams(
+                    dimension_semantics=("arbitrary",), vmem_limit_bytes=20 * 1024 * 1024
+                ),
+                cost_estimate=pl.CostEstimate(
+                    flops=count * (1 << 29), bytes_accessed=count << 19, transcendentals=0
+                ),
+            )(*args)
+
+    if not placed:
+        joined = jnp.concatenate(focused, axis=0)
+        detector = narrow_tiles(joined, owner, wide_rows, row_taps, col_taps, lane_count)
+        return exit_wave, detector[None]
+
+    tile_waves = [
+        lax.all_to_all(value, "lat", split_axis=0, concat_axis=0, tiled=True) for value in focused
+    ]
+    image = jnp.zeros((total_rows, tile_cols), jnp.float32) if waves == 1 else None
+    for tile_wave in tile_waves[:-1]:
+        before = [] if image is None else [image]
+
+        def kernel(*refs, alone=image is None):
+            tile_ref, band_ref, out_ref = refs[0], refs[-2], refs[-1]
+            intensity_kernel(tile_ref, None if alone else refs[1], band_ref, out_ref)
+
+        image = pl.pallas_call(
+            kernel,
+            name="intensity",
+            out_shape=made((total_rows, tile_cols), jnp.float32),
+            in_specs=[in_vmem] * (2 + len(before)),
+            out_specs=in_vmem,
+            compiler_params=pltpu.CompilerParams(vmem_limit_bytes=20 * 1024 * 1024),
+            cost_estimate=pl.CostEstimate(
+                flops=1 << 31, bytes_accessed=2 << 20, transcendentals=0
             ),
-            piece(2 * row_count + HALO),
-            piece(HALO),
-            fixed(*ex.shape),
-            fixed(*ey.shape),
-            fixed(*mats.shape),
-        ]
-        aliases = {}
-        if given is not None:
-            args += given
-            in_specs += [fixed(*shape) for shape, _ in carried] + [anywhere, anywhere]
-            aliases = {len(args) - 2: 0, len(args) - 1: 1}
-        out_shape = list(outputs)
-        out_specs = [
-            pl.BlockSpec((waves, 2, row_count, STEP), lambda g, *_, done=done: (0, 0, 0, done(g))),
-            focused_spec,
-        ]
-        if not last_call:
-            out_shape += [made(shape, dtype) for shape, dtype in carried]
-            out_specs += [fixed(*shape) for shape, _ in carried]
-        results = pl.pallas_call(
-            functools.partial(
-                steps_kernel, waves, row_count, col_count, begin, count, given is not None, not last_call
-            ),
-            name="steps",
-            out_shape=out_shape,
-            grid_spec=pltpu.PrefetchScalarGridSpec(
-                num_scalar_prefetch=2,
-                grid=(count,),
-                in_specs=in_specs,
-                out_specs=out_specs,
-                scratch_shapes=[ring(rows, 768) for rows in (rows1, rows2, rows3, row_count)]
-                + [pltpu.VMEM(shape, dtype) for shape, dtype in carried[4:]]
-                + [ring(2 * rows, 256) for rows in (rows1, rows2, rows3)]
-                + [ring(2 * rows, 256, jnp.float32) for rows in (rows2, rows3)],
-            ),
-            input_output_aliases=aliases,
-            compiler_params=pltpu.CompilerParams(
-                dimension_semantics=("arbitrary",), vmem_limit_bytes=24 * 1024 * 1024
-            ),
-            cost_estimate=pl.CostEstimate(
-                flops=count * (1 << 30), bytes_accessed=count << 19, transcendentals=0
-            ),
-        )(*args)
-        given = list(results[2:]) + list(results[:2])
-    exit_wave, focused = results[:2]
-
-    if not placed:
-        detector = narrow_tiles(focused, owner, wide_rows, row_taps, col_taps, lane_count)
-        return exit_wave, detector[None]
-
-    tile_wave = lax.all_to_all(focused, "lat", split_axis=0, concat_axis=0, tiled=True)
+        )(tile_wave, *before, wide_rows)
     detector = pl.pallas_call(
         functools.partial(detector_kernel, waves),
         name="detector",
-        out_shape=jax.ShapeDtypeStruct((tile_cols, total_rows), jnp.float32),
-        in_specs=[pl.BlockSpec(memory_space=pltpu.VMEM)] * 4,
-        out_specs=pl.BlockSpec(memory_space=pltpu.VMEM),
+        out_shape=made((tile_cols, total_rows), jnp.float32),
+        in_specs=[in_vmem] * 5,
+        out_specs=in_vmem,
         scratch_shapes=[pltpu.VMEM((total_rows + 128, tile_cols), jnp.float32)],
-        compiler_params=pltpu.CompilerParams(vmem_limit_bytes=48 * 1024 * 1024),
-        cost_estimate=pl.CostEstimate(
-            flops=1 << 33, bytes_accessed=4 << 20, transcendentals=0
-        ),
-    )(tile_wave, wide_rows, row_taps, col_taps)
+        compiler_params=pltpu.CompilerParams(vmem_limit_bytes=20 * 1024 * 1024),
+        cost_estimate=pl.CostEstimate(flops=1 << 33, bytes_accessed=4 << 20, transcendentals=0),
+    )(tile_waves[-1], image, wide_rows, row_taps, col_taps)
     return exit_wave, detector[None]
 
 

time: 149 us -> 178 us (1.19)
  blocking collectives: 54.9 us -> 0 us
  Pallas kernels: 58 us -> 98 us
  waiting for transfers between devices: 9.26 us -> 35.4 us
  starting transfers between devices: 20.8 us -> 31.9 us
  local copies, waits for them, and re-layouts: 3.98 us -> 11.1 us
    all_to_all x1 -> x0, blocking collectives: 54.9 us -> none  [local(): lax.all_to_all(focused, 'lat', split_axis=0, concat_axis=0, tiled=True)]
    pallas_call x2 -> x5, Pallas kernels: 45.3 us -> 84.6 us  [the longest x4 82.6 us: local(): pl.pallas_call(functools.partial(steps_kernel, 1, first_wave, row_count,...]
    all_to_all x0 -> x2, waiting for transfers between devices: none -> 22 us  [local(): lax.all_to_all(value, 'lat', split_axis=0, concat_axis=0, tiled=True)]
    all_to_all x0 -> x2, starting transfers between devices: none -> 12.8 us  [local(): lax.all_to_all(value, 'lat', split_axis=0, concat_axis=0, tiled=True)]
    unnamed x21 -> x35, local copies, waits for them, and re-layouts: 3.98 us -> 11.1 us
    ppermute x8 -> x6, waiting for transfers between devices: 9.26 us -> 13.4 us  [neighbour(): return lax.ppermute(value, 'lat', pairs)]
    ppermute x8 -> x6, starting transfers between devices: 20.8 us -> 19.1 us  [neighbour(): return lax.ppermute(value, 'lat', pairs)]
  transfers between devices with their start and end apart: 8 -> 8, of which waited for: 1 -> 2; matrix products, arithmetic and copies ran while one was open for 0% -> 1% of each run, Pallas kernels for 17% -> 37%
where the time goes in v4:
time: 178 us; the launch traced here: 177 us
  Pallas kernels  98 us (55%)
  waiting for transfers between devices  35.4 us (20%)
  starting transfers between devices  31.9 us (18%)
  local copies, waits for them, and re-layouts  11.1 us (6%)
    pallas_call x4, Pallas kernels, local(): pl.pallas_call(functools.partial(steps_kernel, 1, first_wave, row_count,...  82.6 us
    all_to_all x2, waiting for transfers between devices, local(): lax.all_to_all(value, 'lat', split_axis=0, concat_axis=0, tiled=True)  22 us
    ppermute x6, starting transfers between devices, neighbour(): return lax.ppermute(value, 'lat', pairs)  19.1 us
    ppermute x6, waiting for transfers between devices, neighbour(): return lax.ppermute(value, 'lat', pairs)  13.4 us
    all_to_all x2, starting transfers between devices, local(): lax.all_to_all(value, 'lat', split_axis=0, concat_axis=0, tiled=True)  12.8 us
    unnamed x35, local copies, waits for them, and re-layouts  11.1 us
    pallas_call x1, Pallas kernels, local(): pl.pallas_call(functools.partial(detector_kernel, waves), name='detector'...  6.04 us
    pallas_call x1, Pallas kernels, local(): pl.pallas_call(functools.partial(pick_kernel, HALO, edges), name='pick_ro...  3.84 us
  transfers between devices with their start and end apart: 8, of which 2 were waited for; matrix products, arithmetic and copies ran while one was open for 1% of the time, Pallas kernels for 37%

profile of v4, /device:TPU:13, one launch (start us, length us, event | category | flops | bytes accessed | tf_op | source)
XLA Modules:
  0.0 177.2 jit_solution(7273280693744966424)
XLA Ops:
  0.6 3.8 %pick_rows.1 = (bf16[32,4096]{1,0:T(8,128)(2,1)}, bf16[32,4096]{1,0:T(8,128)(2,1)}, bf16[160,2048]{1,0:T(8,128)(2,1)}, bf16[160,2048]{1,0:T(8,128)(2,1)}, bf16[1...) custom-call(s32[3]{0:T(128)} %order.9, bf16[6,64,4096]{2,1,0:T(8,128)(2,1)} %refs_2_.7), custom_call_target="tpu_custom_call" | custom-call | bytes 4194304 | tf_op jit(solution)/shard_map/pick_rows/pallas_call | solution.py:478
  4.5 0.0 copy-start
  4.5 0.0 copy-start.3
  4.5 0.0 copy-start.4
  4.5 4.0 %collective-permute-start.4 = (bf16[160,2048]{1,0:T(8,128)(2,1)}, bf16[160,2048]{1,0:T(8,128)(2,1)}, u32[]{:S(2)}, u32[]{:S(2)}) collective-permute-start(bf16[160,2048]{1,0:T(8,128)(2,1)} %get-tuple-element.43), channel_id=1, source_target_pairs={{0,1},{1,2},{2,3},{3,4},{4,5},{5,6},{6,7},{7,8},{8,9},{9,10},{10,1... | collective-permute-start | bytes 1966088 | tf_op jit(solution)/shard_map/ppermute | solution.py:469
  8.5 1.9 %collective-permute-start.5 = (bf16[160,2048]{1,0:T(8,128)(2,1)}, bf16[160,2048]{1,0:T(8,128)(2,1)}, u32[]{:S(2)}, u32[]{:S(2)}) collective-permute-start(bf16[160,2048]{1,0:T(8,128)(2,1)} %get-tuple-element.44), channel_id=1, source_target_pairs={{1,0},{2,1},{3,2},{4,3},{5,4},{6,5},{7,6},{8,7},{9,8},{10,9},{11,1... | collective-permute-start | bytes 1966088 | tf_op jit(solution)/shard_map/ppermute | solution.py:469
  10.4 3.1 %collective-permute-start = (bf16[32,4096]{1,0:T(8,128)(2,1)}, bf16[32,4096]{1,0:T(8,128)(2,1)S(1)}, u32[]{:S(2)}, u32[]{:S(2)}) collective-permute-start(bf16[32,4096]{1,0:T(8,128)(2,1)} %get-tuple-element.36), channel_id=1, source_target_pairs={{0,2},{1,3},{2,4},{3,5},{4,6},{5,7},{6,8},{7,9},{8,10},{9,11},{10,... | collective-permute-start | bytes 786440 | tf_op jit(solution)/shard_map/ppermute | solution.py:469
  13.6 2.1 %collective-permute-start.3 = (bf16[32,4096]{1,0:T(8,128)(2,1)}, bf16[32,4096]{1,0:T(8,128)(2,1)}, u32[]{:S(2)}, u32[]{:S(2)}) collective-permute-start(bf16[32,4096]{1,0:T(8,128)(2,1)} %get-tuple-element.39), channel_id=1, source_target_pairs={{2,0},{3,1},{4,2},{5,3},{6,4},{7,5},{8,6},{9,7},{10,8},{11,9},{12,... | collective-permute-start | bytes 786440 | tf_op jit(solution)/shard_map/ppermute | solution.py:469
  15.7 6.0 %collective-permute-start.1 = (bf16[160,2048]{1,0:T(8,128)(2,1)}, bf16[160,2048]{1,0:T(8,128)(2,1)}, u32[]{:S(2)}, u32[]{:S(2)}) collective-permute-start(bf16[160,2048]{1,0:T(8,128)(2,1)} %get-tuple-element.37), channel_id=1, source_target_pairs={{0,1},{1,2},{2,3},{3,4},{4,5},{5,6},{6,7},{7,8},{8,9},{9,10},{10,1... | collective-permute-start | bytes 1966088 | tf_op jit(solution)/shard_map/ppermute | solution.py:469
  21.7 13.4 %collective-permute-done.refs_0_ = bf16[32,4096]{1,0:T(8,128)(2,1)S(1)} collective-permute-done((bf16[32,4096]{1,0:T(8,128)(2,1)}, bf16[32,4096]{1,0:T(8,128)(2,1)S(1)}, u32[]{:S(2)}, u32[]{:S(2)}) %collective-permute-start) | collective-permute-done | bytes 262176 | tf_op jit(solution)/shard_map/ppermute | solution.py:469
  35.1 1.9 %collective-permute-start.2 = (bf16[160,2048]{1,0:T(8,128)(2,1)}, bf16[160,2048]{1,0:T(8,128)(2,1)}, u32[]{:S(2)}, u32[]{:S(2)}) collective-permute-start(bf16[160,2048]{1,0:T(8,128)(2,1)} %get-tuple-element.38), channel_id=1, source_target_pairs={{1,0},{2,1},{3,2},{4,3},{5,4},{6,5},{7,6},{8,7},{9,8},{10,9},{11,1... | collective-permute-start | bytes 1966088 | tf_op jit(solution)/shard_map/ppermute | solution.py:469
  37.1 1.4 copy.15.tilt_table
  38.4 3.5 %prepare.1 = (bf16[1280,512]{1,0:T(8,128)(2,1)}, bf16[256,256]{1,0:T(8,128)(2,1)}, f32[128,256]{1,0:T(8,128)}, f32[256,256]{1,0:T(8,128)}, f32[4,256,128]{2,1,0:T(8,128)}, /*index=5*/f32[4,4352]{1,0:T(4,128)}) custom-call(s32[2]{0:T(128)} %tilt_index.1, s32[1]{0:T(128)} %bitcast.first_row, f32[41,2]{1,0:T(8,128)} %copy.15.tilt_table, f32[2,63]{1,0:T(2,128)} %fresnel.1, ...), custom_call_target="tpu_custom_call" | custom-call | flops 2147483648 | bytes 2097152 | tf_op jit(solution)/shard_map/prepare/pallas_call | solution.py:507
  42.0 0.0 collective-permute-done.3.refs_4_
  42.0 1.3 copy-done.5
  43.3 1.0 copy-done.9
  44.4 0.9 copy-done.13
  45.3 19.6 %steps.4 = (f32[2,2,64,4096]{3,2,1,0:T(8,128)}, bf16[16,1,2,64,256]{4,3,2,1,0:T(8,128)(2,1)S(1)}, bf16[1,256,256]{2,1,0:T(8,128)(2,1)S(1)}, bf16[1,192,256]{2,1,...) custom-call(s32[3]{0:T(128)S(1)} %copy-done.3, ...), custom_call_target="tpu_custom_call" | custom-call | flops 4294967296 | bytes 4194304 | tf_op jit(solution)/shard_map/steps/pallas_call | solution.py:608
  64.9 21.7 %steps.5 = (f32[2,2,64,4096]{3,2,1,0:T(8,128)}, bf16[16,1,2,64,256]{4,3,2,1,0:T(8,128)(2,1)S(1)}) custom-call(s32[3]{0:T(128)S(1)} %copy-done.3, s32[16]{0:T(128)S(1)} %copy-done.4, bf16[32,4096]{1,0:T(8,128)(2,1)S(1)} %collective-permute-done.refs_0_, ...), custom_call_target="tpu_custom_call", output_to_operand_aliasing={{0}: (17, {}), {1}: (18, {})} | custom-call | flops 4831838208 | bytes 4718592 | tf_op jit(solution)/shard_map/steps/pallas_call | solution.py:608
  86.6 1.0 copy-done.2
  87.5 6.8 %all-to-all-start.1 = ((bf16[16,1,2,64,256]{4,3,2,1,0:T(8,128)(2,1)}), bf16[16,1,2,64,256]{4,3,2,1,0:T(8,128)(2,1)}, u32[]{:S(2)}, u32[]{:S(2)}) async-start(bf16[16,1,2,64,256]{4,3,2,1,0:T(8,128)(2,1)} %copy-done.2), calls=%async_computation.1 | async-start | bytes 2097152 | tf_op jit(solution)/shard_map/all_to_all | solution.py:640
  94.4 1.3 copy-done.6
  95.7 1.0 copy-done.10
  96.7 19.6 %steps.6 = (f32[2,2,64,4096]{3,2,1,0:T(8,128)}, bf16[16,1,2,64,256]{4,3,2,1,0:T(8,128)(2,1)S(1)}, bf16[1,256,256]{2,1,0:T(8,128)(2,1)S(1)}, bf16[1,192,256]{2,1,...) custom-call(s32[3]{0:T(128)S(1)} %copy-done.3, ...), custom_call_target="tpu_custom_call", output_to_operand_aliasing={{0}: (10, {})} | custom-call | flops 4294967296 | bytes 4194304 | tf_op jit(solution)/shard_map/steps/pallas_call | solution.py:608
  116.3 21.7 %steps.7 = (f32[2,2,64,4096]{3,2,1,0:T(8,128)}, bf16[16,1,2,64,256]{4,3,2,1,0:T(8,128)(2,1)S(1)}) custom-call(s32[3]{0:T(128)S(1)} %copy-done.3, s32[16]{0:T(128)S(1)} %copy-done.4, bf16[32,4096]{1,0:T(8,128)(2,1)S(1)} %collective-permute-done.refs_0_, ...), custom_call_target="tpu_custom_call", output_to_operand_aliasing={{0}: (17, {}), {1}: (18, {})} | custom-call | flops 4831838208 | bytes 4718592 | tf_op jit(solution)/shard_map/steps/pallas_call | solution.py:608
  138.0 1.0 copy-done.1
  139.0 6.0 %all-to-all-start = ((bf16[16,1,2,64,256]{4,3,2,1,0:T(8,128)(2,1)}), bf16[16,1,2,64,256]{4,3,2,1,0:T(8,128)(2,1)}, u32[]{:S(2)}, u32[]{:S(2)}) async-start(bf16[16,1,2,64,256]{4,3,2,1,0:T(8,128)(2,1)} %copy-done.1), calls=%async_computation | async-start | bytes 2097152 | tf_op jit(solution)/shard_map/all_to_all | solution.py:640
  145.0 2.0 %intensity.1.before = f32[1024,256]{1,0:T(8,128)S(1)} custom-call(bf16[16,1,2,64,256]{4,3,2,1,0:T(8,128)(2,1)} %all-to-all-done.1.refs_0_, bf16[256,256]{1,0:T(8,128)(2,1)S(1)} %copy-done.12), custom_call_target="tpu_custom_call" | custom-call | flops 2147483648 | bytes 2097152 | tf_op jit(solution)/shard_map/intensity/pallas_call | solution.py:650
  147.0 1.0 copy-done.7
  148.0 22.0 %all-to-all-done.tile_wave = bf16[16,1,2,64,256]{4,3,2,1,0:T(8,128)(2,1)} async-done(((bf16[16,1,2,64,256]{4,3,2,1,0:T(8,128)(2,1)}), bf16[16,1,2,64,256]{4,3,2,1,0:T(8,128)(2,1)}, u32[]{:S(2)}, u32[]{:S(2)}) %all-to-all-start) | async-done | bytes 1048608 | tf_op jit(solution)/shard_map/all_to_all | solution.py:640
  170.0 1.2 copy-done.8
  171.2 6.0 %detector.1 = f32[256,1024]{1,0:T(8,128)} custom-call(bf16[16,1,2,64,256]{4,3,2,1,0:T(8,128)(2,1)} %all-to-all-done.tile_wave, f32[1024,256]{1,0:T(8,128)S(1)} %copy-done.8, bf16[256,256]{1,0:T(8,128)(2,1)S(1)} %copy-done.12, f32[128,256]{1,0:T(8,128)S(1)} %copy-done.16, f32[256,256]{1,0:T(8,128)S(1)} %copy-done.11), custom_call_target="tpu_custom_call" | custom-call | flops 8589934592 | bytes 4194304 | tf_op jit(solution)/shard_map/detector/pallas_call | solution.py:661
  (27 shorter events, 0.1 us)
Async XLA Ops:
  4.5 37.5 %copy-start = (bf16[6,64,4096]{2,1,0:T(8,128)(2,1)S(1)}, bf16[6,64,4096]{2,1,0:T(8,128)(2,1)}, u32[]{:S(2)}) copy-start(bf16[6,64,4096]{2,1,0:T(8,128)(2,1)} %refs_2_.7) | copy-start | bytes 9437188
  4.5 37.5 %copy-start.3 = (s32[3]{0:T(128)S(1)}, s32[3]{0:T(128)}, u32[]{:S(2)}) copy-start(s32[3]{0:T(128)} %order.9) | copy-start | bytes 40
  4.5 37.5 %copy-start.4 = (s32[16]{0:T(128)S(1)}, s32[16]{0:T(128)}, u32[]{:S(2)}) copy-start(s32[16]{0:T(128)} %owner.7) | copy-start | bytes 196
  4.5 37.5 %collective-permute-start.4 = (bf16[160,2048]{1,0:T(8,128)(2,1)}, bf16[160,2048]{1,0:T(8,128)(2,1)}, u32[]{:S(2)}, u32[]{:S(2)}) collective-permute-start(bf16[160,2048]{1,0:T(8,128)(2,1)} %get-tuple-element.43), channel_id=1, source_target_pairs={{0,1},{1,2},{2,3},{3,4},{4,5},{5,6},{6,7},{7,8},{8,9},{9,10},{10,1... | collective-permute-start | bytes 1966088 | tf_op jit(solution)/shard_map/ppermute | solution.py:469
  8.5 33.5 %collective-permute-start.5 = (bf16[160,2048]{1,0:T(8,128)(2,1)}, bf16[160,2048]{1,0:T(8,128)(2,1)}, u32[]{:S(2)}, u32[]{:S(2)}) collective-permute-start(bf16[160,2048]{1,0:T(8,128)(2,1)} %get-tuple-element.44), channel_id=1, source_target_pairs={{1,0},{2,1},{3,2},{4,3},{5,4},{6,5},{7,6},{8,7},{9,8},{10,9},{11,1... | collective-permute-start | bytes 1966088 | tf_op jit(solution)/shard_map/ppermute | solution.py:469
  10.4 24.7 %collective-permute-start = (bf16[32,4096]{1,0:T(8,128)(2,1)}, bf16[32,4096]{1,0:T(8,128)(2,1)S(1)}, u32[]{:S(2)}, u32[]{:S(2)}) collective-permute-start(bf16[32,4096]{1,0:T(8,128)(2,1)} %get-tuple-element.36), channel_id=1, source_target_pairs={{0,2},{1,3},{2,4},{3,5},{4,6},{5,7},{6,8},{7,9},{8,10},{9,11},{10,... | collective-permute-start | bytes 786440 | tf_op jit(solution)/shard_map/ppermute | solution.py:469
  13.6 28.4 %collective-permute-start.3 = (bf16[32,4096]{1,0:T(8,128)(2,1)}, bf16[32,4096]{1,0:T(8,128)(2,1)}, u32[]{:S(2)}, u32[]{:S(2)}) collective-permute-start(bf16[32,4096]{1,0:T(8,128)(2,1)} %get-tuple-element.39), channel_id=1, source_target_pairs={{2,0},{3,1},{4,2},{5,3},{6,4},{7,5},{8,6},{9,7},{10,8},{11,9},{12,... | collective-permute-start | bytes 786440 | tf_op jit(solution)/shard_map/ppermute | solution.py:469
  15.7 49.2 %collective-permute-start.1 = (bf16[160,2048]{1,0:T(8,128)(2,1)}, bf16[160,2048]{1,0:T(8,128)(2,1)}, u32[]{:S(2)}, u32[]{:S(2)}) collective-permute-start(bf16[160,2048]{1,0:T(8,128)(2,1)} %get-tuple-element.37), channel_id=1, source_target_pairs={{0,1},{1,2},{2,3},{3,4},{4,5},{5,6},{6,7},{7,8},{8,9},{9,10},{10,1... | collective-permute-start | bytes 1966088 | tf_op jit(solution)/shard_map/ppermute | solution.py:469
  35.1 29.7 %collective-permute-start.2 = (bf16[160,2048]{1,0:T(8,128)(2,1)}, bf16[160,2048]{1,0:T(8,128)(2,1)}, u32[]{:S(2)}, u32[]{:S(2)}) collective-permute-start(bf16[160,2048]{1,0:T(8,128)(2,1)} %get-tuple-element.38), channel_id=1, source_target_pairs={{1,0},{2,1},{3,2},{4,3},{5,4},{6,5},{7,6},{8,7},{9,8},{10,9},{11,1... | collective-permute-start | bytes 1966088 | tf_op jit(solution)/shard_map/ppermute | solution.py:469
  42.0 1.3 copy-start.5
  43.3 1.0 copy-start.9
  44.4 0.9 copy-start.13
  64.9 29.5 %copy-start.14 = (f32[4,4352]{1,0:T(4,128)S(1)}, f32[4,4352]{1,0:T(4,128)}, u32[]{:S(2)}) copy-start(f32[4,4352]{1,0:T(4,128)} %get-tuple-element.41.refs_6_) | copy-start | bytes 208900
  86.6 1.0 copy-start.2
  87.5 51.4 %all-to-all-start.1 = ((bf16[16,1,2,64,256]{4,3,2,1,0:T(8,128)(2,1)}), bf16[16,1,2,64,256]{4,3,2,1,0:T(8,128)(2,1)}, u32[]{:S(2)}, u32[]{:S(2)}) async-start(bf16[16,1,2,64,256]{4,3,2,1,0:T(8,128)(2,1)} %copy-done.2), calls=%async_computation.1 | async-start | bytes 2097152 | tf_op jit(solution)/shard_map/all_to_all | solution.py:640
  94.3 1.3 copy-start.6
  95.7 1.0 copy-start.10
  96.7 19.6 %copy-start.15 = (f32[4,4352]{1,0:T(4,128)S(1)}, f32[4,4352]{1,0:T(4,128)}, u32[]{:S(2)}) copy-start(f32[4,4352]{1,0:T(4,128)} %get-tuple-element.41.refs_6_) | copy-start | bytes 208900
  116.3 28.7 %copy-start.12 = (bf16[256,256]{1,0:T(8,128)(2,1)S(1)}, bf16[256,256]{1,0:T(8,128)(2,1)}, u32[]{:S(2)}) copy-start(bf16[256,256]{1,0:T(8,128)(2,1)} %get-tuple-element.67.refs_1_.taps_band) | copy-start | bytes 393220
  138.0 1.0 copy-start.1
  139.0 31.0 %all-to-all-start = ((bf16[16,1,2,64,256]{4,3,2,1,0:T(8,128)(2,1)}), bf16[16,1,2,64,256]{4,3,2,1,0:T(8,128)(2,1)}, u32[]{:S(2)}, u32[]{:S(2)}) async-start(bf16[16,1,2,64,256]{4,3,2,1,0:T(8,128)(2,1)} %copy-done.1), calls=%async_computation | async-start | bytes 2097152 | tf_op jit(solution)/shard_map/all_to_all | solution.py:640
  145.0 25.0 %copy-start.11 = (f32[256,256]{1,0:T(8,128)S(1)}, f32[256,256]{1,0:T(8,128)}, u32[]{:S(2)}) copy-start(f32[256,256]{1,0:T(8,128)} %get-tuple-element.69.col_taps) | copy-start | bytes 786436
  145.0 25.0 %copy-start.16 = (f32[128,256]{1,0:T(8,128)S(1)}, f32[128,256]{1,0:T(8,128)}, u32[]{:S(2)}) copy-start(f32[128,256]{1,0:T(8,128)} %get-tuple-element.68.row_taps) | copy-start | bytes 393220
  147.0 1.0 copy-start.7
  170.0 1.2 copy-start.8

commit v5 on v3

--- a/solution.py
+++ b/solution.py
@@ -42,7 +42,8 @@
     5.977824346636851e-10,
 )
 HALO = 32
-STEP = 256
+STEP = 512
+TILE = 256
 
 
 def horner(coefs, z):
@@ -92,14 +93,14 @@
 
 
 def columns_tasks(ring, band, store):
-    waves = ring.shape[0]
+    waves, blocks = ring.shape[0], ring.shape[2] // 256 - 1
 
     def task(w, blk):
         store(w, blk, dot(ring[w, :, 256 * blk : 256 * blk + 512], band[...]))
-        if blk == 1:
-            ring[w, :, :256] = ring[w, :, 512:768]
-
-    return [functools.partial(task, w, blk) for w in range(waves) for blk in range(2)]
+        if blk == blocks - 1:
+            ring[w, :, :256] = ring[w, :, 256 * blocks :]
+
+    return [functools.partial(task, w, blk) for w in range(waves) for blk in range(blocks)]
 
 
 def spread_store(spread):
@@ -127,10 +128,10 @@
 
 
 def start_tasks(pieces, ex, ey, first_lane, ring):
-    waves = ring.shape[0]
+    waves, blocks = ring.shape[0], ring.shape[2] // 256 - 1
 
     def task(ref, lead, start, row):
-        for blk in range(2):
+        for blk in range(blocks):
             lanes = pl.ds(128 * blk, 128)
             cosine, sine = cos_sin(rows_of(ref, lead, start, 32, lanes))
             to = 256 * (blk + 1)
@@ -152,17 +153,16 @@
 
     def task(ref, lead, start, row):
         here = pl.ds(row, 32)
-        found = [rows_of(ref, lead, start, 32, pl.ds(128 * blk, 128)) for blk in range(2)]
-        if turn:
-            low = lax.broadcasted_iota(jnp.int32, (32, 128), 1) < 64
-            found = [pltpu.roll(value, 64, 1) for value in found]
-            phases = [jnp.where(low, last[here], found[0]), jnp.where(low, found[0], found[1])]
-        else:
-            phases = [last[here], found[0]]
-        last[here] = found[1]
-        for blk in range(2):
-            cosine, sine = cos_sin(phases[blk])
-            cosine, sine = cosine * masks[blk], sine * masks[blk]
+        before = last[here]
+        low = lax.broadcasted_iota(jnp.int32, (32, 128), 1) < 64
+        for blk, mask in enumerate(masks):
+            found = rows_of(ref, lead, start, 32, pl.ds(128 * blk, 128))
+            if turn:
+                found = pltpu.roll(found, 64, 1)
+            phase = jnp.where(low, before, found) if turn else before
+            before = found
+            cosine, sine = cos_sin(phase)
+            cosine, sine = cosine * mask, sine * mask
             to = 256 * (blk + 1)
             for w in range(waves):
                 real = product[w, here, 128 * blk : 128 * blk + 128]
@@ -171,22 +171,27 @@
                 ring[w, here, to + 128 : to + 256] = (real * sine + imag * cosine).astype(
                     jnp.bfloat16
                 )
+        last[here] = before
 
     return [functools.partial(task, *chunk) for chunk in chunks(pieces, 32)]
 
 
 def steps_kernel(waves, rows, col_count, begin, count, resumed, handed, order, owner, *refs):
-    up2, up, own, down, down2, ex, ey, mats = refs[:8]
-    refs = refs[8:]
+    up2, up, own1, own2, own3, down, down2, ex, ey, mats = refs[:10]
+    refs = refs[10:]
     given, refs = (refs[:7], refs[9:]) if resumed else (None, refs)
     exit_wave, focused = refs[:2]
     given_on, refs = (refs[2:9], refs[9:]) if handed else (None, refs[2:])
     ring1, ring2, ring3, waved, last2, last3, turned = carried = refs[:7]
-    spread1, spread2, spread3, product2, product3 = refs[7:]
-    g = pl.program_id(0) + begin
+    spread1, spread2, spread3, product2, product3, exit_held, focused_held, sems = refs[7:]
+    local_step = pl.program_id(0)
+    g = local_step + begin
     rings = carried[:4]
-
-    @pl.when(g == begin)
+    blocks = STEP // 128
+    tiles = STEP // TILE
+    slot = local_step % 2
+
+    @pl.when(local_step == 0)
     def _():
         for i, ref in enumerate(carried):
             if given is None:
@@ -199,6 +204,35 @@
             else:
                 ref[...] = given[i][...]
 
+    def for_copies(step, slot, act):
+        for k in range(tiles):
+            tile = tiles * (step + begin) - 1 + k
+
+            @pl.when((tile >= 0) & (tile < col_count // TILE))
+            def _(tile=tile, k=k):
+                lanes = pl.ds(TILE * k, TILE)
+                there = pl.ds(pl.multiple_of(tile * TILE, TILE), TILE)
+                act(
+                    pltpu.make_async_copy(
+                        exit_held.at[slot, :, :, :, lanes],
+                        exit_wave.at[:, :, :, there],
+                        sems.at[0, slot, k],
+                    )
+                )
+                if len(focused.shape) == 5:
+                    target = focused.at[owner[tile]]
+                else:
+                    target = focused.at[:, :, :, there]
+                act(
+                    pltpu.make_async_copy(
+                        focused_held.at[slot, :, :, :, lanes], target, sems.at[1, slot, k]
+                    )
+                )
+
+    @pl.when(local_step >= 2)
+    def _():
+        for_copies(local_step - 2, slot, lambda copy: copy.wait())
+
     sizes = [ring.shape[1] for ring in rings]
     band2 = mats.at[pl.ds(0, 2 * sizes[1]), pl.ds(0, 2 * sizes[0])]
     at = 2 * sizes[1]
@@ -209,43 +243,40 @@
     band = mats.at[pl.ds(at, 512), pl.ds(0, 256)]
     wide_band = mats.at[pl.ds(at, 512), pl.ds(256, 256)]
     first = (
-        (up2, None, 0, HALO), (up, None, 0, rows), (own, order[0], 0, rows),
+        (up2, None, 0, HALO), (up, None, 0, rows), (own1, 0, 0, rows),
         (down, None, 0, rows), (down2, None, 0, HALO),
     )
-    second = ((up, None, rows, rows), (own, order[1], 0, rows), (down, None, rows, rows))
-    third = (
-        (up, None, 2 * rows, HALO), (own, order[2], 0, rows), (down, None, 2 * rows, HALO)
-    )
-    masks2 = [lanes_inside(2 * g + blk, 64, col_count) for blk in range(2)]
-    masks3 = [lanes_inside(2 * g - 1 + blk, 0, col_count) for blk in range(2)]
-    masks4 = [lanes_inside(2 * g - 1 + blk, 64, col_count) for blk in range(2)]
+    second = ((up, None, rows, rows), (own2, 0, 0, rows), (down, None, rows, rows))
+    third = ((up, None, 2 * rows, HALO), (own3, 0, 0, rows), (down, None, 2 * rows, HALO))
+    masks2 = [lanes_inside(blocks * g + blk, 64, col_count) for blk in range(blocks)]
+    masks3 = [lanes_inside(blocks * g - 1 + blk, 0, col_count) for blk in range(blocks)]
+    masks4 = [lanes_inside(blocks * g - 1 + blk, 64, col_count) for blk in range(blocks)]
     kept = waved.shape[1]
     low = lax.broadcasted_iota(jnp.int32, (kept, 128), 1) < 64
 
     def exit_task(w):
         product = dot(band4[...], spread3[w])
-        for blk in range(2):
-            for part in range(2):
+        for part in range(2):
+            before = turned[w, part]
+            for blk in range(blocks):
                 value = product[kept * part : kept * part + kept, 128 * blk : 128 * blk + 128]
                 lane = 256 * (blk + 1) + 128 * part
                 waved[w, :, lane : lane + 128] = (value * masks4[blk]).astype(jnp.bfloat16)
                 rolled = pltpu.roll(value, 64, 1)
-                exit_wave[w, part, :, 128 * blk : 128 * blk + 128] = jnp.where(
-                    low, turned[w, part], rolled
+                exit_held[slot, w, part, :, 128 * blk : 128 * blk + 128] = jnp.where(
+                    low, before, rolled
                 )
-                turned[w, part] = rolled
+                before = rolled
+            turned[w, part] = before
 
     def focused_store(w, blk, value):
         for part in range(2):
             block = value[:, 128 * part : 128 * part + 128].astype(jnp.bfloat16)
-            if len(focused.shape) == 5:
-                focused[0, w, part, :, 128 * blk : 128 * blk + 128] = block
-            else:
-                focused[w, part, :, 128 * blk : 128 * blk + 128] = block
+            focused_held[slot, w, part, :, 128 * blk : 128 * blk + 128] = block
 
     first_lane = pl.multiple_of(g * STEP, STEP)
-    start = start_tasks(first, ex, ey, first_lane, ring1)
-    run(start, columns_tasks(ring1, band, spread_store(spread1)))
+    run(start_tasks(first, ex, ey, first_lane, ring1))
+    run(columns_tasks(ring1, band, spread_store(spread1)))
     run(rows_tasks(product2, band2, spread1))
     run(transmit_tasks(second, product2, ring2, last2, masks2, True))
     run(columns_tasks(ring2, band, spread_store(spread2)))
@@ -254,11 +285,14 @@
     run(columns_tasks(ring3, band, spread_store(spread3)))
     run([functools.partial(exit_task, w) for w in range(waves)])
     run(columns_tasks(waved, wide_band, focused_store))
-
-    if handed:
-
-        @pl.when(g == begin + count - 1)
-        def _():
+    for_copies(local_step, slot, lambda copy: copy.start())
+
+    @pl.when(local_step == count - 1)
+    def _():
+        if count > 1:
+            for_copies(local_step - 1, 1 - slot, lambda copy: copy.wait())
+        for_copies(local_step, slot, lambda copy: copy.wait())
+        if handed:
             for i, ref in enumerate(carried):
                 given_on[i][...] = ref[:, :, :256] if i < 4 else ref[...]
 
@@ -511,7 +545,7 @@
     def fixed(*shape):
         return pl.BlockSpec(shape, lambda g, *_: (0,) * len(shape))
 
-    placed = tile_cols == STEP
+    placed = tile_cols == TILE
     if placed:
         focused_shape = (lane_count, waves, 2, row_count, tile_cols)
     else:
@@ -538,27 +572,19 @@
         def piece(rows, width=width):
             return pl.BlockSpec((rows, STEP), lambda g, *_: (0, jnp.minimum(g, width - 1)))
 
-        def done(g, begin=begin):
-            return clamp(g + begin - 1)
-
-        if placed:
-            focused_spec = pl.BlockSpec(
-                (1, waves, 2, row_count, tile_cols),
-                lambda g, order, owner, done=done: (owner[done(g)], 0, 0, 0, 0),
+        def mine(step, begin=begin):
+            return pl.BlockSpec(
+                (1, row_count, STEP), lambda g, order, *_: (order[step], 0, clamp(g + begin))
             )
-        else:
-            focused_spec = pl.BlockSpec(
-                (waves, 2, row_count, STEP), lambda g, *_, done=done: (0, 0, 0, done(g))
-            )
+
         up, down, up2, down2 = halos[i]
-        args = [slice_order, owner, up2, up, potential, down, down2, ex, ey, mats]
+        args = [slice_order, owner, up2, up, potential, potential, potential, down, down2, ex, ey, mats]
         in_specs = [
             piece(HALO),
             piece(2 * row_count + HALO),
-            pl.BlockSpec(
-                (potential.shape[0], row_count, STEP),
-                lambda g, *_, begin=begin: (0, 0, clamp(g + begin)),
-            ),
+            mine(0),
+            mine(1),
+            mine(2),
             piece(2 * row_count + HALO),
             piece(HALO),
             fixed(*ex.shape),
@@ -571,10 +597,7 @@
             in_specs += [fixed(*shape) for shape, _ in carried] + [anywhere, anywhere]
             aliases = {len(args) - 2: 0, len(args) - 1: 1}
         out_shape = list(outputs)
-        out_specs = [
-            pl.BlockSpec((waves, 2, row_count, STEP), lambda g, *_, done=done: (0, 0, 0, done(g))),
-            focused_spec,
-        ]
+        out_specs = [anywhere, anywhere]
         if not last_call:
             out_shape += [made(shape, dtype) for shape, dtype in carried]
             out_specs += [fixed(*shape) for shape, _ in carried]
@@ -589,17 +612,24 @@
                 grid=(count,),
                 in_specs=in_specs,
                 out_specs=out_specs,
-                scratch_shapes=[ring(rows, 768) for rows in (rows1, rows2, rows3, row_count)]
+                scratch_shapes=[
+                    ring(rows, 256 + 2 * STEP) for rows in (rows1, rows2, rows3, row_count)
+                ]
                 + [pltpu.VMEM(shape, dtype) for shape, dtype in carried[4:]]
-                + [ring(2 * rows, 256) for rows in (rows1, rows2, rows3)]
-                + [ring(2 * rows, 256, jnp.float32) for rows in (rows2, rows3)],
+                + [ring(2 * rows, STEP) for rows in (rows1, rows2, rows3)]
+                + [ring(2 * rows, STEP, jnp.float32) for rows in (rows2, rows3)]
+                + [
+                    pltpu.VMEM((2, waves, 2, row_count, STEP), jnp.float32),
+                    pltpu.VMEM((2, waves, 2, row_count, STEP), jnp.bfloat16),
+                    pltpu.SemaphoreType.DMA((2, 2, STEP // TILE)),
+                ],
             ),
             input_output_aliases=aliases,
             compiler_params=pltpu.CompilerParams(
-                dimension_semantics=("arbitrary",), vmem_limit_bytes=24 * 1024 * 1024
+                dimension_semantics=("arbitrary",), vmem_limit_bytes=32 * 1024 * 1024
             ),
             cost_estimate=pl.CostEstimate(
-                flops=count * (1 << 30), bytes_accessed=count << 19, transcendentals=0
+                flops=count * (1 << 31), bytes_accessed=count << 20, transcendentals=0
             ),
         )(*args)
         given = list(results[2:]) + list(results[:2])

time: 149 us -> 144 us (0.966)
  Pallas kernels: 58 us -> 52.2 us
    pallas_call x2, Pallas kernels: 45.3 us -> 39.5 us  [local(): pl.pallas_call(functools.partial(steps_kernel, waves, row_count, col_coun...]
  transfers between devices with their start and end apart: 8 -> 8, of which waited for: 1 -> 1; matrix products, arithmetic and copies ran while one was open for 0% -> 1% of each run, Pallas kernels for 17% -> 15%
where the time goes in v5:
time: 144 us; the launch traced here: 142 us
  blocking collectives  54.9 us (38%)
  Pallas kernels  52.2 us (36%)
  starting transfers between devices  20.8 us (14%)
  waiting for transfers between devices  9.26 us (6%)
  local copies, waits for them, and re-layouts  3.98 us (3%)
    all_to_all x1, blocking collectives, local(): lax.all_to_all(focused, 'lat', split_axis=0, concat_axis=0, tiled=True)  54.9 us
    pallas_call x2, Pallas kernels, local(): pl.pallas_call(functools.partial(steps_kernel, waves, row_count, col_coun...  39.5 us
    ppermute x8, starting transfers between devices, neighbour(): return lax.ppermute(value, 'lat', pairs)  20.8 us
    ppermute x8, waiting for transfers between devices, neighbour(): return lax.ppermute(value, 'lat', pairs)  9.26 us
    pallas_call x1, Pallas kernels, local(): pl.pallas_call(functools.partial(detector_kernel, waves), name='detector'...  5.28 us
    unnamed x21, local copies, waits for them, and re-layouts  3.98 us
    pallas_call x1, Pallas kernels, local(): pl.pallas_call(functools.partial(pick_kernel, HALO, edges), name='pick_ro...  3.96 us
    pallas_call x1, Pallas kernels, local(): pl.pallas_call(functools.partial(prepare_kernel, waves, row_count, total_...  3.47 us
  transfers between devices with their start and end apart: 8, of which 1 were waited for; matrix products, arithmetic and copies ran while one was open for 1% of the time, Pallas kernels for 15%

profile of v5, /device:TPU:13, one launch (start us, length us, event | category | flops | bytes accessed | tf_op | source)
XLA Modules:
  0.0 141.9 jit_solution(8936865748996747791)
XLA Ops:
  0.6 0.0 copy-start.9
  0.6 4.0 %pick_rows.1 = (bf16[160,2048]{1,0:T(8,128)(2,1)}, bf16[160,2048]{1,0:T(8,128)(2,1)}, bf16[32,2048]{1,0:T(8,128)(2,1)}, bf16[32,2048]{1,0:T(8,128)(2,1)}, bf16[1...) custom-call(s32[3]{0:T(128)} %order.5, ...), custom_call_target="tpu_custom_call" | custom-call | bytes 4194304 | tf_op jit(solution)/shard_map/pick_rows/pallas_call | solution.py:498
  4.6 3.7 %collective-permute-start.5 = (bf16[160,2048]{1,0:T(8,128)(2,1)}, bf16[160,2048]{1,0:T(8,128)(2,1)}, u32[]{:S(2)}, u32[]{:S(2)}) collective-permute-start(bf16[160,2048]{1,0:T(8,128)(2,1)} %get-tuple-element.35), channel_id=1, source_target_pairs={{0,1},{1,2},{2,3},{3,4},{4,5},{5,6},{6,7},{7,8},{8,9},{9,10},{10,1... | collective-permute-start | bytes 1966088 | tf_op jit(solution)/shard_map/ppermute | solution.py:489
  8.3 1.9 %collective-permute-start.6 = (bf16[160,2048]{1,0:T(8,128)(2,1)}, bf16[160,2048]{1,0:T(8,128)(2,1)}, u32[]{:S(2)}, u32[]{:S(2)}) collective-permute-start(bf16[160,2048]{1,0:T(8,128)(2,1)} %get-tuple-element.36), channel_id=1, source_target_pairs={{1,0},{2,1},{3,2},{4,3},{5,4},{6,5},{7,6},{8,7},{9,8},{10,9},{11,1... | collective-permute-start | bytes 1966088 | tf_op jit(solution)/shard_map/ppermute | solution.py:489
  10.3 3.1 %collective-permute-start = (bf16[32,2048]{1,0:T(8,128)(2,1)}, bf16[32,2048]{1,0:T(8,128)(2,1)S(1)}, u32[]{:S(2)}, u32[]{:S(2)}) collective-permute-start(bf16[32,2048]{1,0:T(8,128)(2,1)} %get-tuple-element.27), channel_id=1, source_target_pairs={{0,2},{1,3},{2,4},{3,5},{4,6},{5,7},{6,8},{7,9},{8,10},{9,11},{10,... | collective-permute-start | bytes 393224 | tf_op jit(solution)/shard_map/ppermute | solution.py:489
  13.4 3.1 %collective-permute-start.4 = (bf16[32,2048]{1,0:T(8,128)(2,1)}, bf16[32,2048]{1,0:T(8,128)(2,1)S(1)}, u32[]{:S(2)}, u32[]{:S(2)}) collective-permute-start(bf16[32,2048]{1,0:T(8,128)(2,1)} %get-tuple-element.34), channel_id=1, source_target_pairs={{0,2},{1,3},{2,4},{3,5},{4,6},{5,7},{6,8},{7,9},{8,10},{9,11},{10,... | collective-permute-start | bytes 393224 | tf_op jit(solution)/shard_map/ppermute | solution.py:489
  16.6 2.1 %collective-permute-start.7 = (bf16[32,2048]{1,0:T(8,128)(2,1)}, bf16[32,2048]{1,0:T(8,128)(2,1)S(1)}, u32[]{:S(2)}, u32[]{:S(2)}) collective-permute-start(bf16[32,2048]{1,0:T(8,128)(2,1)} %get-tuple-element.37), channel_id=1, source_target_pairs={{2,0},{3,1},{4,2},{5,3},{6,4},{7,5},{8,6},{9,7},{10,8},{11,9},{12,... | collective-permute-start | bytes 393224 | tf_op jit(solution)/shard_map/ppermute | solution.py:489
  18.7 0.0 copy-done.9
  18.7 0.7 copy.12.tilt_table
  19.4 3.5 %prepare.1 = (bf16[1280,512]{1,0:T(8,128)(2,1)}, bf16[256,256]{1,0:T(8,128)(2,1)}, f32[128,256]{1,0:T(8,128)}, f32[256,256]{1,0:T(8,128)}, f32[4,256,128]{2,1,0:T(8,128)}, /*index=5*/f32[4,4608]{1,0:T(4,128)}) custom-call(s32[2]{0:T(128)} %tilt_index.1, s32[1]{0:T(128)} %bitcast.first_row, f32[41,2]{1,0:T(8,128)} %copy.12.tilt_table, f32[2,63]{1,0:T(2,128)} %fresnel.1, ...), custom_call_target="tpu_custom_call" | custom-call | flops 2147483648 | bytes 2097152 | tf_op jit(solution)/shard_map/prepare/pallas_call | solution.py:525
  22.9 9.2 %collective-permute-done.4.refs_0_ = bf16[32,2048]{1,0:T(8,128)(2,1)S(1)} collective-permute-done((bf16[32,2048]{1,0:T(8,128)(2,1)}, bf16[32,2048]{1,0:T(8,128)(2,1)S(1)}, u32[]{:S(2)}, u32[]{:S(2)}) %collective-permute-start.4) | collective-permute-done | bytes 131104 | tf_op jit(solution)/shard_map/ppermute | solution.py:489
  32.2 1.9 %collective-permute-start.3 = (bf16[32,2048]{1,0:T(8,128)(2,1)}, bf16[32,2048]{1,0:T(8,128)(2,1)S(1)}, u32[]{:S(2)}, u32[]{:S(2)}) collective-permute-start(bf16[32,2048]{1,0:T(8,128)(2,1)} %get-tuple-element.30), channel_id=1, source_target_pairs={{2,0},{3,1},{4,2},{5,3},{6,4},{7,5},{8,6},{9,7},{10,8},{11,9},{12,... | collective-permute-start | bytes 393224 | tf_op jit(solution)/shard_map/ppermute | solution.py:489
  34.1 0.0 collective-permute-done.7.refs_6_
  34.1 2.9 %collective-permute-start.1 = (bf16[160,2048]{1,0:T(8,128)(2,1)}, bf16[160,2048]{1,0:T(8,128)(2,1)S(1)}, u32[]{:S(2)}, u32[]{:S(2)}) collective-permute-start(bf16[160,2048]{1,0:T(8,128)(2,1)} %get-tuple-element.28), channel_id=1, source_target_pairs={{0,1},{1,2},{2,3},{3,4},{4,5},{5,6},{6,7},{7,8},{8,9},{9,10},{10,1... | collective-permute-start | bytes 1966088 | tf_op jit(solution)/shard_map/ppermute | solution.py:489
  37.0 0.0 collective-permute-done.5.refs_1_
  37.0 1.9 %collective-permute-start.2 = (bf16[160,2048]{1,0:T(8,128)(2,1)}, bf16[160,2048]{1,0:T(8,128)(2,1)S(1)}, u32[]{:S(2)}, u32[]{:S(2)}) collective-permute-start(bf16[160,2048]{1,0:T(8,128)(2,1)} %get-tuple-element.29), channel_id=1, source_target_pairs={{1,0},{2,1},{3,2},{4,3},{5,4},{6,5},{7,6},{8,7},{9,8},{10,9},{11,1... | collective-permute-start | bytes 1966088 | tf_op jit(solution)/shard_map/ppermute | solution.py:489
  38.9 0.0 collective-permute-done.6.refs_5_
  38.9 0.0 copy-done
  39.0 0.0 copy-start.3
  39.0 1.3 copy-done.3
  40.3 1.0 copy-done.4
  41.3 0.9 copy-done.8
  42.2 18.3 %steps.2 = (f32[2,2,64,4096]{3,2,1,0:T(8,128)}, bf16[16,2,2,64,256]{4,3,2,1,0:T(8,128)(2,1)S(1)}, bf16[2,256,256]{2,1,0:T(8,128)(2,1)S(1)}, bf16[2,192,256]{2,1,...) custom-call(s32[3]{0:T(128)S(1)} %copy-done.1, ...), custom_call_target="tpu_custom_call" | custom-call | flops 8589934592 | bytes 4194304 | tf_op jit(solution)/shard_map/steps/pallas_call | solution.py:604
  60.5 0.0 collective-permute-done.refs_0_
  60.5 0.0 collective-permute-done.3.refs_6_
  60.5 0.0 collective-permute-done.1.refs_1_
  60.5 0.0 collective-permute-done.2.refs_5_
  60.5 21.2 %steps.3 = (f32[2,2,64,4096]{3,2,1,0:T(8,128)}, bf16[16,2,2,64,256]{4,3,2,1,0:T(8,128)(2,1)S(1)}) custom-call(s32[3]{0:T(128)S(1)} %copy-done.1, s32[16]{0:T(128)S(1)} %copy-done.2, bf16[32,2048]{1,0:T(8,128)(2,1)S(1)} %collective-permute-done.refs_0_, ...), custom_call_target="tpu_custom_call", output_to_operand_aliasing={{0}: (19, {}), {1}: (20, {})} | custom-call | flops 10737418240 | bytes 5242880 | tf_op jit(solution)/shard_map/steps/pallas_call | solution.py:604
  81.8 54.9 %all_to_all.5.tile_wave = bf16[16,2,2,64,256]{4,3,2,1,0:T(8,128)(2,1)S(1)} all-to-all(bf16[16,2,2,64,256]{4,3,2,1,0:T(8,128)(2,1)S(1)} %get-tuple-element.48), channel_id=1, replica_groups=mesh['lamella'=2,'lat'=16] {'lat'}, dimensions={0} | all-to-all | bytes 4194304 | tf_op jit(solution)/shard_map/all_to_all | solution.py:642
  136.6 0.0 copy-done.5
  136.6 0.0 copy-done.7
  136.7 5.3 %detector.1 = f32[256,1024]{1,0:T(8,128)} custom-call(bf16[16,2,2,64,256]{4,3,2,1,0:T(8,128)(2,1)S(1)} %all_to_all.5.tile_wave, bf16[256,256]{1,0:T(8,128)(2,1)S(1)} %copy-done.6, f32[128,256]{1,0:T(8,128)S(1)} %copy-done.7, f32[256,256]{1,0:T(8,128)S(1)} %copy-done.5), custom_call_target="tpu_custom_call" | custom-call | flops 8589934592 | bytes 4194304 | tf_op jit(solution)/shard_map/detector/pallas_call | solution.py:643
  (11 shorter events, 0.0 us)
Async XLA Ops:
  0.6 18.1 %copy-start.9 = (f32[41,2]{0,1:T(2,128)S(1)}, f32[41,2]{0,1:T(2,128)}, u32[]{:S(2)}) copy-start(f32[41,2]{0,1:T(2,128)} %param.11) | copy-start | bytes 988
  4.6 32.4 %collective-permute-start.5 = (bf16[160,2048]{1,0:T(8,128)(2,1)}, bf16[160,2048]{1,0:T(8,128)(2,1)}, u32[]{:S(2)}, u32[]{:S(2)}) collective-permute-start(bf16[160,2048]{1,0:T(8,128)(2,1)} %get-tuple-element.35), channel_id=1, source_target_pairs={{0,1},{1,2},{2,3},{3,4},{4,5},{5,6},{6,7},{7,8},{8,9},{9,10},{10,1... | collective-permute-start | bytes 1966088 | tf_op jit(solution)/shard_map/ppermute | solution.py:489
  8.3 30.6 %collective-permute-start.6 = (bf16[160,2048]{1,0:T(8,128)(2,1)}, bf16[160,2048]{1,0:T(8,128)(2,1)}, u32[]{:S(2)}, u32[]{:S(2)}) collective-permute-start(bf16[160,2048]{1,0:T(8,128)(2,1)} %get-tuple-element.36), channel_id=1, source_target_pairs={{1,0},{2,1},{3,2},{4,3},{5,4},{6,5},{7,6},{8,7},{9,8},{10,9},{11,1... | collective-permute-start | bytes 1966088 | tf_op jit(solution)/shard_map/ppermute | solution.py:489
  10.3 50.2 %collective-permute-start = (bf16[32,2048]{1,0:T(8,128)(2,1)}, bf16[32,2048]{1,0:T(8,128)(2,1)S(1)}, u32[]{:S(2)}, u32[]{:S(2)}) collective-permute-start(bf16[32,2048]{1,0:T(8,128)(2,1)} %get-tuple-element.27), channel_id=1, source_target_pairs={{0,2},{1,3},{2,4},{3,5},{4,6},{5,7},{6,8},{7,9},{8,10},{9,11},{10,... | collective-permute-start | bytes 393224 | tf_op jit(solution)/shard_map/ppermute | solution.py:489
  13.4 18.7 %collective-permute-start.4 = (bf16[32,2048]{1,0:T(8,128)(2,1)}, bf16[32,2048]{1,0:T(8,128)(2,1)S(1)}, u32[]{:S(2)}, u32[]{:S(2)}) collective-permute-start(bf16[32,2048]{1,0:T(8,128)(2,1)} %get-tuple-element.34), channel_id=1, source_target_pairs={{0,2},{1,3},{2,4},{3,5},{4,6},{5,7},{6,8},{7,9},{8,10},{9,11},{10,... | collective-permute-start | bytes 393224 | tf_op jit(solution)/shard_map/ppermute | solution.py:489
  16.6 17.5 %collective-permute-start.7 = (bf16[32,2048]{1,0:T(8,128)(2,1)}, bf16[32,2048]{1,0:T(8,128)(2,1)S(1)}, u32[]{:S(2)}, u32[]{:S(2)}) collective-permute-start(bf16[32,2048]{1,0:T(8,128)(2,1)} %get-tuple-element.37), channel_id=1, source_target_pairs={{2,0},{3,1},{4,2},{5,3},{6,4},{7,5},{8,6},{9,7},{10,8},{11,9},{12,... | collective-permute-start | bytes 393224 | tf_op jit(solution)/shard_map/ppermute | solution.py:489
  19.4 19.5 %copy-start = (bf16[6,64,4096]{2,1,0:T(8,128)(2,1)S(1)}, bf16[6,64,4096]{2,1,0:T(8,128)(2,1)}, u32[]{:S(2)}) copy-start(bf16[6,64,4096]{2,1,0:T(8,128)(2,1)} %refs_4_.3) | copy-start | bytes 9437188
  19.4 19.5 %copy-start.1 = (s32[3]{0:T(128)S(1)}, s32[3]{0:T(128)}, u32[]{:S(2)}) copy-start(s32[3]{0:T(128)} %order.5) | copy-start | bytes 40
  19.4 19.5 %copy-start.2 = (s32[16]{0:T(128)S(1)}, s32[16]{0:T(128)}, u32[]{:S(2)}) copy-start(s32[16]{0:T(128)} %owner.3) | copy-start | bytes 196
  32.2 28.4 %collective-permute-start.3 = (bf16[32,2048]{1,0:T(8,128)(2,1)}, bf16[32,2048]{1,0:T(8,128)(2,1)S(1)}, u32[]{:S(2)}, u32[]{:S(2)}) collective-permute-start(bf16[32,2048]{1,0:T(8,128)(2,1)} %get-tuple-element.30), channel_id=1, source_target_pairs={{2,0},{3,1},{4,2},{5,3},{6,4},{7,5},{8,6},{9,7},{10,8},{11,9},{12,... | collective-permute-start | bytes 393224 | tf_op jit(solution)/shard_map/ppermute | solution.py:489
  34.1 26.4 %collective-permute-start.1 = (bf16[160,2048]{1,0:T(8,128)(2,1)}, bf16[160,2048]{1,0:T(8,128)(2,1)S(1)}, u32[]{:S(2)}, u32[]{:S(2)}) collective-permute-start(bf16[160,2048]{1,0:T(8,128)(2,1)} %get-tuple-element.28), channel_id=1, source_target_pairs={{0,1},{1,2},{2,3},{3,4},{4,5},{5,6},{6,7},{7,8},{8,9},{9,10},{10,1... | collective-permute-start | bytes 1966088 | tf_op jit(solution)/shard_map/ppermute | solution.py:489
  37.0 23.5 %collective-permute-start.2 = (bf16[160,2048]{1,0:T(8,128)(2,1)}, bf16[160,2048]{1,0:T(8,128)(2,1)S(1)}, u32[]{:S(2)}, u32[]{:S(2)}) collective-permute-start(bf16[160,2048]{1,0:T(8,128)(2,1)} %get-tuple-element.29), channel_id=1, source_target_pairs={{1,0},{2,1},{3,2},{4,3},{5,4},{6,5},{7,6},{8,7},{9,8},{10,9},{11,1... | collective-permute-start | bytes 1966088 | tf_op jit(solution)/shard_map/ppermute | solution.py:489
  39.0 1.3 copy-start.3
  40.3 1.0 copy-start.4
  41.3 0.9 copy-start.8
  81.7 54.9 %copy-start.5 = (f32[256,256]{1,0:T(8,128)S(1)}, f32[256,256]{1,0:T(8,128)}, u32[]{:S(2)}) copy-start(f32[256,256]{1,0:T(8,128)} %get-tuple-element.51.col_taps) | copy-start | bytes 786436
  81.7 54.9 %copy-start.6 = (bf16[256,256]{1,0:T(8,128)(2,1)S(1)}, bf16[256,256]{1,0:T(8,128)(2,1)}, u32[]{:S(2)}) copy-start(bf16[256,256]{1,0:T(8,128)(2,1)} %get-tuple-element.49.taps_band) | copy-start | bytes 393220
  81.8 54.9 %copy-start.7 = (f32[128,256]{1,0:T(8,128)S(1)}, f32[128,256]{1,0:T(8,128)}, u32[]{:S(2)}) copy-start(f32[128,256]{1,0:T(8,128)} %get-tuple-element.50.row_taps) | copy-start | bytes 393220

commit v6 on v5

--- a/solution.py
+++ b/solution.py
@@ -114,11 +114,22 @@
     return store
 
 
+def rows_product(rows_band, spread, w, block):
+    half = spread.shape[1] // 2
+    window = [spread[w, half * part + 64 * block : half * part + 64 * block + 128] for part in range(2)]
+    return dot(rows_band[...], jnp.concatenate(window, axis=0))
+
+
 def rows_tasks(product, rows_band, spread):
-    def task(w):
-        product[w] = dot(rows_band[...], spread[w])
-
-    return [functools.partial(task, w) for w in range(spread.shape[0])]
+    waves, rows = product.shape[0], product.shape[1] // 2
+
+    def task(w, block):
+        result = rows_product(rows_band, spread, w, block)
+        at = 64 * block
+        product[w, at : at + 64] = result[:64]
+        product[w, rows + at : rows + at + 64] = result[64:]
+
+    return [functools.partial(task, w, block) for w in range(waves) for block in range(rows // 64)]
 
 
 def run(*lists):
@@ -127,7 +138,7 @@
             task()
 
 
-def start_tasks(pieces, ex, ey, first_lane, ring):
+def start_tasks(pieces, table, first_block, ring):
     waves, blocks = ring.shape[0], ring.shape[2] // 256 - 1
 
     def task(ref, lead, start, row):
@@ -135,11 +146,11 @@
             lanes = pl.ds(128 * blk, 128)
             cosine, sine = cos_sin(rows_of(ref, lead, start, 32, lanes))
             to = 256 * (blk + 1)
+            at = pl.ds(ring.shape[1] + first_block + blk, 1)
             for w in range(waves):
-                at = pl.ds(first_lane + 128 * blk, 128)
-                yr, yi = ey[2 * w : 2 * w + 1, at], ey[2 * w + 1 : 2 * w + 2, at]
+                yr, yi = table[2 * w, at], table[2 * w + 1, at]
                 ur, ui = cosine * yr - sine * yi, cosine * yi + sine * yr
-                xr, xi = ex[2 * w, pl.ds(row, 32)], ex[2 * w + 1, pl.ds(row, 32)]
+                xr, xi = table[2 * w, pl.ds(row, 32)], table[2 * w + 1, pl.ds(row, 32)]
                 ring[w, pl.ds(row, 32), to : to + 128] = (ur * xr - ui * xi).astype(jnp.bfloat16)
                 ring[w, pl.ds(row, 32), to + 128 : to + 256] = (ur * xi + ui * xr).astype(
                     jnp.bfloat16
@@ -148,11 +159,13 @@
     return [functools.partial(task, *chunk) for chunk in chunks(pieces, 32)]
 
 
-def transmit_tasks(pieces, product, ring, last, masks, turn):
+def transmit_tasks(pieces, product, ring, last, masks, turn, first_row, total_rows):
     waves, rows = ring.shape[:2]
 
     def task(ref, lead, start, row):
         here = pl.ds(row, 32)
+        at = first_row + row
+        inside = ((at >= 0) & (at < total_rows)).astype(jnp.float32)
         before = last[here]
         low = lax.broadcasted_iota(jnp.int32, (32, 128), 1) < 64
         for blk, mask in enumerate(masks):
@@ -162,7 +175,7 @@
             phase = jnp.where(low, before, found) if turn else before
             before = found
             cosine, sine = cos_sin(phase)
-            cosine, sine = cosine * mask, sine * mask
+            cosine, sine = cosine * (mask * inside), sine * (mask * inside)
             to = 256 * (blk + 1)
             for w in range(waves):
                 real = product[w, here, 128 * blk : 128 * blk + 128]
@@ -176,9 +189,11 @@
     return [functools.partial(task, *chunk) for chunk in chunks(pieces, 32)]
 
 
-def steps_kernel(waves, rows, col_count, begin, count, resumed, handed, order, owner, *refs):
-    up2, up, own1, own2, own3, down, down2, ex, ey, mats = refs[:10]
-    refs = refs[10:]
+def steps_kernel(
+    waves, rows, total_rows, col_count, begin, count, resumed, handed, order, owner, first_row, *refs
+):
+    up2, up, own1, own2, own3, down, down2, table, mats = refs[:9]
+    refs = refs[9:]
     given, refs = (refs[:7], refs[9:]) if resumed else (None, refs)
     exit_wave, focused = refs[:2]
     given_on, refs = (refs[2:9], refs[9:]) if handed else (None, refs[2:])
@@ -186,7 +201,6 @@
     spread1, spread2, spread3, product2, product3, exit_held, focused_held, sems = refs[7:]
     local_step = pl.program_id(0)
     g = local_step + begin
-    rings = carried[:4]
     blocks = STEP // 128
     tiles = STEP // TILE
     slot = local_step % 2
@@ -233,15 +247,9 @@
     def _():
         for_copies(local_step - 2, slot, lambda copy: copy.wait())
 
-    sizes = [ring.shape[1] for ring in rings]
-    band2 = mats.at[pl.ds(0, 2 * sizes[1]), pl.ds(0, 2 * sizes[0])]
-    at = 2 * sizes[1]
-    band3 = mats.at[pl.ds(at, 2 * sizes[2]), pl.ds(0, 2 * sizes[1])]
-    at += 2 * sizes[2]
-    band4 = mats.at[pl.ds(at, 2 * sizes[3]), pl.ds(0, 2 * sizes[2])]
-    at += 2 * sizes[3]
-    band = mats.at[pl.ds(at, 512), pl.ds(0, 256)]
-    wide_band = mats.at[pl.ds(at, 512), pl.ds(256, 256)]
+    rows_band = mats.at[pl.ds(0, 128), pl.ds(0, 256)]
+    band = mats.at[pl.ds(128, 512), pl.ds(0, 256)]
+    wide_band = mats.at[pl.ds(128, 512), pl.ds(256, 256)]
     first = (
         (up2, None, 0, HALO), (up, None, 0, rows), (own1, 0, 0, rows),
         (down, None, 0, rows), (down2, None, 0, HALO),
@@ -255,7 +263,7 @@
     low = lax.broadcasted_iota(jnp.int32, (kept, 128), 1) < 64
 
     def exit_task(w):
-        product = dot(band4[...], spread3[w])
+        product = rows_product(rows_band, spread3, w, 0)
         for part in range(2):
             before = turned[w, part]
             for blk in range(blocks):
@@ -274,14 +282,15 @@
             block = value[:, 128 * part : 128 * part + 128].astype(jnp.bfloat16)
             focused_held[slot, w, part, :, 128 * blk : 128 * blk + 128] = block
 
-    first_lane = pl.multiple_of(g * STEP, STEP)
-    run(start_tasks(first, ex, ey, first_lane, ring1))
+    run(start_tasks(first, table, blocks * g, ring1))
     run(columns_tasks(ring1, band, spread_store(spread1)))
-    run(rows_tasks(product2, band2, spread1))
-    run(transmit_tasks(second, product2, ring2, last2, masks2, True))
+    run(rows_tasks(product2, rows_band, spread1))
+    at = first_row[0] - 2 * HALO
+    run(transmit_tasks(second, product2, ring2, last2, masks2, True, at, total_rows))
     run(columns_tasks(ring2, band, spread_store(spread2)))
-    run(rows_tasks(product3, band3, spread2))
-    run(transmit_tasks(third, product3, ring3, last3, masks3, False))
+    run(rows_tasks(product3, rows_band, spread2))
+    at = first_row[0] - HALO
+    run(transmit_tasks(third, product3, ring3, last3, masks3, False, at, total_rows))
     run(columns_tasks(ring3, band, spread_store(spread3)))
     run([functools.partial(exit_task, w) for w in range(waves)])
     run(columns_tasks(waved, wide_band, focused_store))
@@ -305,20 +314,21 @@
         load = pltpu.make_async_copy(potential.at[order[step]], held.at[step], load_sems.at[step])
         load.start()
         loads.append(load)
-    for load in loads:
+    high, low = pl.ds(rows - halo, halo), pl.ds(0, halo)
+    copies = []
+    for step, load in enumerate(loads):
         load.wait()
-    copies = []
-    for i, (left, right) in enumerate(zip(edges[:-1], edges[1:])):
-        lanes = pl.ds(left, right - left)
-        up, down, up2, down2 = outs[4 * i : 4 * i + 4]
-        high, low = pl.ds(rows - halo, halo), pl.ds(0, halo)
-        after = pl.ds(2 * rows, halo)
         pairs = []
-        for target, part in ((up, high), (down, low)):
-            for step in range(2):
-                pairs.append((held.at[step, :, lanes], target.at[pl.ds(rows * step, rows)]))
-            pairs.append((held.at[2, part, lanes], target.at[after]))
-        pairs += [(held.at[0, high, lanes], up2), (held.at[0, low, lanes], down2)]
+        for i, (left, right) in enumerate(zip(edges[:-1], edges[1:])):
+            lanes = pl.ds(left, right - left)
+            up, down, up2, down2 = outs[4 * i : 4 * i + 4]
+            for target, far, part in ((up, up2, high), (down, down2, low)):
+                if step == 2:
+                    pairs.append((held.at[2, part, lanes], target.at[pl.ds(2 * rows, halo)]))
+                else:
+                    pairs.append((held.at[step, :, lanes], target.at[pl.ds(rows * step, rows)]))
+                if step == 0:
+                    pairs.append((held.at[0, part, lanes], far))
         for source, target in pairs:
             copy = pltpu.make_async_copy(source, target, sems.at[len(copies)])
             copy.start()
@@ -339,15 +349,10 @@
 
 def prepare_kernel(
     waves, rows, total_rows, col_count, tilt_index, first_row, tilt_table, fresnel, ctf, mtf,
-    mats, wide_rows, row_taps, col_taps, ex, ey, line,
+    mats, wide_rows, row_taps, col_taps, table, line,
 ):
-    rows3, rows2, rows1 = (rows + 2 * HALO * k for k in (1, 2, 3))
-    mats[...] = jnp.zeros_like(mats)
-    at = 2 * rows2 + 2 * rows3 + 2 * rows
-    band, wide_band = (mats.at[pl.ds(at, 512), pl.ds(256 * i, 256)] for i in range(2))
-    band2 = mats.at[pl.ds(0, 2 * rows2), pl.ds(0, 2 * rows1)]
-    band3 = mats.at[pl.ds(2 * rows2, 2 * rows3), pl.ds(0, 2 * rows2)]
-    band4 = mats.at[pl.ds(2 * rows2 + 2 * rows3, 2 * rows), pl.ds(0, 2 * rows3)]
+    mats[:128, 256:] = jnp.zeros((128, mats.shape[1] - 256), jnp.bfloat16)
+    band, wide_band = (mats.at[pl.ds(128, 512), pl.ds(256 * i, 256)] for i in range(2))
     line[...] = jnp.zeros_like(line)
     line[0:2, : fresnel.shape[1]] = fresnel[...].astype(jnp.bfloat16).astype(jnp.float32)
     line[2:4, : ctf.shape[1]] = ctf[...].astype(jnp.bfloat16).astype(jnp.float32)
@@ -369,18 +374,15 @@
 
     columns(band, 0, 65 - (fresnel.shape[1] + 1) // 2)
     columns(wide_band, 2, 65 - (ctf.shape[1] + 1) // 2)
-    for target, halo in ((band2, 2 * HALO), (band3, HALO), (band4, 0)):
-        count, count_in = target.shape[0] // 2, target.shape[1] // 2
-        keep = inside_rows(first - halo, count, total_rows)
-        for part in range(2):
-            made = toeplitz(line[part : part + 1], count, HALO - (fresnel.shape[1] - 1) // 2) * keep
-            made = made[:, :count_in].astype(jnp.bfloat16)
-            if part == 0:
-                target[:count, :count_in] = made
-                target[count:, count_in:] = made
-            else:
-                target[:count, count_in:] = -made
-                target[count:, :count_in] = made
+    for part in range(2):
+        made = toeplitz(line[part : part + 1], 64, HALO - (fresnel.shape[1] - 1) // 2)
+        made = made[:, :128].astype(jnp.bfloat16)
+        if part == 0:
+            mats[:64, :128] = made
+            mats[64:128, 128:256] = made
+        else:
+            mats[:64, 128:256] = -made
+            mats[64:128, :128] = made
     for part in range(2):
         made = toeplitz(line[2 + part : 3 + part], 128, 65 - (ctf.shape[1] + 1) // 2)
         wide_rows[128 * part : 128 * part + 128] = made.astype(jnp.bfloat16)
@@ -392,20 +394,36 @@
     )
     made = jnp.where(jnp.abs(off) <= reach, toeplitz(line[4:5], width, -reach), 0.0)
     col_taps[...] = made[:, :width]
-    count = ex.shape[1]
+    count = rows + 6 * HALO
+    wide = table.shape[1] - count
     at = first - 3 * HALO + lax.broadcasted_iota(jnp.int32, (count, 128), 0)
     keep = ((at >= 0) & (at < total_rows)).astype(jnp.float32)
     at = at.astype(jnp.float32) * (1.0 / total_rows)
-    across = lax.broadcasted_iota(jnp.int32, (1, ey.shape[1]), 1)
+    across = 128 * lax.broadcasted_iota(jnp.int32, (wide, 128), 0)
+    across = across + lax.broadcasted_iota(jnp.int32, (wide, 128), 1)
     keep_cols = (across < col_count).astype(jnp.float32)
     across = across.astype(jnp.float32) * (1.0 / col_count)
     for w in range(waves):
         cosine, sine = cos_sin_turns(at * tilt_table[tilt_index[w], 0])
-        ex[2 * w] = cosine * keep
-        ex[2 * w + 1] = sine * keep
+        table[2 * w, :count] = cosine * keep
+        table[2 * w + 1, :count] = sine * keep
         cosine, sine = cos_sin_turns(across * tilt_table[tilt_index[w], 1])
-        ey[2 * w : 2 * w + 1] = cosine * keep_cols
-        ey[2 * w + 1 : 2 * w + 2] = sine * keep_cols
+        table[2 * w, count:] = cosine * keep_cols
+        table[2 * w + 1, count:] = sine * keep_cols
+
+
+def halves(value):
+    high = value.astype(jnp.bfloat16)
+    return high, (value - high.astype(jnp.float32)).astype(jnp.bfloat16)
+
+
+def three_products(a, b, contracted):
+    def product(left, right):
+        return lax.dot_general(
+            left, right, (((1,), (contracted,)), ((), ())), preferred_element_type=jnp.float32
+        )
+
+    return product(a[0], b[0]) + (product(a[0], b[1]) + product(a[1], b[0]))
 
 
 def detector_kernel(waves, tile_wave, taps_band, row_taps, col_taps, out, padded):
@@ -432,20 +450,12 @@
             term = re * re + im * im
             image = term if image is None else image + term
         padded[64 + 128 * b : 192 + 128 * b] = image / waves
+    taps_rows, taps_cols = halves(row_taps[...]), halves(col_taps[...])
+    image_high, image_low = halves(padded[...])
     for b in range(total // 128):
-        rows_done = jnp.dot(
-            row_taps[...],
-            padded[128 * b : 128 * b + 256],
-            precision=highest,
-            preferred_element_type=jnp.float32,
-        )
-        out[:, 128 * b : 128 * b + 128] = lax.dot_general(
-            col_taps[...],
-            rows_done,
-            (((1,), (1,)), ((), ())),
-            precision=highest,
-            preferred_element_type=jnp.float32,
-        )
+        window = tuple(part[128 * b : 128 * b + 256] for part in (image_high, image_low))
+        rows_done = halves(three_products(taps_rows, window, 0))
+        out[:, 128 * b : 128 * b + 128] = three_products(taps_cols, rows_done, 1)
 
 
 def block_windows(values):
@@ -517,12 +527,12 @@
         for i in range(len(widths))
     ]
 
-    mats_shape = (2 * rows2 + 2 * rows3 + 2 * row_count + 512, 2 * rows1)
+    mats_shape = (128 + 512, 512)
 
     def made(shape, dtype):
         return jax.ShapeDtypeStruct(shape, dtype)
 
-    mats, wide_rows, row_taps, col_taps, ex, ey = pl.pallas_call(
+    mats, wide_rows, row_taps, col_taps, table = pl.pallas_call(
         functools.partial(prepare_kernel, waves, row_count, total_rows, col_count),
         name="prepare",
         out_shape=[
@@ -530,11 +540,10 @@
             made((256, 256), jnp.bfloat16),
             made((128, 256), jnp.float32),
             made((tile_cols, tile_cols), jnp.float32),
-            made((2 * waves, rows1, 128), jnp.float32),
-            made((2 * waves, col_count + STEP), jnp.float32),
+            made((2 * waves, rows1 + -(-(col_count + STEP) // 1024) * 8, 128), jnp.float32),
         ],
         in_specs=[in_smem] * 3 + [in_vmem] * 3,
-        out_specs=[in_vmem] * 6,
+        out_specs=[in_vmem] * 5,
         scratch_shapes=[pltpu.VMEM((8, 256), jnp.float32)],
         cost_estimate=pl.CostEstimate(flops=1 << 31, bytes_accessed=2 << 20, transcendentals=0),
     )(tilt_index, first_row[None], tilt_table, fresnel_taps, ctf_taps, mtf_taps[None])
@@ -578,7 +587,8 @@
             )
 
         up, down, up2, down2 = halos[i]
-        args = [slice_order, owner, up2, up, potential, potential, potential, down, down2, ex, ey, mats]
+        args = [slice_order, owner, first_row[None]]
+        args += [up2, up, potential, potential, potential, down, down2, table, mats]
         in_specs = [
             piece(HALO),
             piece(2 * row_count + HALO),
@@ -587,8 +597,7 @@
             mine(2),
             piece(2 * row_count + HALO),
             piece(HALO),
-            fixed(*ex.shape),
-            fixed(*ey.shape),
+            fixed(*table.shape),
             fixed(*mats.shape),
         ]
         aliases = {}
@@ -603,12 +612,12 @@
             out_specs += [fixed(*shape) for shape, _ in carried]
         results = pl.pallas_call(
             functools.partial(
-                steps_kernel, waves, row_count, col_count, begin, count, given is not None, not last_call
+                steps_kernel, waves, row_count, total_rows, col_count, begin, count, given is not None, not last_call
             ),
             name="steps",
             out_shape=out_shape,
             grid_spec=pltpu.PrefetchScalarGridSpec(
-                num_scalar_prefetch=2,
+                num_scalar_prefetch=3,
                 grid=(count,),
                 in_specs=in_specs,
                 out_specs=out_specs,

time: 144 us -> 140 us (0.972)
  Pallas kernels: 52.2 us -> 49.5 us
    unnamed x21 -> x19, local copies, waits for them, and re-layouts: 3.98 us -> 2.88 us
where the time goes in v6:
time: 140 us; the launch traced here: 139 us
  blocking collectives  54.9 us (39%)
  Pallas kernels  49.5 us (35%)
  starting transfers between devices  20.8 us (15%)
  waiting for transfers between devices  9.64 us (7%)
  local copies, waits for them, and re-layouts  2.88 us (2%)
    all_to_all x1, blocking collectives, local(): lax.all_to_all(focused, 'lat', split_axis=0, concat_axis=0, tiled=True)  54.9 us
    pallas_call x2, Pallas kernels, local(): pl.pallas_call(functools.partial(steps_kernel, waves, row_count, total_ro...  38.7 us
    ppermute x8, starting transfers between devices, neighbour(): return lax.ppermute(value, 'lat', pairs)  20.8 us
    ppermute x8, waiting for transfers between devices, neighbour(): return lax.ppermute(value, 'lat', pairs)  9.64 us
    pallas_call x1, Pallas kernels, local(): pl.pallas_call(functools.partial(detector_kernel, waves), name='detector'...  3.95 us
    pallas_call x1, Pallas kernels, local(): pl.pallas_call(functools.partial(pick_kernel, HALO, edges), name='pick_ro...  3.81 us
    pallas_call x1, Pallas kernels, local(): pl.pallas_call(functools.partial(prepare_kernel, waves, row_count, total_...  3.11 us
    unnamed x19, local copies, waits for them, and re-layouts  2.88 us
  transfers between devices with their start and end apart: 8, of which 1 were waited for; matrix products, arithmetic and copies ran while one was open for 1% of the time, Pallas kernels for 15%

profile of v6, /device:TPU:13, one launch (start us, length us, event | category | flops | bytes accessed | tf_op | source)
XLA Modules:
  0.0 138.6 jit_solution(13001215432944601782)
XLA Ops:
  0.6 0.0 copy-start.8
  0.6 3.8 %pick_rows.1 = (bf16[160,2048]{1,0:T(8,128)(2,1)}, bf16[160,2048]{1,0:T(8,128)(2,1)}, bf16[32,2048]{1,0:T(8,128)(2,1)}, bf16[32,2048]{1,0:T(8,128)(2,1)}, bf16[1...) custom-call(s32[3]{0:T(128)} %order.5, ...), custom_call_target="tpu_custom_call" | custom-call | bytes 4194304 | tf_op jit(solution)/shard_map/pick_rows/pallas_call | solution.py:508
  4.5 3.7 %collective-permute-start.5 = (bf16[160,2048]{1,0:T(8,128)(2,1)}, bf16[160,2048]{1,0:T(8,128)(2,1)}, u32[]{:S(2)}, u32[]{:S(2)}) collective-permute-start(bf16[160,2048]{1,0:T(8,128)(2,1)} %get-tuple-element.33), channel_id=1, source_target_pairs={{0,1},{1,2},{2,3},{3,4},{4,5},{5,6},{6,7},{7,8},{8,9},{9,10},{10,1... | collective-permute-start | bytes 1966088 | tf_op jit(solution)/shard_map/ppermute | solution.py:499
  8.2 1.9 %collective-permute-start.6 = (bf16[160,2048]{1,0:T(8,128)(2,1)}, bf16[160,2048]{1,0:T(8,128)(2,1)}, u32[]{:S(2)}, u32[]{:S(2)}) collective-permute-start(bf16[160,2048]{1,0:T(8,128)(2,1)} %get-tuple-element.34), channel_id=1, source_target_pairs={{1,0},{2,1},{3,2},{4,3},{5,4},{6,5},{7,6},{8,7},{9,8},{10,9},{11,1... | collective-permute-start | bytes 1966088 | tf_op jit(solution)/shard_map/ppermute | solution.py:499
  10.1 3.1 %collective-permute-start = (bf16[32,2048]{1,0:T(8,128)(2,1)}, bf16[32,2048]{1,0:T(8,128)(2,1)S(1)}, u32[]{:S(2)}, u32[]{:S(2)}) collective-permute-start(bf16[32,2048]{1,0:T(8,128)(2,1)} %get-tuple-element.26), channel_id=1, source_target_pairs={{0,2},{1,3},{2,4},{3,5},{4,6},{5,7},{6,8},{7,9},{8,10},{9,11},{10,... | collective-permute-start | bytes 393224 | tf_op jit(solution)/shard_map/ppermute | solution.py:499
  13.3 3.1 %collective-permute-start.4 = (bf16[32,2048]{1,0:T(8,128)(2,1)}, bf16[32,2048]{1,0:T(8,128)(2,1)S(1)}, u32[]{:S(2)}, u32[]{:S(2)}) collective-permute-start(bf16[32,2048]{1,0:T(8,128)(2,1)} %get-tuple-element.32), channel_id=1, source_target_pairs={{0,2},{1,3},{2,4},{3,5},{4,6},{5,7},{6,8},{7,9},{8,10},{9,11},{10,... | collective-permute-start | bytes 393224 | tf_op jit(solution)/shard_map/ppermute | solution.py:499
  16.4 2.1 %collective-permute-start.7 = (bf16[32,2048]{1,0:T(8,128)(2,1)}, bf16[32,2048]{1,0:T(8,128)(2,1)S(1)}, u32[]{:S(2)}, u32[]{:S(2)}) collective-permute-start(bf16[32,2048]{1,0:T(8,128)(2,1)} %get-tuple-element.35), channel_id=1, source_target_pairs={{2,0},{3,1},{4,2},{5,3},{6,4},{7,5},{8,6},{9,7},{10,8},{11,9},{12,... | collective-permute-start | bytes 393224 | tf_op jit(solution)/shard_map/ppermute | solution.py:499
  18.6 0.0 copy-done.8
  18.6 0.7 copy.12.tilt_table
  19.3 3.1 %prepare.1 = (bf16[640,512]{1,0:T(8,128)(2,1)}, bf16[256,256]{1,0:T(8,128)(2,1)}, f32[128,256]{1,0:T(8,128)}, f32[256,256]{1,0:T(8,128)}, f32[4,296,128]{2,1,0:T(8,128)}) custom-call(s32[2]{0:T(128)} %tilt_index.1, s32[1]{0:T(128)} %bitcast.first_row, f32[41,2]{1,0:T(8,128)} %copy.12.tilt_table, f32[2,63]{1,0:T(2,128)} %fresnel.1, f32[2,127]{1,0:T(2,128)} %ctf.1, ...), custom_call_target="tpu_custom_call" | custom-call | flops 2147483648 | bytes 2097152 | tf_op jit(solution)/shard_map/prepare/pallas_call | solution.py:535
  22.4 9.6 %collective-permute-done.4.refs_0_ = bf16[32,2048]{1,0:T(8,128)(2,1)S(1)} collective-permute-done((bf16[32,2048]{1,0:T(8,128)(2,1)}, bf16[32,2048]{1,0:T(8,128)(2,1)S(1)}, u32[]{:S(2)}, u32[]{:S(2)}) %collective-permute-start.4) | collective-permute-done | bytes 131104 | tf_op jit(solution)/shard_map/ppermute | solution.py:499
  32.0 1.9 %collective-permute-start.3 = (bf16[32,2048]{1,0:T(8,128)(2,1)}, bf16[32,2048]{1,0:T(8,128)(2,1)S(1)}, u32[]{:S(2)}, u32[]{:S(2)}) collective-permute-start(bf16[32,2048]{1,0:T(8,128)(2,1)} %get-tuple-element.29), channel_id=1, source_target_pairs={{2,0},{3,1},{4,2},{5,3},{6,4},{7,5},{8,6},{9,7},{10,8},{11,9},{12,... | collective-permute-start | bytes 393224 | tf_op jit(solution)/shard_map/ppermute | solution.py:499
  33.9 0.0 collective-permute-done.7.refs_6_
  33.9 2.9 %collective-permute-start.1 = (bf16[160,2048]{1,0:T(8,128)(2,1)}, bf16[160,2048]{1,0:T(8,128)(2,1)S(1)}, u32[]{:S(2)}, u32[]{:S(2)}) collective-permute-start(bf16[160,2048]{1,0:T(8,128)(2,1)} %get-tuple-element.27), channel_id=1, source_target_pairs={{0,1},{1,2},{2,3},{3,4},{4,5},{5,6},{6,7},{7,8},{8,9},{9,10},{10,1... | collective-permute-start | bytes 1966088 | tf_op jit(solution)/shard_map/ppermute | solution.py:499
  36.8 0.0 collective-permute-done.5.refs_1_
  36.8 1.9 %collective-permute-start.2 = (bf16[160,2048]{1,0:T(8,128)(2,1)}, bf16[160,2048]{1,0:T(8,128)(2,1)S(1)}, u32[]{:S(2)}, u32[]{:S(2)}) collective-permute-start(bf16[160,2048]{1,0:T(8,128)(2,1)} %get-tuple-element.28), channel_id=1, source_target_pairs={{1,0},{2,1},{3,2},{4,3},{5,4},{6,5},{7,6},{8,7},{9,8},{10,9},{11,1... | collective-permute-start | bytes 1966088 | tf_op jit(solution)/shard_map/ppermute | solution.py:499
  38.8 0.0 collective-permute-done.6.refs_5_
  38.8 0.0 copy-done
  38.8 0.0 copy-done.1
  38.8 0.0 copy-done.2
  38.8 0.0 copy-start.3
  38.8 1.1 copy-done.3
  39.9 1.1 copy-done.4
  41.0 17.9 %steps.2 = (f32[2,2,64,4096]{3,2,1,0:T(8,128)}, bf16[16,2,2,64,256]{4,3,2,1,0:T(8,128)(2,1)S(1)}, bf16[2,256,256]{2,1,0:T(8,128)(2,1)S(1)}, bf16[2,192,256]{2,1,...) custom-call(s32[3]{0:T(128)S(1)} %copy-done.1, ...), custom_call_target="tpu_custom_call" | custom-call | flops 8589934592 | bytes 4194304 | tf_op jit(solution)/shard_map/steps/pallas_call | solution.py:613
  58.9 0.0 collective-permute-done.refs_0_
  58.9 0.0 collective-permute-done.3.refs_6_
  58.9 0.0 collective-permute-done.1.refs_1_
  59.0 0.0 collective-permute-done.2.refs_5_
  59.0 20.7 %steps.3 = (f32[2,2,64,4096]{3,2,1,0:T(8,128)}, bf16[16,2,2,64,256]{4,3,2,1,0:T(8,128)(2,1)S(1)}) custom-call(s32[3]{0:T(128)S(1)} %copy-done.1, s32[16]{0:T(128)S(1)} %copy-done.2, s32[1]{0:T(128)} %bitcast.first_row, bf16[32,2048]{1,0:T(8,128)(2,1)S(1)} %collective-permute-done.refs_0_, ...), custom_call_target="tpu_custom_call", output_to_operand_aliasing={{0}: (19, {}), {1}: (20, {})} | custom-call | flops 10737418240 | bytes 5242880 | tf_op jit(solution)/shard_map/steps/pallas_call | solution.py:613
  79.7 54.9 %all_to_all.5.tile_wave = bf16[16,2,2,64,256]{4,3,2,1,0:T(8,128)(2,1)S(1)} all-to-all(bf16[16,2,2,64,256]{4,3,2,1,0:T(8,128)(2,1)S(1)} %get-tuple-element.46), channel_id=1, replica_groups=mesh['lamella'=2,'lat'=16] {'lat'}, dimensions={0} | all-to-all | bytes 4194304 | tf_op jit(solution)/shard_map/all_to_all | solution.py:651
  134.6 0.0 copy-done.6
  134.6 3.9 %detector.1 = f32[256,1024]{1,0:T(8,128)} custom-call(bf16[16,2,2,64,256]{4,3,2,1,0:T(8,128)(2,1)S(1)} %all_to_all.5.tile_wave, bf16[256,256]{1,0:T(8,128)(2,1)S(1)} %copy-done.6, f32[128,256]{1,0:T(8,128)S(1)} %copy-done.7, f32[256,256]{1,0:T(8,128)S(1)} %copy-done.5), custom_call_target="tpu_custom_call" | custom-call | flops 8589934592 | bytes 4194304 | tf_op jit(solution)/shard_map/detector/pallas_call | solution.py:652
  (9 shorter events, 0.0 us)
Async XLA Ops:
  0.6 17.9 %copy-start.8 = (f32[41,2]{0,1:T(2,128)S(1)}, f32[41,2]{0,1:T(2,128)}, u32[]{:S(2)}) copy-start(f32[41,2]{0,1:T(2,128)} %param.11) | copy-start | bytes 988
  4.5 32.4 %collective-permute-start.5 = (bf16[160,2048]{1,0:T(8,128)(2,1)}, bf16[160,2048]{1,0:T(8,128)(2,1)}, u32[]{:S(2)}, u32[]{:S(2)}) collective-permute-start(bf16[160,2048]{1,0:T(8,128)(2,1)} %get-tuple-element.33), channel_id=1, source_target_pairs={{0,1},{1,2},{2,3},{3,4},{4,5},{5,6},{6,7},{7,8},{8,9},{9,10},{10,1... | collective-permute-start | bytes 1966088 | tf_op jit(solution)/shard_map/ppermute | solution.py:499
  8.2 30.6 %collective-permute-start.6 = (bf16[160,2048]{1,0:T(8,128)(2,1)}, bf16[160,2048]{1,0:T(8,128)(2,1)}, u32[]{:S(2)}, u32[]{:S(2)}) collective-permute-start(bf16[160,2048]{1,0:T(8,128)(2,1)} %get-tuple-element.34), channel_id=1, source_target_pairs={{1,0},{2,1},{3,2},{4,3},{5,4},{6,5},{7,6},{8,7},{9,8},{10,9},{11,1... | collective-permute-start | bytes 1966088 | tf_op jit(solution)/shard_map/ppermute | solution.py:499
  10.1 48.8 %collective-permute-start = (bf16[32,2048]{1,0:T(8,128)(2,1)}, bf16[32,2048]{1,0:T(8,128)(2,1)S(1)}, u32[]{:S(2)}, u32[]{:S(2)}) collective-permute-start(bf16[32,2048]{1,0:T(8,128)(2,1)} %get-tuple-element.26), channel_id=1, source_target_pairs={{0,2},{1,3},{2,4},{3,5},{4,6},{5,7},{6,8},{7,9},{8,10},{9,11},{10,... | collective-permute-start | bytes 393224 | tf_op jit(solution)/shard_map/ppermute | solution.py:499
  13.3 18.7 %collective-permute-start.4 = (bf16[32,2048]{1,0:T(8,128)(2,1)}, bf16[32,2048]{1,0:T(8,128)(2,1)S(1)}, u32[]{:S(2)}, u32[]{:S(2)}) collective-permute-start(bf16[32,2048]{1,0:T(8,128)(2,1)} %get-tuple-element.32), channel_id=1, source_target_pairs={{0,2},{1,3},{2,4},{3,5},{4,6},{5,7},{6,8},{7,9},{8,10},{9,11},{10,... | collective-permute-start | bytes 393224 | tf_op jit(solution)/shard_map/ppermute | solution.py:499
  16.4 17.5 %collective-permute-start.7 = (bf16[32,2048]{1,0:T(8,128)(2,1)}, bf16[32,2048]{1,0:T(8,128)(2,1)S(1)}, u32[]{:S(2)}, u32[]{:S(2)}) collective-permute-start(bf16[32,2048]{1,0:T(8,128)(2,1)} %get-tuple-element.35), channel_id=1, source_target_pairs={{2,0},{3,1},{4,2},{5,3},{6,4},{7,5},{8,6},{9,7},{10,8},{11,9},{12,... | collective-permute-start | bytes 393224 | tf_op jit(solution)/shard_map/ppermute | solution.py:499
  19.3 19.5 %copy-start = (bf16[6,64,4096]{2,1,0:T(8,128)(2,1)S(1)}, bf16[6,64,4096]{2,1,0:T(8,128)(2,1)}, u32[]{:S(2)}) copy-start(bf16[6,64,4096]{2,1,0:T(8,128)(2,1)} %refs_4_.3) | copy-start | bytes 9437188
  19.3 19.5 %copy-start.1 = (s32[3]{0:T(128)S(1)}, s32[3]{0:T(128)}, u32[]{:S(2)}) copy-start(s32[3]{0:T(128)} %order.5) | copy-start | bytes 40
  19.3 19.5 %copy-start.2 = (s32[16]{0:T(128)S(1)}, s32[16]{0:T(128)}, u32[]{:S(2)}) copy-start(s32[16]{0:T(128)} %owner.3) | copy-start | bytes 196
  32.0 26.9 %collective-permute-start.3 = (bf16[32,2048]{1,0:T(8,128)(2,1)}, bf16[32,2048]{1,0:T(8,128)(2,1)S(1)}, u32[]{:S(2)}, u32[]{:S(2)}) collective-permute-start(bf16[32,2048]{1,0:T(8,128)(2,1)} %get-tuple-element.29), channel_id=1, source_target_pairs={{2,0},{3,1},{4,2},{5,3},{6,4},{7,5},{8,6},{9,7},{10,8},{11,9},{12,... | collective-permute-start | bytes 393224 | tf_op jit(solution)/shard_map/ppermute | solution.py:499
  33.9 25.0 %collective-permute-start.1 = (bf16[160,2048]{1,0:T(8,128)(2,1)}, bf16[160,2048]{1,0:T(8,128)(2,1)S(1)}, u32[]{:S(2)}, u32[]{:S(2)}) collective-permute-start(bf16[160,2048]{1,0:T(8,128)(2,1)} %get-tuple-element.27), channel_id=1, source_target_pairs={{0,1},{1,2},{2,3},{3,4},{4,5},{5,6},{6,7},{7,8},{8,9},{9,10},{10,1... | collective-permute-start | bytes 1966088 | tf_op jit(solution)/shard_map/ppermute | solution.py:499
  36.8 22.1 %collective-permute-start.2 = (bf16[160,2048]{1,0:T(8,128)(2,1)}, bf16[160,2048]{1,0:T(8,128)(2,1)S(1)}, u32[]{:S(2)}, u32[]{:S(2)}) collective-permute-start(bf16[160,2048]{1,0:T(8,128)(2,1)} %get-tuple-element.28), channel_id=1, source_target_pairs={{1,0},{2,1},{3,2},{4,3},{5,4},{6,5},{7,6},{8,7},{9,8},{10,9},{11,1... | collective-permute-start | bytes 1966088 | tf_op jit(solution)/shard_map/ppermute | solution.py:499
  38.8 1.1 copy-start.3
  39.9 1.1 copy-start.4
  79.7 54.9 %copy-start.5 = (f32[256,256]{1,0:T(8,128)S(1)}, f32[256,256]{1,0:T(8,128)}, u32[]{:S(2)}) copy-start(f32[256,256]{1,0:T(8,128)} %get-tuple-element.49.col_taps) | copy-start | bytes 786436
  79.7 54.9 %copy-start.6 = (bf16[256,256]{1,0:T(8,128)(2,1)S(1)}, bf16[256,256]{1,0:T(8,128)(2,1)}, u32[]{:S(2)}) copy-start(bf16[256,256]{1,0:T(8,128)(2,1)} %get-tuple-element.47.taps_band) | copy-start | bytes 393220
  79.7 54.9 %copy-start.7 = (f32[128,256]{1,0:T(8,128)S(1)}, f32[128,256]{1,0:T(8,128)}, u32[]{:S(2)}) copy-start(f32[128,256]{1,0:T(8,128)} %get-tuple-element.48.row_taps) | copy-start | bytes 393220

commit v7 on v6

--- a/solution.py
+++ b/solution.py
@@ -256,44 +256,67 @@
     )
     second = ((up, None, rows, rows), (own2, 0, 0, rows), (down, None, rows, rows))
     third = ((up, None, 2 * rows, HALO), (own3, 0, 0, rows), (down, None, 2 * rows, HALO))
-    masks2 = [lanes_inside(blocks * g + blk, 64, col_count) for blk in range(blocks)]
-    masks3 = [lanes_inside(blocks * g - 1 + blk, 0, col_count) for blk in range(blocks)]
-    masks4 = [lanes_inside(blocks * g - 1 + blk, 64, col_count) for blk in range(blocks)]
-    kept = waved.shape[1]
-    low = lax.broadcasted_iota(jnp.int32, (kept, 128), 1) < 64
-
-    def exit_task(w):
-        product = rows_product(rows_band, spread3, w, 0)
-        for part in range(2):
-            before = turned[w, part]
-            for blk in range(blocks):
-                value = product[kept * part : kept * part + kept, 128 * blk : 128 * blk + 128]
-                lane = 256 * (blk + 1) + 128 * part
-                waved[w, :, lane : lane + 128] = (value * masks4[blk]).astype(jnp.bfloat16)
-                rolled = pltpu.roll(value, 64, 1)
-                exit_held[slot, w, part, :, 128 * blk : 128 * blk + 128] = jnp.where(
-                    low, before, rolled
-                )
-                before = rolled
-            turned[w, part] = before
-
-    def focused_store(w, blk, value):
-        for part in range(2):
-            block = value[:, 128 * part : 128 * part + 128].astype(jnp.bfloat16)
-            focused_held[slot, w, part, :, 128 * blk : 128 * blk + 128] = block
-
-    run(start_tasks(first, table, blocks * g, ring1))
-    run(columns_tasks(ring1, band, spread_store(spread1)))
-    run(rows_tasks(product2, rows_band, spread1))
-    at = first_row[0] - 2 * HALO
-    run(transmit_tasks(second, product2, ring2, last2, masks2, True, at, total_rows))
-    run(columns_tasks(ring2, band, spread_store(spread2)))
-    run(rows_tasks(product3, rows_band, spread2))
-    at = first_row[0] - HALO
-    run(transmit_tasks(third, product3, ring3, last3, masks3, False, at, total_rows))
-    run(columns_tasks(ring3, band, spread_store(spread3)))
-    run([functools.partial(exit_task, w) for w in range(waves)])
-    run(columns_tasks(waved, wide_band, focused_store))
+    low = lax.broadcasted_iota(jnp.int32, (waved.shape[1], 128), 1) < 64
+
+    def advance(now):
+        def masks(shift, offset):
+            return [lanes_inside(blocks * g + shift + blk, offset, col_count) for blk in range(now)]
+
+        def part_of(ref, lanes):
+            return ref.at[:, :, pl.ds(0, lanes)]
+
+        part1, part2, part3, part4 = (
+            part_of(ref, 256 * (now + 1)) for ref in (ring1, ring2, ring3, waved)
+        )
+        made1, made2, made3, rows2, rows3 = (
+            part_of(ref, 128 * now) for ref in (spread1, spread2, spread3, product2, product3)
+        )
+        masks4 = masks(-1, 64)
+        kept = waved.shape[1]
+
+        def exit_task(w):
+            product = rows_product(rows_band, made3, w, 0)
+            for part in range(2):
+                before = turned[w, part]
+                for blk in range(now):
+                    value = product[kept * part : kept * part + kept, 128 * blk : 128 * blk + 128]
+                    lane = 256 * (blk + 1) + 128 * part
+                    waved[w, :, lane : lane + 128] = (value * masks4[blk]).astype(jnp.bfloat16)
+                    rolled = pltpu.roll(value, 64, 1)
+                    exit_held[slot, w, part, :, 128 * blk : 128 * blk + 128] = jnp.where(
+                        low, before, rolled
+                    )
+                    before = rolled
+                turned[w, part] = before
+
+        def focused_store(w, blk, value):
+            for part in range(2):
+                block = value[:, 128 * part : 128 * part + 128].astype(jnp.bfloat16)
+                focused_held[slot, w, part, :, 128 * blk : 128 * blk + 128] = block
+
+        at = first_row[0]
+        run(start_tasks(first, table, blocks * g, part1))
+        run(columns_tasks(part1, band, spread_store(made1)))
+        run(rows_tasks(rows2, rows_band, made1))
+        run(
+            transmit_tasks(
+                second, rows2, part2, last2, masks(0, 64), True, at - 2 * HALO, total_rows
+            )
+        )
+        run(columns_tasks(part2, band, spread_store(made2)))
+        run(rows_tasks(rows3, rows_band, made2))
+        run(
+            transmit_tasks(third, rows3, part3, last3, masks(-1, 0), False, at - HALO, total_rows)
+        )
+        run(columns_tasks(part3, band, spread_store(made3)))
+        run([functools.partial(exit_task, w) for w in range(waves)])
+        run(columns_tasks(part4, wide_band, focused_store))
+
+    if handed:
+        advance(blocks)
+    else:
+        pl.when(local_step < count - 1)(functools.partial(advance, blocks))
+        pl.when(local_step == count - 1)(functools.partial(advance, TILE // 128))
     for_copies(local_step, slot, lambda copy: copy.start())
 
     @pl.when(local_step == count - 1)

time: 140 us -> 139 us (level)
  Pallas kernels: 49.5 us -> 48 us
where the time goes in v7:
time: 139 us; the launch traced here: 137 us
  blocking collectives  54.9 us (39%)
  Pallas kernels  48 us (35%)
  starting transfers between devices  20.8 us (15%)
  waiting for transfers between devices  9.64 us (7%)
  local copies, waits for them, and re-layouts  2.88 us (2%)
    all_to_all x1, blocking collectives, local(): lax.all_to_all(focused, 'lat', split_axis=0, concat_axis=0, tiled=True)  54.9 us
    pallas_call x2, Pallas kernels, local(): pl.pallas_call(functools.partial(steps_kernel, waves, row_count, total_ro...  37.3 us
    ppermute x8, starting transfers between devices, neighbour(): return lax.ppermute(value, 'lat', pairs)  20.8 us
    ppermute x8, waiting for transfers between devices, neighbour(): return lax.ppermute(value, 'lat', pairs)  9.64 us
    pallas_call x1, Pallas kernels, local(): pl.pallas_call(functools.partial(detector_kernel, waves), name='detector'...  3.95 us
    pallas_call x1, Pallas kernels, local(): pl.pallas_call(functools.partial(pick_kernel, HALO, edges), name='pick_ro...  3.64 us
    pallas_call x1, Pallas kernels, local(): pl.pallas_call(functools.partial(prepare_kernel, waves, row_count, total_...  3.11 us
    unnamed x19, local copies, waits for them, and re-layouts  2.88 us
  transfers between devices with their start and end apart: 8, of which 1 were waited for; matrix products, arithmetic and copies ran while one was open for 1% of the time, Pallas kernels for 15%

profile of v7, /device:TPU:13, one launch (start us, length us, event | category | flops | bytes accessed | tf_op | source)
XLA Modules:
  0.0 137.1 jit_solution(18355754745392574729)
XLA Ops:
  0.6 0.0 copy-start.8
  0.6 3.6 %pick_rows.1 = (bf16[160,2048]{1,0:T(8,128)(2,1)}, bf16[160,2048]{1,0:T(8,128)(2,1)}, bf16[32,2048]{1,0:T(8,128)(2,1)}, bf16[32,2048]{1,0:T(8,128)(2,1)}, bf16[1...) custom-call(s32[3]{0:T(128)} %order.5, ...), custom_call_target="tpu_custom_call" | custom-call | bytes 4194304 | tf_op jit(solution)/shard_map/pick_rows/pallas_call | solution.py:531
  4.3 3.7 %collective-permute-start.5 = (bf16[160,2048]{1,0:T(8,128)(2,1)}, bf16[160,2048]{1,0:T(8,128)(2,1)}, u32[]{:S(2)}, u32[]{:S(2)}) collective-permute-start(bf16[160,2048]{1,0:T(8,128)(2,1)} %get-tuple-element.33), channel_id=1, source_target_pairs={{0,1},{1,2},{2,3},{3,4},{4,5},{5,6},{6,7},{7,8},{8,9},{9,10},{10,1... | collective-permute-start | bytes 1966088 | tf_op jit(solution)/shard_map/ppermute | solution.py:522
  8.0 1.9 %collective-permute-start.6 = (bf16[160,2048]{1,0:T(8,128)(2,1)}, bf16[160,2048]{1,0:T(8,128)(2,1)}, u32[]{:S(2)}, u32[]{:S(2)}) collective-permute-start(bf16[160,2048]{1,0:T(8,128)(2,1)} %get-tuple-element.34), channel_id=1, source_target_pairs={{1,0},{2,1},{3,2},{4,3},{5,4},{6,5},{7,6},{8,7},{9,8},{10,9},{11,1... | collective-permute-start | bytes 1966088 | tf_op jit(solution)/shard_map/ppermute | solution.py:522
  9.9 3.1 %collective-permute-start = (bf16[32,2048]{1,0:T(8,128)(2,1)}, bf16[32,2048]{1,0:T(8,128)(2,1)S(1)}, u32[]{:S(2)}, u32[]{:S(2)}) collective-permute-start(bf16[32,2048]{1,0:T(8,128)(2,1)} %get-tuple-element.26), channel_id=1, source_target_pairs={{0,2},{1,3},{2,4},{3,5},{4,6},{5,7},{6,8},{7,9},{8,10},{9,11},{10,... | collective-permute-start | bytes 393224 | tf_op jit(solution)/shard_map/ppermute | solution.py:522
  13.1 3.1 %collective-permute-start.4 = (bf16[32,2048]{1,0:T(8,128)(2,1)}, bf16[32,2048]{1,0:T(8,128)(2,1)S(1)}, u32[]{:S(2)}, u32[]{:S(2)}) collective-permute-start(bf16[32,2048]{1,0:T(8,128)(2,1)} %get-tuple-element.32), channel_id=1, source_target_pairs={{0,2},{1,3},{2,4},{3,5},{4,6},{5,7},{6,8},{7,9},{8,10},{9,11},{10,... | collective-permute-start | bytes 393224 | tf_op jit(solution)/shard_map/ppermute | solution.py:522
  16.2 2.1 %collective-permute-start.7 = (bf16[32,2048]{1,0:T(8,128)(2,1)}, bf16[32,2048]{1,0:T(8,128)(2,1)S(1)}, u32[]{:S(2)}, u32[]{:S(2)}) collective-permute-start(bf16[32,2048]{1,0:T(8,128)(2,1)} %get-tuple-element.35), channel_id=1, source_target_pairs={{2,0},{3,1},{4,2},{5,3},{6,4},{7,5},{8,6},{9,7},{10,8},{11,9},{12,... | collective-permute-start | bytes 393224 | tf_op jit(solution)/shard_map/ppermute | solution.py:522
  18.4 0.0 copy-done.8
  18.4 0.7 copy.12.tilt_table
  19.1 3.1 %prepare.1 = (bf16[640,512]{1,0:T(8,128)(2,1)}, bf16[256,256]{1,0:T(8,128)(2,1)}, f32[128,256]{1,0:T(8,128)}, f32[256,256]{1,0:T(8,128)}, f32[4,296,128]{2,1,0:T(8,128)}) custom-call(s32[2]{0:T(128)} %tilt_index.1, s32[1]{0:T(128)} %bitcast.first_row, f32[41,2]{1,0:T(8,128)} %copy.12.tilt_table, f32[2,63]{1,0:T(2,128)} %fresnel.1, f32[2,127]{1,0:T(2,128)} %ctf.1, ...), custom_call_target="tpu_custom_call" | custom-call | flops 2147483648 | bytes 2097152 | tf_op jit(solution)/shard_map/prepare/pallas_call | solution.py:558
  22.2 9.6 %collective-permute-done.4.refs_0_ = bf16[32,2048]{1,0:T(8,128)(2,1)S(1)} collective-permute-done((bf16[32,2048]{1,0:T(8,128)(2,1)}, bf16[32,2048]{1,0:T(8,128)(2,1)S(1)}, u32[]{:S(2)}, u32[]{:S(2)}) %collective-permute-start.4) | collective-permute-done | bytes 131104 | tf_op jit(solution)/shard_map/ppermute | solution.py:522
  31.8 1.9 %collective-permute-start.3 = (bf16[32,2048]{1,0:T(8,128)(2,1)}, bf16[32,2048]{1,0:T(8,128)(2,1)S(1)}, u32[]{:S(2)}, u32[]{:S(2)}) collective-permute-start(bf16[32,2048]{1,0:T(8,128)(2,1)} %get-tuple-element.29), channel_id=1, source_target_pairs={{2,0},{3,1},{4,2},{5,3},{6,4},{7,5},{8,6},{9,7},{10,8},{11,9},{12,... | collective-permute-start | bytes 393224 | tf_op jit(solution)/shard_map/ppermute | solution.py:522
  33.8 0.0 collective-permute-done.7.refs_6_
  33.8 2.9 %collective-permute-start.1 = (bf16[160,2048]{1,0:T(8,128)(2,1)}, bf16[160,2048]{1,0:T(8,128)(2,1)S(1)}, u32[]{:S(2)}, u32[]{:S(2)}) collective-permute-start(bf16[160,2048]{1,0:T(8,128)(2,1)} %get-tuple-element.27), channel_id=1, source_target_pairs={{0,1},{1,2},{2,3},{3,4},{4,5},{5,6},{6,7},{7,8},{8,9},{9,10},{10,1... | collective-permute-start | bytes 1966088 | tf_op jit(solution)/shard_map/ppermute | solution.py:522
  36.7 0.0 collective-permute-done.5.refs_1_
  36.7 1.9 %collective-permute-start.2 = (bf16[160,2048]{1,0:T(8,128)(2,1)}, bf16[160,2048]{1,0:T(8,128)(2,1)S(1)}, u32[]{:S(2)}, u32[]{:S(2)}) collective-permute-start(bf16[160,2048]{1,0:T(8,128)(2,1)} %get-tuple-element.28), channel_id=1, source_target_pairs={{1,0},{2,1},{3,2},{4,3},{5,4},{6,5},{7,6},{8,7},{9,8},{10,9},{11,1... | collective-permute-start | bytes 1966088 | tf_op jit(solution)/shard_map/ppermute | solution.py:522
  38.6 0.0 collective-permute-done.6.refs_5_
  38.6 0.0 copy-done
  38.6 1.1 copy-done.3
  39.7 1.1 copy-done.4
  40.8 18.0 %steps.2 = (f32[2,2,64,4096]{3,2,1,0:T(8,128)}, bf16[16,2,2,64,256]{4,3,2,1,0:T(8,128)(2,1)S(1)}, bf16[2,256,256]{2,1,0:T(8,128)(2,1)S(1)}, bf16[2,192,256]{2,1,...) custom-call(s32[3]{0:T(128)S(1)} %copy-done.1, ...), custom_call_target="tpu_custom_call" | custom-call | flops 8589934592 | bytes 4194304 | tf_op jit(solution)/shard_map/steps/pallas_call | solution.py:636
  58.8 0.0 collective-permute-done.refs_0_
  58.8 0.0 collective-permute-done.3.refs_6_
  58.8 0.0 collective-permute-done.1.refs_1_
  58.8 0.0 collective-permute-done.2.refs_5_
  58.8 19.4 %steps.3 = (f32[2,2,64,4096]{3,2,1,0:T(8,128)}, bf16[16,2,2,64,256]{4,3,2,1,0:T(8,128)(2,1)S(1)}) custom-call(s32[3]{0:T(128)S(1)} %copy-done.1, s32[16]{0:T(128)S(1)} %copy-done.2, s32[1]{0:T(128)} %bitcast.first_row, bf16[32,2048]{1,0:T(8,128)(2,1)S(1)} %collective-permute-done.refs_0_, ...), custom_call_target="tpu_custom_call", output_to_operand_aliasing={{0}: (19, {}), {1}: (20, {})} | custom-call | flops 10737418240 | bytes 5242880 | tf_op jit(solution)/shard_map/steps/pallas_call | solution.py:636
  78.2 0.0 copy-start.5
  78.2 0.0 copy-start.6
  78.2 0.0 copy-start.7
  78.2 54.9 %all_to_all.5.tile_wave = bf16[16,2,2,64,256]{4,3,2,1,0:T(8,128)(2,1)S(1)} all-to-all(bf16[16,2,2,64,256]{4,3,2,1,0:T(8,128)(2,1)S(1)} %get-tuple-element.46), channel_id=1, replica_groups=mesh['lamella'=2,'lat'=16] {'lat'}, dimensions={0} | all-to-all | bytes 4194304 | tf_op jit(solution)/shard_map/all_to_all | solution.py:674
  133.1 0.0 copy-done.6
  133.1 4.0 %detector.1 = f32[256,1024]{1,0:T(8,128)} custom-call(bf16[16,2,2,64,256]{4,3,2,1,0:T(8,128)(2,1)S(1)} %all_to_all.5.tile_wave, bf16[256,256]{1,0:T(8,128)(2,1)S(1)} %copy-done.6, f32[128,256]{1,0:T(8,128)S(1)} %copy-done.7, f32[256,256]{1,0:T(8,128)S(1)} %copy-done.5), custom_call_target="tpu_custom_call" | custom-call | flops 8589934592 | bytes 4194304 | tf_op jit(solution)/shard_map/detector/pallas_call | solution.py:675
  (9 shorter events, 0.0 us)
Async XLA Ops:
  0.6 17.8 %copy-start.8 = (f32[41,2]{0,1:T(2,128)S(1)}, f32[41,2]{0,1:T(2,128)}, u32[]{:S(2)}) copy-start(f32[41,2]{0,1:T(2,128)} %param.11) | copy-start | bytes 988
  4.3 32.4 %collective-permute-start.5 = (bf16[160,2048]{1,0:T(8,128)(2,1)}, bf16[160,2048]{1,0:T(8,128)(2,1)}, u32[]{:S(2)}, u32[]{:S(2)}) collective-permute-start(bf16[160,2048]{1,0:T(8,128)(2,1)} %get-tuple-element.33), channel_id=1, source_target_pairs={{0,1},{1,2},{2,3},{3,4},{4,5},{5,6},{6,7},{7,8},{8,9},{9,10},{10,1... | collective-permute-start | bytes 1966088 | tf_op jit(solution)/shard_map/ppermute | solution.py:522
  8.0 30.6 %collective-permute-start.6 = (bf16[160,2048]{1,0:T(8,128)(2,1)}, bf16[160,2048]{1,0:T(8,128)(2,1)}, u32[]{:S(2)}, u32[]{:S(2)}) collective-permute-start(bf16[160,2048]{1,0:T(8,128)(2,1)} %get-tuple-element.34), channel_id=1, source_target_pairs={{1,0},{2,1},{3,2},{4,3},{5,4},{6,5},{7,6},{8,7},{9,8},{10,9},{11,1... | collective-permute-start | bytes 1966088 | tf_op jit(solution)/shard_map/ppermute | solution.py:522
  9.9 48.8 %collective-permute-start = (bf16[32,2048]{1,0:T(8,128)(2,1)}, bf16[32,2048]{1,0:T(8,128)(2,1)S(1)}, u32[]{:S(2)}, u32[]{:S(2)}) collective-permute-start(bf16[32,2048]{1,0:T(8,128)(2,1)} %get-tuple-element.26), channel_id=1, source_target_pairs={{0,2},{1,3},{2,4},{3,5},{4,6},{5,7},{6,8},{7,9},{8,10},{9,11},{10,... | collective-permute-start | bytes 393224 | tf_op jit(solution)/shard_map/ppermute | solution.py:522
  13.1 18.7 %collective-permute-start.4 = (bf16[32,2048]{1,0:T(8,128)(2,1)}, bf16[32,2048]{1,0:T(8,128)(2,1)S(1)}, u32[]{:S(2)}, u32[]{:S(2)}) collective-permute-start(bf16[32,2048]{1,0:T(8,128)(2,1)} %get-tuple-element.32), channel_id=1, source_target_pairs={{0,2},{1,3},{2,4},{3,5},{4,6},{5,7},{6,8},{7,9},{8,10},{9,11},{10,... | collective-permute-start | bytes 393224 | tf_op jit(solution)/shard_map/ppermute | solution.py:522
  16.2 17.5 %collective-permute-start.7 = (bf16[32,2048]{1,0:T(8,128)(2,1)}, bf16[32,2048]{1,0:T(8,128)(2,1)S(1)}, u32[]{:S(2)}, u32[]{:S(2)}) collective-permute-start(bf16[32,2048]{1,0:T(8,128)(2,1)} %get-tuple-element.35), channel_id=1, source_target_pairs={{2,0},{3,1},{4,2},{5,3},{6,4},{7,5},{8,6},{9,7},{10,8},{11,9},{12,... | collective-permute-start | bytes 393224 | tf_op jit(solution)/shard_map/ppermute | solution.py:522
  19.1 19.5 %copy-start = (bf16[6,64,4096]{2,1,0:T(8,128)(2,1)S(1)}, bf16[6,64,4096]{2,1,0:T(8,128)(2,1)}, u32[]{:S(2)}) copy-start(bf16[6,64,4096]{2,1,0:T(8,128)(2,1)} %refs_4_.3) | copy-start | bytes 9437188
  19.1 19.5 %copy-start.1 = (s32[3]{0:T(128)S(1)}, s32[3]{0:T(128)}, u32[]{:S(2)}) copy-start(s32[3]{0:T(128)} %order.5) | copy-start | bytes 40
  19.1 19.5 %copy-start.2 = (s32[16]{0:T(128)S(1)}, s32[16]{0:T(128)}, u32[]{:S(2)}) copy-start(s32[16]{0:T(128)} %owner.3) | copy-start | bytes 196
  31.8 26.9 %collective-permute-start.3 = (bf16[32,2048]{1,0:T(8,128)(2,1)}, bf16[32,2048]{1,0:T(8,128)(2,1)S(1)}, u32[]{:S(2)}, u32[]{:S(2)}) collective-permute-start(bf16[32,2048]{1,0:T(8,128)(2,1)} %get-tuple-element.29), channel_id=1, source_target_pairs={{2,0},{3,1},{4,2},{5,3},{6,4},{7,5},{8,6},{9,7},{10,8},{11,9},{12,... | collective-permute-start | bytes 393224 | tf_op jit(solution)/shard_map/ppermute | solution.py:522
  33.8 25.0 %collective-permute-start.1 = (bf16[160,2048]{1,0:T(8,128)(2,1)}, bf16[160,2048]{1,0:T(8,128)(2,1)S(1)}, u32[]{:S(2)}, u32[]{:S(2)}) collective-permute-start(bf16[160,2048]{1,0:T(8,128)(2,1)} %get-tuple-element.27), channel_id=1, source_target_pairs={{0,1},{1,2},{2,3},{3,4},{4,5},{5,6},{6,7},{7,8},{8,9},{9,10},{10,1... | collective-permute-start | bytes 1966088 | tf_op jit(solution)/shard_map/ppermute | solution.py:522
  36.7 22.1 %collective-permute-start.2 = (bf16[160,2048]{1,0:T(8,128)(2,1)}, bf16[160,2048]{1,0:T(8,128)(2,1)S(1)}, u32[]{:S(2)}, u32[]{:S(2)}) collective-permute-start(bf16[160,2048]{1,0:T(8,128)(2,1)} %get-tuple-element.28), channel_id=1, source_target_pairs={{1,0},{2,1},{3,2},{4,3},{5,4},{6,5},{7,6},{8,7},{9,8},{10,9},{11,1... | collective-permute-start | bytes 1966088 | tf_op jit(solution)/shard_map/ppermute | solution.py:522
  38.6 1.1 copy-start.3
  39.7 1.1 copy-start.4
  78.2 54.9 %copy-start.5 = (f32[256,256]{1,0:T(8,128)S(1)}, f32[256,256]{1,0:T(8,128)}, u32[]{:S(2)}) copy-start(f32[256,256]{1,0:T(8,128)} %get-tuple-element.49.col_taps) | copy-start | bytes 786436
  78.2 54.9 %copy-start.6 = (bf16[256,256]{1,0:T(8,128)(2,1)S(1)}, bf16[256,256]{1,0:T(8,128)(2,1)}, u32[]{:S(2)}) copy-start(bf16[256,256]{1,0:T(8,128)(2,1)} %get-tuple-element.47.taps_band) | copy-start | bytes 393220
  78.2 54.9 %copy-start.7 = (f32[128,256]{1,0:T(8,128)S(1)}, f32[128,256]{1,0:T(8,128)}, u32[]{:S(2)}) copy-start(f32[128,256]{1,0:T(8,128)} %get-tuple-element.48.row_taps) | copy-start | bytes 393220
